TPU v7x, 32 devices: a whole 2x2x4 slice. The times are simulated.
32 devices in a mesh: wide: 8 (over z, x), narrow: 4 (over y, core).
Axes of the slice: x: 2, y: 2, z: 4, core: 2. Of those that a mesh axis runs over, the one named last changes fastest.
Arguments:
- tokens: bfloat16 [32, 1024, 768], P('wide', 'narrow'), may hold values from -6 to 6
- condition: bfloat16 [32, 768], P('wide'), may hold values from -6 to 6
- cotangent: bfloat16 [32, 1024, 768], P('wide', 'narrow'), may hold values from -6 to 6
- counts: int32 [8], P('wide'), may hold values from 1 to 4, as said below
- w_ada: bfloat16 [768, 4608], replicated, may hold values from -0.21875 to 0.21875
- k_attn: bfloat16 [3, 3, 768], replicated, may hold values from -2 to 2
- w_qkv: bfloat16 [768, 3, 768], P(None, None, 'narrow'), may hold values from -0.21875 to 0.21875
- w_out: bfloat16 [768, 768], P('narrow'), may hold values from -1.75 to 1.75
- w_up: bfloat16 [768, 3072], P(None, 'narrow'), may hold values from -0.21875 to 0.21875
- k_ffn: bfloat16 [3, 3, 3072], P(None, None, 'narrow'), may hold values from -2 to 2
- w_down: bfloat16 [3072, 768], P('narrow'), may hold values from -0.109375 to 0.109375
Outputs:
- block: bfloat16 [32, 1024, 768], P('wide', 'narrow')
- grad_tokens: float32 [32, 1024, 768], P('wide', 'narrow')
- grad_condition: float32 [32, 768], P('wide')
- grad_w_ada: float32 [768, 4608], replicated
- grad_k_attn: float32 [3, 3, 768], replicated
- grad_w_qkv: float32 [768, 3, 768], P(None, None, 'narrow')
- grad_w_out: float32 [768, 768], P('narrow')
- grad_w_up: float32 [768, 3072], P(None, 'narrow')
- grad_k_ffn: float32 [3, 3, 3072], P(None, None, 'narrow')
- grad_w_down: float32 [3072, 768], P('narrow')
Inputs may be any that keep to these rules, and one draw needn't show every extreme that they name: counts[w] is the number of live latents among the 4 slots of wide index w (slots 0 to counts[w] - 1 are live); some index has all 4 live.
All inputs are finite; a program needn't handle non-finite values.
Results may differ from a plain program's by a relative error of at most 0.015.
The roundings to bfloat16 on the way count: a program that leaves them out, or rounds other values in their place, can miss the bound.
Values may be sent and summed in bfloat16 or wider, within the bound.
A program may use at most 192 MiB of HBM per device.

v0:
```python
from functools import partial

import jax
import jax.numpy as jnp
from jax import lax
from jax.sharding import PartitionSpec as P

HEAD_DIM = 64
SIDE = 32


CONTRACT_ROWS = (((0,), (0,)), ((), ()))
CONTRACT_COLS = (((1,), (1,)), ((), ()))


def layer_norm(values_in):
    mean_val = jnp.mean(values_in, axis=-1, keepdims=True)
    centred = values_in - mean_val
    return centred * lax.rsqrt(jnp.mean(centred * centred, axis=-1, keepdims=True) + 1e-06)


def conv_grid(values_in, kernel):
    channels = values_in.shape[-1]
    shaped = values_in.reshape(SIDE, SIDE, channels)
    padded = jnp.pad(shaped, ((1, 1), (1, 1), (0, 0)))
    summed_taps = jnp.zeros_like(shaped)
    for tap_row in range(3):
        for tap_col in range(3):
            summed_taps = (
                summed_taps
                + kernel[tap_row, tap_col]
                * padded[tap_row : tap_row + SIDE, tap_col : tap_col + SIDE]
            )
    return summed_taps.reshape(SIDE * SIDE, channels)


def to_groups(matrix):
    channels = matrix.shape[-1]
    blocks_five = matrix.reshape(SIDE // 2, 2, SIDE // 2, 2, channels)
    return blocks_five.transpose(1, 3, 0, 2, 4).reshape(4, SIDE * SIDE // 4, channels)


def from_groups(groups):
    channels = groups.shape[-1]
    blocks_five = groups.reshape(2, 2, SIDE // 2, SIDE // 2, channels)
    return blocks_five.transpose(2, 0, 3, 1, 4).reshape(SIDE * SIDE, channels)


def per_device(
    tokens, condition, cotangent, counts, w_ada, k_attn, w_qkv, w_out, w_up, k_ffn, w_down
):
    lat_dev, shard_rows, model_width = tokens.shape
    heads_here = w_out.shape[0] // HEAD_DIM
    local_width = heads_here * HEAD_DIM
    group_rows = SIDE * SIDE // 4
    scale_qk = HEAD_DIM ** (-0.5)
    gelu_tanh = partial(jax.nn.gelu, approximate=True)
    cond_f = condition.astype(jnp.float32)
    silu_low = jax.nn.silu(cond_f).astype(jnp.bfloat16)
    modulation = jnp.dot(silu_low, w_ada, preferred_element_type=jnp.float32)
    kernel_attn = k_attn.astype(jnp.float32)
    kernel_ffn = k_ffn.astype(jnp.float32)
    live_count = counts[0]

    def one_latent(slot_index, state_in):
        block_buf, grad_x_buf, grad_mod_buf, grad_sums = state_in
        live_one = (slot_index < live_count).astype(jnp.float32)
        latent = lax.dynamic_index_in_dim(tokens, slot_index, 0, keepdims=False).astype(jnp.float32)
        cot_row = (
            lax.dynamic_index_in_dim(cotangent, slot_index, 0, keepdims=False).astype(jnp.float32)
            * live_one
        )
        mod_row = lax.dynamic_index_in_dim(modulation, slot_index, 0, keepdims=False)
        shift_one, scale_one, gate_one, shift_two, scale_two, gate_two = jnp.split(mod_row, 6)
        normed_one, pull_one = jax.vjp(layer_norm, latent)
        h_one = lax.all_gather(
            (normed_one * (1.0 + scale_one) + shift_one).astype(jnp.bfloat16),
            "narrow",
            axis=0,
            tiled=True,
        )
        h_one_f = h_one.astype(jnp.float32)
        conv_attn_out, pull_conv_attn = jax.vjp(conv_grid, h_one_f, kernel_attn)
        mixed_in = conv_attn_out.astype(jnp.bfloat16)
        projected = jnp.einsum(
            "sd,dte->tse", mixed_in, w_qkv, preferred_element_type=jnp.float32
        ).astype(jnp.bfloat16)
        grouped = jax.vmap(to_groups)(projected).reshape(3, 4, group_rows, heads_here, HEAD_DIM)
        queries, key_heads, values = (grouped[0], grouped[1], grouped[2])
        scores = (
            jnp.einsum("pqhe,pkhe->phqk", queries, key_heads, preferred_element_type=jnp.float32)
            * scale_qk
        )
        row_top = jnp.max(scores, axis=-1, keepdims=True)
        log_total = row_top + jnp.log(jnp.sum(jnp.exp(scores - row_top), axis=-1, keepdims=True))
        probs_f = jnp.exp(scores - log_total)
        probs_low = probs_f.astype(jnp.bfloat16)
        context = jnp.einsum(
            "phqk,pkhe->pqhe", probs_low, values, preferred_element_type=jnp.float32
        )
        context = from_groups(context.reshape(4, group_rows, local_width)).astype(jnp.bfloat16)
        attended = lax.psum_scatter(
            jnp.dot(context, w_out, preferred_element_type=jnp.float32),
            "narrow",
            scatter_dimension=0,
            tiled=True,
        )
        after_mix = latent + gate_one * attended
        normed_two, pull_two = jax.vjp(layer_norm, after_mix)
        h_two = lax.all_gather(
            (normed_two * (1.0 + scale_two) + shift_two).astype(jnp.bfloat16),
            "narrow",
            axis=0,
            tiled=True,
        )
        hidden = jnp.dot(h_two, w_up, preferred_element_type=jnp.float32)
        conv_ffn_out, pull_conv_ffn = jax.vjp(conv_grid, hidden, kernel_ffn)
        gelu_out, pull_gelu = jax.vjp(gelu_tanh, conv_ffn_out)
        activated = gelu_out.astype(jnp.bfloat16)
        branch = lax.psum_scatter(
            jnp.dot(
                lax.slice_in_dim(activated, 0, shard_rows * lax.axis_size("narrow"), axis=0),
                w_down,
                preferred_element_type=jnp.float32,
            ).astype(jnp.bfloat16),
            "narrow",
            scatter_dimension=0,
            tiled=True,
        ).astype(jnp.float32)
        result = after_mix + gate_two * branch
        block_buf = lax.dynamic_update_index_in_dim(
            block_buf, (result * live_one).astype(jnp.bfloat16), slot_index, 0
        )
        grad_gate_two = jnp.sum(cot_row * branch, axis=0)
        grad_branch = lax.all_gather(
            (cot_row * gate_two).astype(jnp.bfloat16), "narrow", axis=0, tiled=True
        )
        grad_w_down = lax.dot_general(
            activated, grad_branch, CONTRACT_ROWS, preferred_element_type=jnp.float32
        )
        grad_act = lax.dot_general(
            grad_branch, w_down, CONTRACT_COLS, preferred_element_type=jnp.float32
        )
        (grad_conv_ffn,) = pull_gelu(grad_act)
        grad_hidden, grad_k_ffn = pull_conv_ffn(grad_conv_ffn)
        grad_hidden = grad_hidden.astype(jnp.bfloat16)
        grad_w_up = lax.dot_general(
            h_two, grad_hidden, CONTRACT_ROWS, preferred_element_type=jnp.float32
        )
        grad_h_two = lax.psum_scatter(
            lax.dot_general(grad_hidden, w_up, CONTRACT_COLS, preferred_element_type=jnp.float32),
            "narrow",
            scatter_dimension=0,
            tiled=True,
        )
        grad_scale_two = jnp.sum(grad_h_two * normed_two, axis=0)
        grad_shift_two = jnp.sum(grad_h_two, axis=0)
        (grad_after,) = pull_two(grad_h_two * (1.0 + scale_two))
        grad_after = grad_after + cot_row
        grad_gate_one = jnp.sum(grad_after * attended, axis=0)
        grad_attended = lax.all_gather(
            (grad_after * gate_one).astype(jnp.bfloat16), "narrow", axis=0, tiled=True
        )
        grad_w_out = lax.dot_general(
            context, grad_attended, CONTRACT_ROWS, preferred_element_type=jnp.float32
        )
        grad_context = lax.dot_general(
            grad_attended, w_out, CONTRACT_COLS, preferred_element_type=jnp.float32
        ).astype(jnp.bfloat16)
        grad_ctx_groups = to_groups(grad_context).reshape(4, group_rows, heads_here, HEAD_DIM)
        grad_probs = jnp.einsum(
            "pqhe,pkhe->phqk", grad_ctx_groups, values, preferred_element_type=jnp.float32
        )
        grad_values = jnp.einsum(
            "phqk,pqhe->pkhe", probs_low, grad_ctx_groups, preferred_element_type=jnp.float32
        )
        row_inner = jnp.sum(grad_probs * probs_f, axis=-1, keepdims=True)
        grad_scores = (probs_f * (grad_probs - row_inner)).astype(jnp.bfloat16)
        grad_queries = (
            jnp.einsum(
                "phqk,pkhe->pqhe", grad_scores, key_heads, preferred_element_type=jnp.float32
            )
            * scale_qk
        )
        grad_keys = (
            jnp.einsum("phqk,pqhe->pkhe", grad_scores, queries, preferred_element_type=jnp.float32)
            * scale_qk
        )
        grad_grouped = jnp.stack([grad_queries, grad_keys, grad_values]).reshape(
            3, 4, group_rows, local_width
        )
        grad_projected = jax.vmap(from_groups)(grad_grouped).astype(jnp.bfloat16)
        grad_w_qkv = jnp.einsum(
            "sd,tse->dte", mixed_in, grad_projected, preferred_element_type=jnp.float32
        )
        grad_mixed = jnp.einsum(
            "tse,dte->sd", grad_projected, w_qkv, preferred_element_type=jnp.float32
        )
        grad_h_full, grad_k_attn = pull_conv_attn(grad_mixed)
        grad_h_one = lax.psum_scatter(
            grad_h_full.astype(jnp.bfloat16), "narrow", scatter_dimension=0, tiled=True
        ).astype(jnp.float32)
        grad_scale_one = jnp.sum(grad_h_one * normed_one, axis=0)
        grad_shift_one = jnp.sum(grad_h_one, axis=0)
        (grad_latent,) = pull_one(grad_h_one * (1.0 + scale_one))
        grad_latent = grad_latent + grad_after
        grad_x_buf = lax.dynamic_update_index_in_dim(grad_x_buf, grad_latent, slot_index, 0)
        grad_mod_row = jnp.concatenate(
            [
                grad_shift_one,
                grad_scale_one,
                grad_gate_one,
                grad_shift_two,
                grad_scale_two,
                grad_gate_two,
            ]
        )
        grad_mod_buf = lax.dynamic_update_index_in_dim(grad_mod_buf, grad_mod_row, slot_index, 0)
        grad_sums = jax.tree.map(
            jnp.add,
            grad_sums,
            (grad_k_attn, grad_w_qkv, grad_w_out, grad_w_up, grad_k_ffn, grad_w_down),
        )
        return (block_buf, grad_x_buf, grad_mod_buf, grad_sums)

    zero_sums = (
        jnp.zeros(k_attn.shape, jnp.float32),
        jnp.zeros(w_qkv.shape, jnp.float32),
        jnp.zeros(w_out.shape, jnp.float32),
        jnp.zeros(w_up.shape, jnp.float32),
        jnp.zeros(k_ffn.shape, jnp.float32),
        jnp.zeros(w_down.shape, jnp.float32),
    )
    start_state = (
        jnp.zeros(tokens.shape, jnp.bfloat16),
        jnp.zeros(tokens.shape, jnp.float32),
        jnp.zeros(modulation.shape, jnp.float32),
        zero_sums,
    )
    block, grad_tokens, grad_mod, grad_sums = lax.fori_loop(0, lat_dev, one_latent, start_state)
    grad_mod, grad_k_attn = lax.psum((grad_mod, grad_sums[0]), "narrow")
    mod_low = grad_mod.astype(jnp.bfloat16)
    grad_silu = lax.dot_general(mod_low, w_ada, CONTRACT_COLS, preferred_element_type=jnp.float32)
    silu_value, pull_silu = jax.vjp(jax.nn.silu, cond_f)
    (grad_condition,) = pull_silu(grad_silu)
    silu_all, mod_all = (
        lax.all_gather(silu_low, "wide", axis=0, tiled=True),
        lax.all_gather(mod_low, "wide", axis=0, tiled=True),
    )
    grad_w_ada = lax.dot_general(
        silu_all, mod_all, CONTRACT_ROWS, preferred_element_type=jnp.float32
    )
    grad_k_attn, grad_w_qkv, grad_w_out, grad_w_up, grad_k_ffn, grad_w_down = (
        lax.psum(grad_k_attn.astype(jnp.bfloat16), "wide").astype(jnp.float32),
        lax.psum(grad_sums[1].astype(jnp.bfloat16), "wide").astype(jnp.float32),
        lax.psum(grad_sums[2].astype(jnp.bfloat16), "wide").astype(jnp.float32),
        lax.psum(grad_sums[3].astype(jnp.bfloat16), "wide").astype(jnp.float32),
        lax.psum(grad_sums[4].astype(jnp.bfloat16), "wide").astype(jnp.float32),
        lax.psum(grad_sums[5].astype(jnp.bfloat16), "wide").astype(jnp.float32),
    )
    return (
        block,
        grad_tokens,
        grad_condition,
        grad_w_ada,
        grad_k_attn,
        grad_w_qkv,
        grad_w_out,
        grad_w_up,
        grad_k_ffn,
        grad_w_down,
    )


def solution(mesh):
    placed = (
        P("wide", "narrow", None),
        P("wide", None),
        P("wide", "narrow", None),
        P("wide"),
        P(),
        P(),
        P(None, None, "narrow"),
        P("narrow", None),
        P(None, "narrow"),
        P(None, None, "narrow"),
        P("narrow", None),
    )
    return jax.shard_map(
        per_device,
        mesh=mesh,
        in_specs=placed,
        out_specs=(
            P("wide", "narrow", None),
            P("wide", "narrow", None),
            P("wide", None),
            P(),
            P(),
            P(None, None, "narrow"),
            P("narrow", None),
            P(None, "narrow"),
            P(None, None, "narrow"),
            P("narrow", None),
        ),
        check_vma=False,
    )
```

profile of v0, /device:TPU:0, one launch (start us, length us, event | category | flops | bytes accessed | tf_op | source)
XLA Modules:
  0.0 1630.8 jit_solution(4670444608319074679)
XLA Ops:
  15.4 1451.2 %while.32 = (s32[]{:T(128)}, bf16[4,256,768]{2,1,0:T(8,128)(2,1)}, f32[4,256,768]{2,1,0:T(8,128)}, f32[4,4608]{1,0:T(4,128)}, f32[3,3,768]{2,1,0:T(4,128)}, /*in...) while((s32[]{:T(128)}, bf16[4,256,768]{2,1,0:T(8,128)(2,1)}, ...), condition=%wide.region_40.41_spmd.clone, body=%wide.region_0.40_spmd.clone.sunk | while | flops 11619670016 | bytes 582872384 | solution.py:240
  23.6 21.4 %all-gather.7.cloned.1.call-done = bf16[1024,768]{1,0:T(8,128)(2,1)} async-done(((bf16[256,768]{1,0:T(8,128)(2,1)}), bf16[1024,768]{1,0:T(8,128)(2,1)}) %all-gather.7.cloned.1.call-update) | async-done | bytes 1572880 | tf_op jit(solution)/shard_map/while/body/eval_jaxpr/all_gather | solution.py:76
  79.3 38.1 %reduce-scatter.5.cloned.1.call-done = f32[256,768]{1,0:T(8,128)} async-done(((f32[1024,768]{1,0:T(8,128)}), f32[256,768]{1,0:T(8,128)}) %reduce-scatter.5.cloned.1.call-update) | async-done | bytes 786448 | tf_op jit(solution)/shard_map/while/body/eval_jaxpr/reduce_scatter | solution.py:102
  126.5 15.0 all-gather.9.cloned.1.call-done
  199.9 33.5 %reduce-scatter.9.cloned.1.call-done = f32[256,768]{1,0:T(8,128)} async-done(((f32[1024,768]{1,0:T(8,128)}), f32[256,768]{1,0:T(8,128)}) %reduce-scatter.9.cloned.1.call-update) | async-done | bytes 786448 | tf_op jit(solution)/shard_map/while/body/eval_jaxpr/reduce_scatter | solution.py:150
  239.4 24.8 %reduce-scatter.7.cloned.1.call-done = bf16[256,768]{1,0:T(8,128)(2,1)} async-done(((bf16[1024,768]{1,0:T(8,128)(2,1)}), bf16[256,768]{1,0:T(8,128)(2,1)}) %reduce-scatter.7.cloned.1.call-update) | async-done | bytes 393232 | tf_op jit(solution)/shard_map/while/body/eval_jaxpr/reduce_scatter | solution.py:120
  268.8 18.5 %all-gather.13.cloned.1.call-done = bf16[1024,768]{1,0:T(8,128)(2,1)} async-done(((bf16[256,768]{1,0:T(8,128)(2,1)}), bf16[1024,768]{1,0:T(8,128)(2,1)}) %all-gather.13.cloned.1.call-update) | async-done | bytes 1572880 | tf_op jit(solution)/shard_map/while/body/eval_jaxpr/all_gather | solution.py:161
  318.7 12.7 fusion.231
  387.4 18.7 %all-gather.7.cloned.1.call-done = bf16[1024,768]{1,0:T(8,128)(2,1)} async-done(((bf16[256,768]{1,0:T(8,128)(2,1)}), bf16[1024,768]{1,0:T(8,128)(2,1)}) %all-gather.7.cloned.1.call-update) | async-done | bytes 1572880 | tf_op jit(solution)/shard_map/while/body/eval_jaxpr/all_gather | solution.py:76
  440.4 38.1 %reduce-scatter.5.cloned.1.call-done = f32[256,768]{1,0:T(8,128)} async-done(((f32[1024,768]{1,0:T(8,128)}), f32[256,768]{1,0:T(8,128)}) %reduce-scatter.5.cloned.1.call-update) | async-done | bytes 786448 | tf_op jit(solution)/shard_map/while/body/eval_jaxpr/reduce_scatter | solution.py:102
  487.5 15.2 all-gather.9.cloned.1.call-done
  561.0 33.5 %reduce-scatter.9.cloned.1.call-done = f32[256,768]{1,0:T(8,128)} async-done(((f32[1024,768]{1,0:T(8,128)}), f32[256,768]{1,0:T(8,128)}) %reduce-scatter.9.cloned.1.call-update) | async-done | bytes 786448 | tf_op jit(solution)/shard_map/while/body/eval_jaxpr/reduce_scatter | solution.py:150
  600.5 24.8 %reduce-scatter.7.cloned.1.call-done = bf16[256,768]{1,0:T(8,128)(2,1)} async-done(((bf16[1024,768]{1,0:T(8,128)(2,1)}), bf16[256,768]{1,0:T(8,128)(2,1)}) %reduce-scatter.7.cloned.1.call-update) | async-done | bytes 393232 | tf_op jit(solution)/shard_map/while/body/eval_jaxpr/reduce_scatter | solution.py:120
  629.9 18.5 %all-gather.13.cloned.1.call-done = bf16[1024,768]{1,0:T(8,128)(2,1)} async-done(((bf16[256,768]{1,0:T(8,128)(2,1)}), bf16[1024,768]{1,0:T(8,128)(2,1)}) %all-gather.13.cloned.1.call-update) | async-done | bytes 1572880 | tf_op jit(solution)/shard_map/while/body/eval_jaxpr/all_gather | solution.py:161
  679.8 12.7 fusion.231
  748.5 18.7 %all-gather.7.cloned.1.call-done = bf16[1024,768]{1,0:T(8,128)(2,1)} async-done(((bf16[256,768]{1,0:T(8,128)(2,1)}), bf16[1024,768]{1,0:T(8,128)(2,1)}) %all-gather.7.cloned.1.call-update) | async-done | bytes 1572880 | tf_op jit(solution)/shard_map/while/body/eval_jaxpr/all_gather | solution.py:76
  801.5 38.1 %reduce-scatter.5.cloned.1.call-done = f32[256,768]{1,0:T(8,128)} async-done(((f32[1024,768]{1,0:T(8,128)}), f32[256,768]{1,0:T(8,128)}) %reduce-scatter.5.cloned.1.call-update) | async-done | bytes 786448 | tf_op jit(solution)/shard_map/while/body/eval_jaxpr/reduce_scatter | solution.py:102
  848.6 15.2 all-gather.9.cloned.1.call-done
  922.1 33.5 %reduce-scatter.9.cloned.1.call-done = f32[256,768]{1,0:T(8,128)} async-done(((f32[1024,768]{1,0:T(8,128)}), f32[256,768]{1,0:T(8,128)}) %reduce-scatter.9.cloned.1.call-update) | async-done | bytes 786448 | tf_op jit(solution)/shard_map/while/body/eval_jaxpr/reduce_scatter | solution.py:150
  961.6 24.9 %reduce-scatter.7.cloned.1.call-done = bf16[256,768]{1,0:T(8,128)(2,1)} async-done(((bf16[1024,768]{1,0:T(8,128)(2,1)}), bf16[256,768]{1,0:T(8,128)(2,1)}) %reduce-scatter.7.cloned.1.call-update) | async-done | bytes 393232 | tf_op jit(solution)/shard_map/while/body/eval_jaxpr/reduce_scatter | solution.py:120
  991.1 18.5 %all-gather.13.cloned.1.call-done = bf16[1024,768]{1,0:T(8,128)(2,1)} async-done(((bf16[256,768]{1,0:T(8,128)(2,1)}), bf16[1024,768]{1,0:T(8,128)(2,1)}) %all-gather.13.cloned.1.call-update) | async-done | bytes 1572880 | tf_op jit(solution)/shard_map/while/body/eval_jaxpr/all_gather | solution.py:161
  1041.1 12.7 fusion.231
  1109.7 18.7 %all-gather.7.cloned.1.call-done = bf16[1024,768]{1,0:T(8,128)(2,1)} async-done(((bf16[256,768]{1,0:T(8,128)(2,1)}), bf16[1024,768]{1,0:T(8,128)(2,1)}) %all-gather.7.cloned.1.call-update) | async-done | bytes 1572880 | tf_op jit(solution)/shard_map/while/body/eval_jaxpr/all_gather | solution.py:76
  1162.8 38.0 %reduce-scatter.5.cloned.1.call-done = f32[256,768]{1,0:T(8,128)} async-done(((f32[1024,768]{1,0:T(8,128)}), f32[256,768]{1,0:T(8,128)}) %reduce-scatter.5.cloned.1.call-update) | async-done | bytes 786448 | tf_op jit(solution)/shard_map/while/body/eval_jaxpr/reduce_scatter | solution.py:102
  1209.8 15.2 all-gather.9.cloned.1.call-done
  1283.5 33.5 %reduce-scatter.9.cloned.1.call-done = f32[256,768]{1,0:T(8,128)} async-done(((f32[1024,768]{1,0:T(8,128)}), f32[256,768]{1,0:T(8,128)}) %reduce-scatter.9.cloned.1.call-update) | async-done | bytes 786448 | tf_op jit(solution)/shard_map/while/body/eval_jaxpr/reduce_scatter | solution.py:150
  1323.0 24.8 %reduce-scatter.7.cloned.1.call-done = bf16[256,768]{1,0:T(8,128)(2,1)} async-done(((bf16[1024,768]{1,0:T(8,128)(2,1)}), bf16[256,768]{1,0:T(8,128)(2,1)}) %reduce-scatter.7.cloned.1.call-update) | async-done | bytes 393232 | tf_op jit(solution)/shard_map/while/body/eval_jaxpr/reduce_scatter | solution.py:120
  1352.3 18.5 %all-gather.13.cloned.1.call-done = bf16[1024,768]{1,0:T(8,128)(2,1)} async-done(((bf16[256,768]{1,0:T(8,128)(2,1)}), bf16[1024,768]{1,0:T(8,128)(2,1)}) %all-gather.13.cloned.1.call-update) | async-done | bytes 1572880 | tf_op jit(solution)/shard_map/while/body/eval_jaxpr/all_gather | solution.py:161
  1472.7 31.6 %all-gather = bf16[8,4,768]{2,1,0:T(4,128)(2,1)S(1)} all-gather(bf16[1,4,768]{2,1,0:T(4,128)(2,1)S(1)} %fusion.66), channel_id=1, replica_groups=mesh['wide'=8,'narrow'=4] {'wide'}, dimensions={0}, use_global_device_ids=true | all-gather | bytes 55296 | tf_op jit(solution)/shard_map/all_gather | solution.py:247
  1516.6 38.2 %all-reduce.39 = (bf16[3,3,768]{2,1,0:T(4,128)(2,1)S(1)}, bf16[3,3,768]{2,1,0:T(4,128)(2,1)S(1)}) all-reduce(bf16[3,3,768]{2,1,0:T(4,128)(2,1)S(1)} %get-tuple-element.643, bf16[3,3,768]{2,1,0:T(4,128)(2,1)S(1)} %convert_element_type.334), channel_id=1, replica_groups=mesh['wide'=8,'narrow'=4] {'wide'}, use_global_device_ids=true, to_apply=%region_43.44 | all-reduce | flops 13824 | bytes 55296 | tf_op jit(solution)/shard_map/psum | solution.py:254
  1556.0 31.7 %all-gather.1 = bf16[8,4,4608]{2,1,0:T(4,128)(2,1)S(1)} all-gather(bf16[1,4,4608]{2,1,0:T(4,128)(2,1)S(1)} %bitcast.355), channel_id=1, replica_groups=mesh['wide'=8,'narrow'=4] {'wide'}, dimensions={0}, use_global_device_ids=true | all-gather | bytes 331776 | tf_op jit(solution)/shard_map/all_gather | solution.py:248
  1600.7 15.1 all-reduce.43.cloned.1.call-done
  (1322 shorter events, 849.2 us)
Async XLA Ops:
  15.4 29.6 %all-gather.7.cloned.1.call-start = ((), (), s32[]{:S(2)}) async-start(), calls=%async_computation.5 | async-start | bytes 1966080 | tf_op jit(solution)/shard_map/while/body/eval_jaxpr/all_gather | solution.py:76
  22.5 94.8 %reduce-scatter.5.cloned.1.call-start = ((), (), s32[]{:S(2)}) async-start(), calls=%async_computation.6 | async-start | bytes 3932160 | tf_op jit(solution)/shard_map/while/body/eval_jaxpr/reduce_scatter | solution.py:102
  79.2 62.3 %all-gather.9.cloned.1.call-start = ((), (), s32[]{:S(2)}) async-start(), calls=%async_computation.7 | async-start | bytes 1966080 | tf_op jit(solution)/shard_map/while/body/eval_jaxpr/all_gather | solution.py:110
  121.7 40.9 %all-gather.11.cloned.1.call-start = ((), (), s32[]{:S(2)}) async-start(), calls=%async_computation.8 | async-start | bytes 1966080 | tf_op jit(solution)/shard_map/while/body/eval_jaxpr/all_gather | solution.py:135
  124.3 109.1 %reduce-scatter.9.cloned.1.call-start = ((), (), s32[]{:S(2)}) async-start(), calls=%async_computation.10 | async-start | bytes 3932160 | tf_op jit(solution)/shard_map/while/body/eval_jaxpr/reduce_scatter | solution.py:150
  195.3 68.9 %reduce-scatter.7.cloned.1.call-start = ((), (), s32[]{:S(2)}) async-start(), calls=%async_computation.9 | async-start | bytes 1966080 | tf_op jit(solution)/shard_map/while/body/eval_jaxpr/reduce_scatter | solution.py:120
  199.6 87.6 %all-gather.13.cloned.1.call-start = ((), (), s32[]{:S(2)}) async-start(), calls=%async_computation.11 | async-start | bytes 1966080 | tf_op jit(solution)/shard_map/while/body/eval_jaxpr/all_gather | solution.py:161
  267.4 104.3 %reduce-scatter.11.cloned.1.call-start = ((), (), s32[]{:S(2)}) async-start(), calls=%async_computation.12 | async-start | bytes 1966080 | tf_op jit(solution)/shard_map/while/body/eval_jaxpr/reduce_scatter | solution.py:200
  379.2 26.9 %all-gather.7.cloned.1.call-start = ((), (), s32[]{:S(2)}) async-start(), calls=%async_computation.5 | async-start | bytes 1966080 | tf_op jit(solution)/shard_map/while/body/eval_jaxpr/all_gather | solution.py:76
  386.3 92.1 %reduce-scatter.5.cloned.1.call-start = ((), (), s32[]{:S(2)}) async-start(), calls=%async_computation.6 | async-start | bytes 3932160 | tf_op jit(solution)/shard_map/while/body/eval_jaxpr/reduce_scatter | solution.py:102
  440.3 62.3 %all-gather.9.cloned.1.call-start = ((), (), s32[]{:S(2)}) async-start(), calls=%async_computation.7 | async-start | bytes 1966080 | tf_op jit(solution)/shard_map/while/body/eval_jaxpr/all_gather | solution.py:110
  482.8 40.9 %all-gather.11.cloned.1.call-start = ((), (), s32[]{:S(2)}) async-start(), calls=%async_computation.8 | async-start | bytes 1966080 | tf_op jit(solution)/shard_map/while/body/eval_jaxpr/all_gather | solution.py:135
  485.4 109.1 %reduce-scatter.9.cloned.1.call-start = ((), (), s32[]{:S(2)}) async-start(), calls=%async_computation.10 | async-start | bytes 3932160 | tf_op jit(solution)/shard_map/while/body/eval_jaxpr/reduce_scatter | solution.py:150
  556.4 68.9 %reduce-scatter.7.cloned.1.call-start = ((), (), s32[]{:S(2)}) async-start(), calls=%async_computation.9 | async-start | bytes 1966080 | tf_op jit(solution)/shard_map/while/body/eval_jaxpr/reduce_scatter | solution.py:120
  560.8 87.6 %all-gather.13.cloned.1.call-start = ((), (), s32[]{:S(2)}) async-start(), calls=%async_computation.11 | async-start | bytes 1966080 | tf_op jit(solution)/shard_map/while/body/eval_jaxpr/all_gather | solution.py:161
  628.5 104.3 %reduce-scatter.11.cloned.1.call-start = ((), (), s32[]{:S(2)}) async-start(), calls=%async_computation.12 | async-start | bytes 1966080 | tf_op jit(solution)/shard_map/while/body/eval_jaxpr/reduce_scatter | solution.py:200
  747.4 92.1 %reduce-scatter.5.cloned.1.call-start = ((), (), s32[]{:S(2)}) async-start(), calls=%async_computation.6 | async-start | bytes 3932160 | tf_op jit(solution)/shard_map/while/body/eval_jaxpr/reduce_scatter | solution.py:102
  801.4 62.3 %all-gather.9.cloned.1.call-start = ((), (), s32[]{:S(2)}) async-start(), calls=%async_computation.7 | async-start | bytes 1966080 | tf_op jit(solution)/shard_map/while/body/eval_jaxpr/all_gather | solution.py:110
  843.9 40.9 %all-gather.11.cloned.1.call-start = ((), (), s32[]{:S(2)}) async-start(), calls=%async_computation.8 | async-start | bytes 1966080 | tf_op jit(solution)/shard_map/while/body/eval_jaxpr/all_gather | solution.py:135
  846.5 109.1 %reduce-scatter.9.cloned.1.call-start = ((), (), s32[]{:S(2)}) async-start(), calls=%async_computation.10 | async-start | bytes 3932160 | tf_op jit(solution)/shard_map/while/body/eval_jaxpr/reduce_scatter | solution.py:150
  917.5 69.0 %reduce-scatter.7.cloned.1.call-start = ((), (), s32[]{:S(2)}) async-start(), calls=%async_computation.9 | async-start | bytes 1966080 | tf_op jit(solution)/shard_map/while/body/eval_jaxpr/reduce_scatter | solution.py:120
  921.8 87.7 %all-gather.13.cloned.1.call-start = ((), (), s32[]{:S(2)}) async-start(), calls=%async_computation.11 | async-start | bytes 1966080 | tf_op jit(solution)/shard_map/while/body/eval_jaxpr/all_gather | solution.py:161
  989.8 104.3 %reduce-scatter.11.cloned.1.call-start = ((), (), s32[]{:S(2)}) async-start(), calls=%async_computation.12 | async-start | bytes 1966080 | tf_op jit(solution)/shard_map/while/body/eval_jaxpr/reduce_scatter | solution.py:200
  1101.5 26.9 %all-gather.7.cloned.1.call-start = ((), (), s32[]{:S(2)}) async-start(), calls=%async_computation.5 | async-start | bytes 1966080 | tf_op jit(solution)/shard_map/while/body/eval_jaxpr/all_gather | solution.py:76
  1108.7 92.1 %reduce-scatter.5.cloned.1.call-start = ((), (), s32[]{:S(2)}) async-start(), calls=%async_computation.6 | async-start | bytes 3932160 | tf_op jit(solution)/shard_map/while/body/eval_jaxpr/reduce_scatter | solution.py:102
  1162.7 62.3 %all-gather.9.cloned.1.call-start = ((), (), s32[]{:S(2)}) async-start(), calls=%async_computation.7 | async-start | bytes 1966080 | tf_op jit(solution)/shard_map/while/body/eval_jaxpr/all_gather | solution.py:110
  1205.2 41.1 %all-gather.11.cloned.1.call-start = ((), (), s32[]{:S(2)}) async-start(), calls=%async_computation.8 | async-start | bytes 1966080 | tf_op jit(solution)/shard_map/while/body/eval_jaxpr/all_gather | solution.py:135
  1207.8 109.2 %reduce-scatter.9.cloned.1.call-start = ((), (), s32[]{:S(2)}) async-start(), calls=%async_computation.10 | async-start | bytes 3932160 | tf_op jit(solution)/shard_map/while/body/eval_jaxpr/reduce_scatter | solution.py:150
  1278.9 68.9 %reduce-scatter.7.cloned.1.call-start = ((), (), s32[]{:S(2)}) async-start(), calls=%async_computation.9 | async-start | bytes 1966080 | tf_op jit(solution)/shard_map/while/body/eval_jaxpr/reduce_scatter | solution.py:120
  1283.2 87.6 %all-gather.13.cloned.1.call-start = ((), (), s32[]{:S(2)}) async-start(), calls=%async_computation.11 | async-start | bytes 1966080 | tf_op jit(solution)/shard_map/while/body/eval_jaxpr/all_gather | solution.py:161
  1351.0 104.3 %reduce-scatter.11.cloned.1.call-start = ((), (), s32[]{:S(2)}) async-start(), calls=%async_computation.12 | async-start | bytes 1966080 | tf_op jit(solution)/shard_map/while/body/eval_jaxpr/reduce_scatter | solution.py:200
  1466.7 149.1 %all-reduce.43.cloned.1.call-start = ((), (), s32[]{:S(2)}) async-start(), calls=%async_computation.4 | async-start | bytes 7077888 | tf_op jit(solution)/shard_map/psum | solution.py:255
  (378 other events, 2839.4 us)
Sparse Core Ops, SparseCore 0:
  22.6 22.3 all-gather.6
  79.4 37.9 reduce-scatter.4
  121.9 19.6 all-gather.8
  143.0 19.6 all-gather.10
  195.4 37.9 reduce-scatter.8
  236.0 28.1 reduce-scatter.6
  267.5 19.6 all-gather.12
  343.5 28.1 reduce-scatter.10
  386.4 19.6 all-gather.6
  440.5 37.9 reduce-scatter.4
  483.0 19.6 all-gather.8
  504.1 19.6 all-gather.10
  556.5 37.9 reduce-scatter.8
  597.1 28.1 reduce-scatter.6
  628.7 19.6 all-gather.12
  704.6 28.1 reduce-scatter.10
  747.5 19.6 all-gather.6
  801.6 37.9 reduce-scatter.4
  844.1 19.6 all-gather.8
  865.2 19.6 all-gather.10
  917.6 37.9 reduce-scatter.8
  958.3 28.1 reduce-scatter.6
  989.9 19.6 all-gather.12
  1065.9 28.1 reduce-scatter.10
  1108.8 19.6 all-gather.6
  1162.8 37.9 reduce-scatter.4
  1205.3 19.6 all-gather.8
  1226.6 19.6 all-gather.10
  1279.0 37.9 reduce-scatter.8
  1319.5 28.1 reduce-scatter.6
  1351.1 19.6 all-gather.12
  1427.1 28.1 reduce-scatter.10
Sparse Core Ops, SparseCore 1:
  1472.7 143.0 all-reduce.42
where the time goes:
time: 1640 us; the launch traced here: 1630 us
  waiting for transfers between devices  669 us (41%)
  other arithmetic  353 us (22%)
  matrix products  240 us (15%)
  local copies, waits for them, and re-layouts  223 us (14%)
  blocking collectives  114 us (7%)
    reduce_scatter x4, waiting for transfers between devices, one_latent(): lax.psum_scatter(jnp.dot(context, w_out, preferred_element_type=jnp.float...  152 us
    reduce_scatter x4, waiting for transfers between devices, one_latent(): lax.psum_scatter(lax.dot_general(grad_hidden, w_up, CONTRACT_COLS, prefer...  134 us
    reduce_scatter x4, waiting for transfers between devices, one_latent(): lax.psum_scatter(jnp.dot(lax.slice_in_dim(activated, 0, shard_rows * lax....  99.2 us
    all_gather x4, waiting for transfers between devices, one_latent(): lax.all_gather((normed_one * (1.0 + scale_one) + shift_one).astype(jnp.bf...  77.6 us
    all_gather x4, waiting for transfers between devices, one_latent(): lax.all_gather((grad_after * gate_one).astype(jnp.bfloat16), 'narrow', ax...  73.9 us
    all_gather x4, waiting for transfers between devices, one_latent(): lax.all_gather((normed_two * (1.0 + scale_two) + shift_two).astype(jnp.bf...  60.6 us
    dot_general x4, matrix products, one_latent(): jnp.einsum('tse,dte->sd', grad_projected, w_qkv, preferred_element_type=j...  50.9 us
    add_any x8, other arithmetic, conv_grid(): padded[tap_row:tap_row + SIDE, tap_col:tap_col + SIDE]  48.1 us
  transfers between devices with their start and end apart: 33, of which 33 were waited for; matrix products, arithmetic and copies ran while one was open for 12% of the time, Pallas kernels for 0%

commit v1 on v0

v1 whole, which is shorter than its diff:
```python
from functools import partial

import jax
import jax.numpy as jnp
from jax import lax
from jax.experimental import pallas as pl
from jax.experimental.pallas import tpu as pltpu
from jax.sharding import PartitionSpec as P

HEAD_DIM = 64
SIDE = 32
HALF = SIDE // 2
PHASE = HALF * HALF
PAD = PHASE + 2 * HALF
LANES = 128
ROWS = 64
CHUNK = 256
LOG2E = 1.4426950408889634
GELU_C = 0.7978845608028654
GELU_A = 0.044715
MIB = 1 << 20
F32 = jnp.float32
BF16 = jnp.bfloat16

NN = (((1,), (0,)), ((), ()))
NT = (((1,), (1,)), ((), ()))
TN = (((0,), (0,)), ((), ()))


def mm(left, right, dims):
    return lax.dot_general(left, right, dims, preferred_element_type=F32)


def ds(start, size, unit=None):
    return pl.ds(pl.multiple_of(start, unit or size), size)


def tap_source(parity, tap):
    return {-1: (1, -1), 0: (0, 0), 1: (1, 0), 2: (0, 1)}[parity + tap - 1]


def shift_cols(base, shifted, lanes):
    col = lax.broadcasted_iota(jnp.int32, (ROWS, LANES), 0) % HALF

    def rows_step(step, carry):
        for group in range(4):
            rows = ds(HALF + step * ROWS, ROWS, HALF)
            value = base[group, rows, lanes]
            if group % 2:
                moved = jnp.where(col == 0, 0.0, pltpu.roll(value, 1, 0))
            else:
                moved = jnp.where(col == HALF - 1, 0.0, pltpu.roll(value, ROWS - 1, 0))
            shifted[group, rows, lanes] = moved
        return carry

    lax.fori_loop(0, PHASE // ROWS, rows_step, 0)


def clear_edges(ref):
    edge = jnp.zeros((HALF, ref.shape[-1]), ref.dtype)
    for group in range(4):
        ref[group, :HALF, :] = edge
        ref[group, PAD - HALF :, :] = edge


def tap_value(base, shifted, group, tap_row, tap_col, start, lanes):
    src_row, row_move = tap_source(group // 2, tap_row)
    src_col, col_move = tap_source(group % 2, tap_col)
    ref = base if col_move == 0 else shifted
    return ref[2 * src_row + src_col, ds(HALF + row_move * HALF + start, ROWS, HALF), lanes]


def normed(values_in):
    mean_val = jnp.mean(values_in, axis=-1, keepdims=True)
    centred = values_in - mean_val
    inv = lax.rsqrt(jnp.mean(centred * centred, axis=-1, keepdims=True) + 1e-06)
    return centred * inv, inv


def norm_back(unit, inv, grad):
    mean_grad = jnp.mean(grad, axis=-1, keepdims=True)
    mean_dot = jnp.mean(grad * unit, axis=-1, keepdims=True)
    return (grad - mean_grad - unit * mean_dot) * inv


def attn_forward_kernel(
    live_ref, x_ref, cot_ref, mod_ref, taps_ref, wqkv_ref, wout_ref,
    u_ref, qkv_ref, probs_ref, ctx_ref, att_ref, x1_ref, h2_ref, h2t_ref, db_ref,
    base, shifted,
):
    width = x_ref.shape[1]
    rows_all = x_ref.shape[0]
    shift_one, scale_one, gate_one = mod_ref[0:1, :], mod_ref[1:2, :], mod_ref[2:3, :]
    shift_two, scale_two, gate_two = mod_ref[3:4, :], mod_ref[4:5, :], mod_ref[5:6, :]
    clear_edges(base)
    clear_edges(shifted)

    def norm_step(step, carry):
        group, part = step // (PHASE // ROWS), step % (PHASE // ROWS)
        unit, _ = normed(x_ref[ds(step * ROWS, ROWS), :].astype(F32))
        h_one = (unit * (1.0 + scale_one) + shift_one).astype(BF16)
        base[group, ds(HALF + part * ROWS, ROWS, HALF), :] = h_one.astype(F32)
        return carry

    lax.fori_loop(0, rows_all // ROWS, norm_step, 0)

    def conv_step(block, carry):
        lanes = ds(block * LANES, LANES)
        shift_cols(base, shifted, lanes)
        taps = [taps_ref[t : t + 1, lanes] for t in range(9)]

        def rows_step(step, carry):
            for group in range(4):
                total = jnp.zeros((ROWS, LANES), F32)
                for tap in range(9):
                    total += taps[tap] * tap_value(
                        base, shifted, group, tap // 3, tap % 3, step * ROWS, lanes
                    )
                u_ref[ds(group * PHASE + step * ROWS, ROWS), lanes] = total.astype(BF16)
            return carry

        return lax.fori_loop(0, PHASE // ROWS, rows_step, carry)

    lax.fori_loop(0, width // LANES, conv_step, 0)

    def project_step(step, carry):
        rows = ds(step * PHASE, PHASE)
        for part in range(3):
            cols = slice(part * width, (part + 1) * width)
            qkv_ref[rows, cols] = mm(u_ref[rows, :], wqkv_ref[:, cols], NT).astype(BF16)
        return carry

    lax.fori_loop(0, 4, project_step, 0)

    pairs = width // LANES
    first = lax.broadcasted_iota(jnp.int32, (PHASE, LANES), 1) < HEAD_DIM
    zero = jnp.zeros((PHASE, LANES), BF16)

    def attend_step(step, carry):
        group, pair = step // pairs, step % pairs
        rows = ds(group * PHASE, PHASE)
        query = qkv_ref[rows, ds(pair * LANES, LANES)]
        key = qkv_ref[rows, ds(width + pair * LANES, LANES)]
        value = qkv_ref[rows, ds(2 * width + pair * LANES, LANES)]
        found = []
        for head in range(2):
            own = jnp.where(first, query, zero) if head == 0 else jnp.where(first, zero, query)
            scores = mm(key, own, NT)
            top = jnp.max(scores, axis=0, keepdims=True)
            raised = jnp.exp2((scores - top) * (LOG2E * HEAD_DIM**-0.5))
            probs = (raised * (1.0 / jnp.sum(raised, axis=0, keepdims=True))).astype(BF16)
            probs_ref[step, :, head * PHASE : (head + 1) * PHASE] = probs
            found.append(mm(probs, value, TN))
        ctx_ref[rows, ds(pair * LANES, LANES)] = jnp.where(first, found[0], found[1]).astype(BF16)
        return carry

    lax.fori_loop(0, 4 * pairs, attend_step, 0)

    def out_step(step, carry):
        rows = ds(step * PHASE, PHASE)
        att_ref[rows, :] = mm(ctx_ref[rows, :], wout_ref[...], NN)
        return carry

    lax.fori_loop(0, 4, out_step, 0)
    live = live_ref[0, 0]

    def second_step(step, carry):
        rows = ds(step * ROWS, ROWS)
        after = x_ref[rows, :].astype(F32) + gate_one * att_ref[rows, :]
        x1_ref[rows, :] = after
        unit, _ = normed(after)
        h2_ref[rows, :] = (unit * (1.0 + scale_two) + shift_two).astype(BF16)
        db_ref[rows, :] = (cot_ref[rows, :].astype(F32) * live * gate_two).astype(BF16)
        return carry

    lax.fori_loop(0, rows_all // ROWS, second_step, 0)
    for part in range(4):
        h2t_ref[:, part * PHASE : (part + 1) * PHASE] = h2_ref[
            part * PHASE : (part + 1) * PHASE, :
        ].T


def whole(memory=pltpu.VMEM):
    return pl.BlockSpec(memory_space=memory)


def attn_forward(live, x, cot, mod, taps, wqkv, wout):
    rows, width = x.shape
    steps = 4 * (width // LANES)
    shape = jax.ShapeDtypeStruct
    return pl.pallas_call(
        attn_forward_kernel,
        out_shape=(
            shape((rows, width), BF16),
            shape((rows, 3 * width), BF16),
            shape((steps, PHASE, 2 * PHASE), BF16),
            shape((rows, width), BF16),
            shape((rows, width), F32),
            shape((rows, width), F32),
            shape((rows, width), BF16),
            shape((width, rows), BF16),
            shape((rows, width), BF16),
        ),
        in_specs=[whole(pltpu.SMEM)] + [whole()] * 6,
        out_specs=(whole(),) * 9,
        scratch_shapes=[pltpu.VMEM((4, PAD, width), F32), pltpu.VMEM((4, PAD, width), F32)],
        compiler_params=pltpu.CompilerParams(vmem_limit_bytes=56 * MIB),
        name="attn_forward",
    )(live, x, cot, mod, taps, wqkv, wout)


def ffn_kernel(
    h2_ref, h2t_ref, db_ref, wup_ref, wdown_ref, taps_ref,
    branch_ref, dh2_ref, dwup_ref, dwdown_ref, dtaps_ref,
    hid, hid_moved, grad, grad_moved, slope, act, dhid,
):
    rows_all = h2_ref.shape[0]

    @pl.when(pl.program_id(0) == 0)
    def _():
        for ref in (hid, hid_moved, grad, grad_moved):
            clear_edges(ref)
        branch_ref[...] = jnp.zeros_like(branch_ref)
        dh2_ref[...] = jnp.zeros_like(dh2_ref)

    def up_step(group, carry):
        rows = ds(group * PHASE, PHASE)
        hid[group, HALF : HALF + PHASE, :] = mm(h2_ref[rows, :], wup_ref[0], NN)
        return carry

    lax.fori_loop(0, 4, up_step, 0)

    for block in range(CHUNK // LANES):
        lanes = slice(block * LANES, (block + 1) * LANES)
        shift_cols(hid, hid_moved, lanes)
        taps = [taps_ref[0, t : t + 1, lanes] for t in range(9)]

        def act_step(step, carry):
            for group in range(4):
                total = jnp.zeros((ROWS, LANES), F32)
                for tap in range(9):
                    total += taps[tap] * tap_value(
                        hid, hid_moved, group, tap // 3, tap % 3, step * ROWS, lanes
                    )
                square = total * total
                turn = jnp.tanh(total * (square * (GELU_C * GELU_A) + GELU_C))
                half = 0.5 * turn + 0.5
                bend = total * (half - half * half)
                rows = ds(group * PHASE + step * ROWS, ROWS)
                act[rows, lanes] = (total * half).astype(BF16)
                slope[rows, lanes] = half + bend * (
                    square * (6.0 * GELU_C * GELU_A) + 2.0 * GELU_C
                )
            return carry

        lax.fori_loop(0, PHASE // ROWS, act_step, 0)

    def dact_step(group, carry):
        rows = ds(group * PHASE, PHASE)
        dact = mm(db_ref[rows, :], wdown_ref[0], NT)
        grad[group, HALF : HALF + PHASE, :] = dact * slope[rows, :]
        return carry

    lax.fori_loop(0, 4, dact_step, 0)

    for block in range(CHUNK // LANES):
        lanes = slice(block * LANES, (block + 1) * LANES)
        shift_cols(grad, grad_moved, lanes)
        conv_back(grad, grad_moved, hid, lanes, [taps_ref[0, t : t + 1, lanes] for t in range(9)],
                  dtaps_ref.at[0], dhid)

    def final_step(group, carry):
        rows = ds(group * PHASE, PHASE)
        branch_ref[rows, :] += mm(act[rows, :], wdown_ref[0], NN)
        dh2_ref[rows, :] += mm(dhid[rows, :], wup_ref[0], NT)
        return carry

    lax.fori_loop(0, 4, final_step, 0)
    dwup_ref[0] = mm(h2t_ref[...], dhid[...], NN).astype(BF16)
    dwdown_ref[0] = mm(act[...], db_ref[...], TN).astype(BF16)


def conv_back(grad, grad_moved, source, lanes, taps, dtaps_ref, out_ref):
    def rows_step(step, sums):
        sums = list(sums)
        for group in range(4):
            total = jnp.zeros((ROWS, LANES), F32)
            own = source[group, ds(HALF + step * ROWS, ROWS, HALF), lanes]
            for tap in range(9):
                moved = tap_value(
                    grad, grad_moved, group, 2 - tap // 3, 2 - tap % 3, step * ROWS, lanes
                )
                total += taps[tap] * moved
                sums[tap] += (own * moved).reshape(ROWS // 8, 8, LANES).sum(axis=0)
            out_ref[ds(group * PHASE + step * ROWS, ROWS), lanes] = total.astype(out_ref.dtype)
        return tuple(sums)

    start = tuple(jnp.zeros((8, LANES), F32) for _ in range(9))
    sums = lax.fori_loop(0, PHASE // ROWS, rows_step, start)
    for tap in range(9):
        dtaps_ref[tap : tap + 1, lanes] = jnp.sum(sums[tap], axis=0, keepdims=True)


def ffn(h2, h2t, db, wup, wdown, taps):
    rows, width = h2.shape
    shards, _, local = wup.shape
    per = local // CHUNK
    shape = jax.ShapeDtypeStruct
    keep = lambda *block: pl.BlockSpec(block, lambda c: (0,) * len(block))
    return pl.pallas_call(
        ffn_kernel,
        grid=(shards * per,),
        out_shape=(
            shape((rows, width), F32),
            shape((rows, width), F32),
            shape(wup.shape, BF16),
            shape(wdown.shape, BF16),
            shape(taps.shape, F32),
        ),
        in_specs=[
            keep(rows, width),
            keep(width, rows),
            keep(rows, width),
            pl.BlockSpec((1, width, CHUNK), lambda c: (c // per, 0, c % per)),
            pl.BlockSpec((1, CHUNK, width), lambda c: (c // per, c % per, 0)),
            pl.BlockSpec((1, 9, CHUNK), lambda c: (c // per, 0, c % per)),
        ],
        out_specs=(
            keep(rows, width),
            keep(rows, width),
            pl.BlockSpec((1, width, CHUNK), lambda c: (c // per, 0, c % per)),
            pl.BlockSpec((1, CHUNK, width), lambda c: (c // per, c % per, 0)),
            pl.BlockSpec((1, 9, CHUNK), lambda c: (c // per, 0, c % per)),
        ),
        scratch_shapes=[pltpu.VMEM((4, PAD, CHUNK), F32)] * 4
        + [pltpu.VMEM((rows, CHUNK), F32)]
        + [pltpu.VMEM((rows, CHUNK), BF16)] * 2,
        compiler_params=pltpu.CompilerParams(vmem_limit_bytes=56 * MIB),
        name="feed_forward",
    )(h2, h2t, db, wup, wdown, taps)


def mid_kernel(
    live_ref, x1_ref, cot_ref, branch_ref, dh2_ref, att_ref, ctx_ref, mod_ref, wout_ref,
    block_ref, dx1_ref, dctx_ref, dwout_ref, dmod_ref,
    datt,
):
    rows_all, width = x1_ref.shape
    gate_one, scale_two, gate_two = mod_ref[2:3, :], mod_ref[4:5, :], mod_ref[5:6, :]
    live = live_ref[0, 0]

    def fold(value):
        return value.reshape(ROWS // 8, 8, width).sum(axis=0)

    def rows_step(step, sums):
        rows = ds(step * ROWS, ROWS)
        after = x1_ref[rows, :]
        dout = cot_ref[rows, :].astype(F32) * live
        branch = branch_ref[rows, :]
        block_ref[rows, :] = ((after + gate_two * branch) * live).astype(BF16)
        unit, inv = normed(after)
        dh2 = dh2_ref[rows, :]
        dx1 = dout + norm_back(unit, inv, dh2 * (1.0 + scale_two))
        dx1_ref[rows, :] = dx1
        datt[rows, :] = (dx1 * gate_one).astype(BF16)
        found = (dx1 * att_ref[rows, :], dh2, dh2 * unit, dout * branch)
        return tuple(total + fold(one) for total, one in zip(sums, found))

    start = tuple(jnp.zeros((8, width), F32) for _ in range(4))
    sums = lax.fori_loop(0, rows_all // ROWS, rows_step, start)
    for at in range(4):
        dmod_ref[at : at + 1, :] = jnp.sum(sums[at], axis=0, keepdims=True)

    def ctx_step(step, carry):
        rows = ds(step * PHASE, PHASE)
        dctx_ref[rows, :] = mm(datt[rows, :], wout_ref[...], NT).astype(BF16)
        return carry

    lax.fori_loop(0, 4, ctx_step, 0)
    for part in range(3):
        cols = slice(part * PHASE, (part + 1) * PHASE)
        dwout_ref[cols, :] = mm(ctx_ref[:, cols], datt[...], TN).astype(BF16)


def mid(live, x1, cot, branch, dh2, att, ctx, mod, wout):
    rows, width = x1.shape
    shape = jax.ShapeDtypeStruct
    return pl.pallas_call(
        mid_kernel,
        out_shape=(
            shape((rows, width), BF16),
            shape((rows, width), F32),
            shape((rows, width), BF16),
            shape(wout.shape, BF16),
            shape((4, width), F32),
        ),
        in_specs=[whole(pltpu.SMEM)] + [whole()] * 8,
        out_specs=(whole(),) * 5,
        scratch_shapes=[pltpu.VMEM((rows, width), BF16)],
        compiler_params=pltpu.CompilerParams(vmem_limit_bytes=56 * MIB),
        name="residual_backward",
    )(live, x1, cot, branch, dh2, att, ctx, mod, wout)


def attn_backward_kernel(
    u_ref, qkv_ref, probs_ref, dctx_ref, dqkv_ref, dw_ref
):
    rows_all, width = u_ref.shape
    pairs = width // LANES
    first = lax.broadcasted_iota(jnp.int32, (PHASE, LANES), 1) < HEAD_DIM
    zero = jnp.zeros((PHASE, LANES), BF16)
    scale = HEAD_DIM**-0.5

    def attend_step(step, carry):
        group, pair = step // pairs, step % pairs
        rows = ds(group * PHASE, PHASE)
        query = qkv_ref[rows, ds(pair * LANES, LANES)]
        key = qkv_ref[rows, ds(width + pair * LANES, LANES)]
        value = qkv_ref[rows, ds(2 * width + pair * LANES, LANES)]
        dctx = dctx_ref[rows, ds(pair * LANES, LANES)]
        dq, dk, dv = [], None, None
        for head in range(2):
            own = lambda full: jnp.where(first, full, zero) if head == 0 else jnp.where(first, zero, full)
            probs = probs_ref[step, :, head * PHASE : (head + 1) * PHASE]
            probs_f = probs.astype(F32)
            dctx_own, query_own = own(dctx), own(query)
            dprobs = mm(value, dctx_own, NT)
            inner = jnp.sum(dprobs * probs_f, axis=0, keepdims=True)
            dscores = (probs_f * (dprobs - inner)).astype(BF16)
            dv_one = mm(probs, dctx_own, NN)
            dk_one = mm(dscores, query_own, NN)
            dv = dv_one if dv is None else dv + dv_one
            dk = dk_one if dk is None else dk + dk_one
            dq.append(mm(dscores, key, TN))
        dqkv_ref[rows, ds(pair * LANES, LANES)] = (
            jnp.where(first, dq[0], dq[1]) * scale
        ).astype(BF16)
        dqkv_ref[rows, ds(width + pair * LANES, LANES)] = (dk * scale).astype(BF16)
        dqkv_ref[rows, ds(2 * width + pair * LANES, LANES)] = dv.astype(BF16)
        return carry

    lax.fori_loop(0, 4 * pairs, attend_step, 0)
    for part in range(3):
        cols = slice(part * width, (part + 1) * width)

        def weight_step(block, carry, cols=cols, part=part):
            out_rows = ds(block * PHASE, PHASE)
            left = dqkv_ref[:, ds(part * width + block * PHASE, PHASE)]
            dw_ref[out_rows, cols] = mm(left, u_ref[...], TN).astype(BF16)
            return carry

        lax.fori_loop(0, width // PHASE, weight_step, 0)


def attn_backward(u, qkv, probs, dctx):
    rows, width = u.shape
    shape = jax.ShapeDtypeStruct
    return pl.pallas_call(
        attn_backward_kernel,
        out_shape=(shape((rows, 3 * width), BF16), shape((width, 3 * width), BF16)),
        in_specs=[whole()] * 4,
        out_specs=(whole(),) * 2,
        compiler_params=pltpu.CompilerParams(vmem_limit_bytes=56 * MIB),
        name="attn_backward",
    )(u, qkv, probs, dctx)


def input_backward_kernel(
    x_ref, dx1_ref, dqkv_ref, mod_ref, taps_ref, wqkv_ref,
    dx_ref, dmod_ref, dtaps_ref,
    base, shifted, first_in, dh1,
):
    rows_all, width = x_ref.shape
    shift_one, scale_one = mod_ref[0:1, :], mod_ref[1:2, :]
    clear_edges(base)
    clear_edges(shifted)

    def norm_step(step, carry):
        group, part = step // (PHASE // ROWS), step % (PHASE // ROWS)
        unit, _ = normed(x_ref[ds(step * ROWS, ROWS), :].astype(F32))
        h_one = (unit * (1.0 + scale_one) + shift_one).astype(BF16)
        first_in[group, ds(HALF + part * ROWS, ROWS, HALF), :] = h_one.astype(F32)
        return carry

    lax.fori_loop(0, rows_all // ROWS, norm_step, 0)

    def du_step(group, carry):
        rows = ds(group * PHASE, PHASE)
        total = None
        for part in range(3):
            cols = slice(part * width, (part + 1) * width)
            one = mm(dqkv_ref[rows, cols], wqkv_ref[:, cols], NN)
            total = one if total is None else total + one
        base[group, HALF : HALF + PHASE, :] = total
        return carry

    lax.fori_loop(0, 4, du_step, 0)

    def conv_step(block, carry):
        lanes = ds(block * LANES, LANES)
        shift_cols(base, shifted, lanes)
        conv_back(base, shifted, first_in, lanes, [taps_ref[t : t + 1, lanes] for t in range(9)],
                  dtaps_ref, dh1)
        return carry

    lax.fori_loop(0, width // LANES, conv_step, 0)

    def fold(value):
        return value.reshape(ROWS // 8, 8, width).sum(axis=0)

    def rows_step(step, sums):
        rows = ds(step * ROWS, ROWS)
        unit, inv = normed(x_ref[rows, :].astype(F32))
        grad = dh1[rows, :]
        dx = dx1_ref[rows, :] + norm_back(unit, inv, grad * (1.0 + scale_one))
        dx_ref[rows, :] = dx.astype(BF16)
        return tuple(total + fold(one) for total, one in zip(sums, (grad, grad * unit)))

    start = tuple(jnp.zeros((8, width), F32) for _ in range(2))
    sums = lax.fori_loop(0, rows_all // ROWS, rows_step, start)
    for at in range(2):
        dmod_ref[at : at + 1, :] = jnp.sum(sums[at], axis=0, keepdims=True)


def input_backward(x, dx1, dqkv, mod, taps, wqkv):
    rows, width = x.shape
    shape = jax.ShapeDtypeStruct
    return pl.pallas_call(
        input_backward_kernel,
        out_shape=(shape((rows, width), BF16), shape((2, width), F32), shape((9, width), F32)),
        in_specs=[whole()] * 6,
        out_specs=(whole(),) * 3,
        scratch_shapes=[pltpu.VMEM((4, PAD, width), F32)] * 3 + [pltpu.VMEM((rows, width), F32)],
        compiler_params=pltpu.CompilerParams(vmem_limit_bytes=56 * MIB),
        name="input_backward",
    )(x, dx1, dqkv, mod, taps, wqkv)


def to_groups(shard):
    latents, rows, width = shard.shape
    split = shard.reshape(latents, rows // (2 * SIDE), 2, HALF, 2, width)
    return split.transpose(0, 2, 4, 1, 3, 5).reshape(latents, 4, rows // 4, width)


def from_groups(groups):
    latents, _, rows, width = groups.shape
    split = groups.reshape(latents, 2, 2, rows // HALF, HALF, width)
    return split.transpose(0, 3, 1, 4, 2, 5).reshape(latents, 4 * rows, width)


def per_device(
    tokens, condition, cotangent, counts, w_ada, k_attn, w_qkv, w_out, w_up, k_ffn, w_down
):
    lat_dev, shard_rows, width = tokens.shape
    here = lax.axis_index("narrow")
    rows_all = shard_rows * lat_dev
    local = w_up.shape[1]
    gather = partial(lax.all_gather, axis_name="narrow")

    def latent_in(shard):
        return lax.all_to_all(to_groups(shard), "narrow", 0, 2, tiled=True).reshape(rows_all, width)

    def latent_out(latent):
        parts = latent.reshape(1, 4, rows_all // 4, width)
        return from_groups(lax.all_to_all(parts, "narrow", 2, 0, tiled=True))

    x = latent_in(tokens)
    cot = latent_in(cotangent)
    qkv_t = w_qkv.transpose(2, 1, 0).reshape(w_qkv.shape[2], 3 * width)
    wqkv = gather(qkv_t, tiled=True)
    wout = gather(w_out, tiled=True)
    wup = gather(w_up)
    wdown = gather(w_down)
    ffn_taps = gather(k_ffn.reshape(9, local)).astype(F32)
    attn_taps = k_attn.reshape(9, width).astype(F32)

    cond_f = condition.astype(F32)
    silu_low = jax.nn.silu(cond_f).astype(BF16)
    own_silu = lax.dynamic_slice_in_dim(silu_low, here, 1, 0)
    mod = mm(own_silu, w_ada, NN).reshape(6, width)
    live = (here < counts[0]).astype(F32).reshape(1, 1)

    u, qkv, probs, ctx, att, x1, h2, h2t, db = attn_forward(
        live, x, cot, mod, attn_taps, wqkv, wout
    )
    branch, dh2, dwup, dwdown, dffn_taps = ffn(h2, h2t, db, wup, wdown, ffn_taps)
    block_g, dx1, dctx, dwout, dmod_mid = mid(live, x1, cot, branch, dh2, att, ctx, mod, wout)
    dqkv, dwqkv = attn_backward(u, qkv, probs, dctx)
    dx, dmod_first, dattn_taps = input_backward(x, dx1, dqkv, mod, attn_taps, wqkv)

    block = latent_out(block_g)
    grad_tokens = latent_out(dx).astype(F32)

    def reduce(parts):
        return lax.psum(lax.psum_scatter(parts, "narrow", scatter_dimension=0, tiled=True), "wide")

    shared = jnp.concatenate(
        [dwup, dwdown, jnp.pad(dffn_taps, ((0, 0), (0, 7), (0, 0))).astype(BF16)], axis=1
    ).reshape(lat_dev * (2 * width + 16), local)
    late = jnp.concatenate(
        [dwout.reshape(lat_dev, -1, width), dwqkv.reshape(lat_dev, -1, width)], axis=1
    ).reshape(-1, width)
    shared = reduce(shared).astype(F32)
    late = reduce(late).astype(F32)
    grad_w_up, grad_w_down = shared[:width], shared[width : 2 * width]
    grad_k_ffn = shared[2 * width : 2 * width + 9].reshape(3, 3, local)
    heads_width = w_out.shape[0]
    grad_w_out = late[:heads_width]
    grad_w_qkv = late[heads_width:].reshape(heads_width, 3, width).transpose(2, 1, 0)

    dmod = jnp.concatenate([dmod_first, dmod_mid], axis=0)
    small = jnp.concatenate([dmod, dattn_taps, jnp.zeros((1, width), F32)], axis=0).astype(BF16)
    small_all = lax.all_gather(small, ("wide", "narrow"))
    silu_all = lax.all_gather(silu_low, "wide", tiled=True)
    mod_all = small_all[:, :6].reshape(-1, 6 * width)
    grad_k_attn = small_all[:, 6:15].astype(F32).sum(axis=0).reshape(3, 3, width)
    grad_w_ada = mm(silu_all, mod_all, TN)
    mod_low = lax.dynamic_slice_in_dim(mod_all, lax.axis_index("wide") * lat_dev, lat_dev, 0)
    grad_silu = mm(mod_low, w_ada, NT)
    _, pull_silu = jax.vjp(jax.nn.silu, cond_f)
    (grad_condition,) = pull_silu(grad_silu)
    return (
        block,
        grad_tokens,
        grad_condition,
        grad_w_ada,
        grad_k_attn,
        grad_w_qkv,
        grad_w_out,
        grad_w_up,
        grad_k_ffn,
        grad_w_down,
    )


def solution(mesh):
    placed = (
        P("wide", "narrow", None),
        P("wide", None),
        P("wide", "narrow", None),
        P("wide"),
        P(),
        P(),
        P(None, None, "narrow"),
        P("narrow", None),
        P(None, "narrow"),
        P(None, None, "narrow"),
        P("narrow", None),
    )
    return jax.shard_map(
        per_device,
        mesh=mesh,
        in_specs=placed,
        out_specs=(
            P("wide", "narrow", None),
            P("wide", "narrow", None),
            P("wide", None),
            P(),
            P(),
            P(None, None, "narrow"),
            P("narrow", None),
            P(None, "narrow"),
            P(None, None, "narrow"),
            P("narrow", None),
        ),
        check_vma=False,
    )
```

time: 1640 us -> 619 us (0.38)
  waiting for transfers between devices: 669 us -> 168 us
  other arithmetic: 353 us -> 15.2 us
  matrix products: 240 us -> 17.8 us
  Pallas kernels: 0 us -> 220 us
  local copies, waits for them, and re-layouts: 223 us -> 56 us
    reduce_scatter x16 -> x2, waiting for transfers between devices: 399 us -> 120 us  [reduce(): lax.psum_scatter(parts, 'narrow', scatter_dimension=0, tiled=True)]
    all_gather x16 -> x4, waiting for transfers between devices: 254 us -> 24.2 us  [the longest x1 24.2 us: per_device(): wdown = gather(w_down)]
    pallas_call x0 -> x5, Pallas kernels: none -> 220 us  [the longest x1 97.1 us: ffn(): pl.pallas_call(ffn_kernel, grid=(shards * per,), out_shape=(shape((rows,...]
    dot_general x67 -> x3, matrix products: 224 us -> 17.8 us  [mm(): return lax.dot_general(left, right, dims, preferred_element_type=F32)]
    reduce_sum x44 -> x1, other arithmetic: 109 us -> 1.38 us  [per_device(): small_all[:, 6:15].astype(F32).sum(axis=0).reshape(3, 3, width)]
    convert_element_type x36 -> x2, local copies, waits for them, and re-layouts: 86.5 us -> 2.65 us  [the longest x1 2.03 us: per_device(): grad_tokens = latent_out(dx).astype(F32)]
    convert_element_type x41 -> x3, other arithmetic: 62.5 us -> 1.04 us  [the longest x1 0.69 us: per_device(): ffn_taps = gather(k_ffn.reshape(9, local)).astype(F32)]
    psum x2 -> x0, blocking collectives: 50.4 us -> none  [the longest x1 38.2 us: per_device(): lax.psum(grad_k_attn.astype(jnp.bfloat16), 'wide').astype(jnp.float32)]
  transfers between devices with their start and end apart: 33 -> 11, of which waited for: 33 -> 5; matrix products, arithmetic and copies ran while one was open for 12% -> 11% of each run, Pallas kernels for 0% -> 12%
where the time goes in v1:
time: 619 us; the launch traced here: 618 us
  Pallas kernels  220 us (36%)
  waiting for transfers between devices  168 us (27%)
  blocking collectives  109 us (18%)
  local copies, waits for them, and re-layouts  56 us (9%)
  matrix products  17.8 us (3%)
  starting transfers between devices  15.4 us (2%)
  other arithmetic  15.2 us (2%)
  between operations  15.1 us (2%)
    reduce_scatter x2, waiting for transfers between devices, reduce(): lax.psum_scatter(parts, 'narrow', scatter_dimension=0, tiled=True)  120 us
    pallas_call x1, Pallas kernels, ffn(): pl.pallas_call(ffn_kernel, grid=(shards * per,), out_shape=(shape((rows,...  97.1 us
    all_gather x1, blocking collectives, per_device(): small_all = lax.all_gather(small, ('wide', 'narrow'))  56.9 us
    pallas_call x1, Pallas kernels, attn_forward(): pl.pallas_call(attn_forward_kernel, out_shape=(shape((rows, width), BF16)...  49.9 us
    pallas_call x1, Pallas kernels, attn_backward(): pl.pallas_call(attn_backward_kernel, out_shape=(shape((rows, 3 * width),...  34.7 us
    all_gather x1, blocking collectives, per_device(): silu_all = lax.all_gather(silu_low, 'wide', tiled=True)  31.8 us
    all_gather x1, waiting for transfers between devices, per_device(): wdown = gather(w_down)  24.2 us
    pallas_call x1, Pallas kernels, input_backward(): pl.pallas_call(input_backward_kernel, out_shape=(shape((rows, width), BF1...  23.1 us
  transfers between devices with their start and end apart: 11, of which 5 were waited for; matrix products, arithmetic and copies ran while one was open for 11% of the time, Pallas kernels for 12%

profile of v1, /device:TPU:0, one launch (start us, length us, event | category | flops | bytes accessed | tf_op | source)
XLA Modules:
  0.0 617.5 jit_solution(1283278705173556190)
XLA Ops:
  8.0 2.1 copy.61
  13.5 4.2 all-to-all-start.1
  17.7 3.6 reshape.156
  22.7 21.4 %all-to-all-done.1 = bf16[4,4,64,768]{3,2,1,0:T(8,128)(2,1)S(1)} async-done(((bf16[4,4,64,768]{3,2,1,0:T(8,128)(2,1)}), bf16[4,4,64,768]{3,2,1,0:T(8,128)(2,1)S(1)}, u32[]{:S(2)}, u32[]{:S(2)}) %all-to-all-start.1) | async-done | bytes 1572896 | tf_op jit(solution)/shard_map/all_to_all | solution.py:561
  44.1 3.6 all-to-all-start
  47.8 10.3 %copy.45 = bf16[768,4608]{0,1:T(8,128)(2,1)} copy(bf16[768,4608]{1,0:T(8,128)(2,1)} %param.15) | data formatting | bytes 14155776 | tf_op args[4]
  58.1 4.9 fusion.12
  65.0 20.7 %all_gather.34 = bf16[4,9,768]{2,1,0:T(8,128)(2,1)S(1)} all-gather(bf16[1,9,768]{2,1,0:T(8,128)(2,1)S(1)} %all_gather_reshape.3), channel_id=1, replica_groups=mesh['wide'=8,'narrow'=4] {'narrow'}, dimensions={0}, use_global_device_ids=true | all-gather | bytes 69120 | tf_op jit(solution)/shard_map/all_gather | solution.py:574
  88.9 49.9 %attn_forward.1 = (bf16[1024,768]{1,0:T(8,128)(2,1)}, bf16[1024,2304]{1,0:T(8,128)(2,1)}, bf16[24,256,512]{2,1,0:T(8,128)(2,1)}, bf16[1024,768]{1,0:T(8,128)(2,1...) custom-call(f32[1,1]{1,0:T(1,128)} %bitcast.1.live_ref, ...), custom_call_target="tpu_custom_call" | custom-call | tf_op jit(solution)/shard_map/attn_forward/pallas_call | solution.py:191
  138.8 24.2 %all-gather.14.cloned.1.call-done = bf16[3072,768]{1,0:T(8,128)(2,1)} async-done(((bf16[768,768]{1,0:T(8,128)(2,1)}), bf16[3072,768]{1,0:T(8,128)(2,1)}) %all-gather.14.cloned.1.call-update) | async-done | bytes 4718608 | tf_op jit(solution)/shard_map/all_gather | solution.py:573
  163.0 97.1 %feed_forward.1 = (f32[1024,768]{1,0:T(8,128)}, f32[1024,768]{1,0:T(8,128)}, bf16[4,768,768]{2,1,0:T(8,128)(2,1)}, bf16[4,768,768]{2,1,0:T(8,128)(2,1)}, f32[4,9,768]{2,1,0:T(8,128)}) custom-call(bf16[1024,768]{1,0:T(8,128)(2,1)} %get-tuple-element.35.h2_ref, bf16[768,1024]{1,0:T(8,128)(2,1)} %get-tuple-element.36.h2t_ref, ...), custom_call_target="tpu_custom_call" | custom-call | tf_op jit(solution)/shard_map/feed_forward/pallas_call | solution.py:310
  260.1 15.7 %residual_backward.1 = (bf16[1024,768]{1,0:T(8,128)(2,1)}, f32[1024,768]{1,0:T(8,128)}, bf16[1024,768]{1,0:T(8,128)(2,1)}, bf16[768,768]{1,0:T(8,128)(2,1)}, f32[4,768]{1,0:T(4,128)}) custom-call(f32[1,1]{1,0:T(1,128)} %bitcast.1.live_ref, f32[1024,768]{1,0:T(8,128)} %get-tuple-element.34.x1_ref, bf16[1024,768]{1,0:T(8,128)(2,1)} %bitcast.74, ...), custom_call_target="tpu_custom_call" | custom-call | tf_op jit(solution)/shard_map/residual_backward/pallas_call | solution.py:388
  275.8 34.7 %attn_backward.1 = (bf16[1024,2304]{1,0:T(8,128)(2,1)}, bf16[768,2304]{1,0:T(8,128)(2,1)}) custom-call(bf16[1024,768]{1,0:T(8,128)(2,1)} %get-tuple-element.44.u_ref, bf16[1024,2304]{1,0:T(8,128)(2,1)} %get-tuple-element.45.qkv_ref, bf16[24,256,512]{2,1,0:T(8,128)(2,1)} %get-tuple-element.46.probs_ref, bf16[1024,768]{1,0:T(8,128)(2,1)} %get-tuple-element.47.dctx_ref), custom_call_target="tpu_custom_call" | custom-call | tf_op jit(solution)/shard_map/attn_backward/pallas_call | solution.py:458
  310.4 5.1 reshape.171
  315.5 3.7 pad_maximum_fusion
  320.1 9.0 %fusion.1 = bf16[4,1552,768]{2,1,0:T(8,128)(2,1)} fusion(bf16[4,9,768]{2,1,0:T(8,128)(2,1)S(1)} %convert.27, bf16[4,768,768]{2,1,0:T(8,128)(2,1)} %get-tuple-element.56, bf16[4,768,768]{2,1,0:T(8,128)(2,1)} %get-tuple-element.55), kind=kLoop, calls=%fused_computation.2 | loop fusion | flops 38141952 | bytes 19027968 | tf_op jit(solution)/shard_map/concatenate | solution.py:597
  329.2 38.0 %reduce-scatter.3.cloned.1.call-done = bf16[768,768]{1,0:T(8,128)(2,1)} async-done(((bf16[3072,768]{1,0:T(8,128)(2,1)}), bf16[768,768]{1,0:T(8,128)(2,1)}) %reduce-scatter.3.cloned.1.call-update) | async-done | bytes 1179664 | tf_op jit(solution)/shard_map/reduce_scatter | solution.py:595
  367.2 82.3 %reduce-scatter.5.cloned.1.call-done = bf16[1552,768]{1,0:T(8,128)(2,1)} async-done(((bf16[6208,768]{1,0:T(8,128)(2,1)}), bf16[1552,768]{1,0:T(8,128)(2,1)}) %reduce-scatter.5.cloned.1.call-update) | async-done | bytes 2383888 | tf_op jit(solution)/shard_map/reduce_scatter | solution.py:595
  449.6 31.8 %all-gather.2 = bf16[8,4,768]{2,1,0:T(4,128)(2,1)S(1)} all-gather(bf16[1,4,768]{2,1,0:T(4,128)(2,1)S(1)} %fusion.23), channel_id=1, replica_groups=mesh['wide'=8,'narrow'=4] {'wide'}, dimensions={0}, use_global_device_ids=true | all-gather | bytes 55296 | tf_op jit(solution)/shard_map/all_gather | solution.py:614
  481.5 23.1 %input_backward.1 = (bf16[1024,768]{1,0:T(8,128)(2,1)}, f32[2,768]{1,0:T(2,128)}, f32[9,768]{1,0:T(8,128)}) custom-call(bf16[1024,768]{1,0:T(8,128)(2,1)} %bitcast.72, f32[1024,768]{1,0:T(8,128)} %get-tuple-element.43.dx1_ref, bf16[1024,2304]{1,0:T(8,128)(2,1)} %get-tuple-element.48.dqkv_ref, f32[6,768]{1,0:T(8,128)} %bitcast.95, ...), custom_call_target="tpu_custom_call" | custom-call | tf_op jit(solution)/shard_map/input_backward/pallas_call | solution.py:528
  504.6 3.8 copy.51
  508.4 3.7 all-to-all-start.3
  512.2 56.9 %all_gather.35 = bf16[32,16,768]{2,1,0:T(8,128)(2,1)S(1)} all-gather(bf16[1,16,768]{2,1,0:T(8,128)(2,1)S(1)} %maximum_maximum_fusion), channel_id=1, replica_groups=mesh['wide'=8,'narrow'=4] {'wide','narrow'}, dimensions={0}, use_global_device_ids=true | all-gather | bytes 811008 | tf_op jit(solution)/shard_map/all_gather | solution.py:613
  570.1 2.4 copy.47
  572.5 3.6 all-to-all-start.2
  578.1 5.6 fusion.9
  583.6 7.3 %fusion.18 = f32[768,4608]{1,0:T(8,128)} fusion(bf16[32,768]{1,0:T(8,128)(2,1)S(1)} %reshape.185, bf16[32,4608]{1,0:T(8,128)(2,1)S(1)} %bitcast.90), kind=kOutput, calls=%fused_computation.28 | convolution fusion | flops 226492416 | bytes 14499840 | tf_op jit(solution)/shard_map/dot_general | solution.py:31
  591.5 2.0 copy.54
  593.5 2.2 copy.56
  598.9 2.6 slice.30
  603.3 2.5 fusion.17
  605.9 2.6 reshape.173
  (74 shorter events, 21.9 us)
Async XLA Ops:
  7.2 4.3 copy-start.2
  7.2 81.7 %all-gather.10.cloned.1.call-start = ((), (), s32[]{:S(2)}) async-start(), calls=%async_computation.7 | async-start | bytes 1474560 | tf_op jit(solution)/shard_map/all_gather | solution.py:571
  7.9 81.0 %all-gather.8.cloned.1.call-start = ((), (), s32[]{:S(2)}) async-start(), calls=%async_computation.6 | async-start | bytes 4423680 | tf_op jit(solution)/shard_map/all_gather | solution.py:570
  10.1 128.7 %all-gather.12.cloned.1.call-start = ((), (), s32[]{:S(2)}) async-start(), calls=%async_computation.10 | async-start | bytes 5898240 | tf_op jit(solution)/shard_map/all_gather | solution.py:572
  10.9 152.1 %all-gather.14.cloned.1.call-start = ((), (), s32[]{:S(2)}) async-start(), calls=%async_computation.11 | async-start | bytes 5898240 | tf_op jit(solution)/shard_map/all_gather | solution.py:573
  13.5 30.6 %all-to-all-start.1 = ((bf16[4,4,64,768]{3,2,1,0:T(8,128)(2,1)}), bf16[4,4,64,768]{3,2,1,0:T(8,128)(2,1)S(1)}, u32[]{:S(2)}, u32[]{:S(2)}) async-start(bf16[4,4,64,768]{3,2,1,0:T(8,128)(2,1)} %bitcast.8), calls=%async_computation.1 | async-start | bytes 3145728 | tf_op jit(solution)/shard_map/all_to_all | solution.py:561
  44.1 43.5 %all-to-all-start = ((bf16[4,4,64,768]{3,2,1,0:T(8,128)(2,1)}), bf16[4,4,64,768]{3,2,1,0:T(8,128)(2,1)S(1)}, u32[]{:S(2)}, u32[]{:S(2)}) async-start(bf16[4,4,64,768]{3,2,1,0:T(8,128)(2,1)} %bitcast.3), calls=%async_computation | async-start | bytes 3145728 | tf_op jit(solution)/shard_map/all_to_all | solution.py:561
  47.7 319.4 %reduce-scatter.3.cloned.1.call-start = ((), (), s32[]{:S(2)}) async-start(), calls=%async_computation.8 | async-start | bytes 5898240 | tf_op jit(solution)/shard_map/reduce_scatter | solution.py:595
  47.8 10.3 %copy-start.5 = (bf16[4,768]{1,0:T(4,128)(2,1)S(1)}, bf16[4,768]{1,0:T(4,128)(2,1)}, u32[]{:S(2)}) copy-start(bf16[4,768]{1,0:T(4,128)(2,1)} %param.12) | copy-start | bytes 18436
  58.1 6.2 %copy-start.7 = (bf16[3,3,768]{2,1,0:T(4,128)(2,1)S(1)}, bf16[3,3,768]{2,1,0:T(4,128)(2,1)}, u32[]{:S(2)}) copy-start(bf16[3,3,768]{2,1,0:T(4,128)(2,1)} %param.16) | copy-start | bytes 41476
  58.1 6.9 %copy-start.8 = (bf16[3,3,768]{2,1,0:T(4,128)(2,1)S(1)}, bf16[3,3,768]{2,1,0:T(4,128)(2,1)}, u32[]{:S(2)}) copy-start(bf16[3,3,768]{2,1,0:T(4,128)(2,1)} %param.20) | copy-start | bytes 41476
  319.2 0.9 copy-start.4
  319.2 130.3 %reduce-scatter.5.cloned.1.call-start = ((), (), s32[]{:S(2)}) async-start(), calls=%async_computation.9 | async-start | bytes 11919360 | tf_op jit(solution)/shard_map/reduce_scatter | solution.py:595
  329.2 269.7 %all-reduce.4.cloned.1.call-start = ((), (), s32[]{:S(2)}) async-start(), calls=%async_computation.12 | async-start | bytes 7127040 | tf_op jit(solution)/shard_map/psum | solution.py:595
  504.6 7.5 %copy-start.10 = (f32[2,768]{1,0:T(2,128)S(1)}, f32[2,768]{1,0:T(2,128)}, u32[]{:S(2)}) copy-start(f32[2,768]{1,0:T(2,128)} %get-tuple-element.50) | copy-start | bytes 18436
  504.6 7.5 %copy-start.9 = (f32[4,768]{1,0:T(4,128)S(1)}, f32[4,768]{1,0:T(4,128)}, u32[]{:S(2)}) copy-start(f32[4,768]{1,0:T(4,128)} %get-tuple-element.51) | copy-start | bytes 36868
  504.6 7.6 %copy-start.6 = (f32[9,768]{1,0:T(8,128)S(1)}, f32[9,768]{1,0:T(8,128)}, u32[]{:S(2)}) copy-start(f32[9,768]{1,0:T(8,128)} %get-tuple-element.52) | copy-start | bytes 82948
  508.4 61.7 %copy-start.3 = (bf16[1024,768]{1,0:T(8,128)(2,1)S(1)}, bf16[1024,768]{1,0:T(8,128)(2,1)}, u32[]{:S(2)}) copy-start(bf16[1024,768]{1,0:T(8,128)(2,1)} %get-tuple-element.42) | copy-start | bytes 4718596
  508.4 64.1 %all-to-all-start.3 = ((bf16[1,4,256,768]{3,1,0,2:T(4,128)(2,1)}), bf16[1,4,256,768]{3,1,0,2:T(4,128)(2,1)S(1)}, u32[]{:S(2)}, u32[]{:S(2)}) async-start(bf16[1,4,256,768]{3,1,0,2:T(4,128)(2,1)} %copy.51), calls=%async_computation.3 | async-start | bytes 3145728 | tf_op jit(solution)/shard_map/all_to_all | solution.py:565
  569.1 0.9 copy-start.1
  572.5 23.6 %all-to-all-start.2 = ((bf16[1,4,256,768]{3,1,0,2:T(4,128)(2,1)}), bf16[1,4,256,768]{3,1,0,2:T(4,128)(2,1)S(1)}, u32[]{:S(2)}, u32[]{:S(2)}) async-start(bf16[1,4,256,768]{3,1,0,2:T(4,128)(2,1)} %copy.47), calls=%async_computation.2 | async-start | bytes 3145728 | tf_op jit(solution)/shard_map/all_to_all | solution.py:565
  598.9 4.5 copy-start
Sparse Core Ops, SparseCore 0:
  9.6 26.4 all-gather.9
  38.2 47.3 all-gather.7
  87.2 36.7 all-gather.11
  125.4 37.5 all-gather.13
  319.3 47.8 reduce-scatter.2
  370.4 79.0 reduce-scatter.4
  453.7 142.3 all-reduce.3

commit v2 on v1

--- a/solution.py
+++ b/solution.py
@@ -1,5 +1,3 @@
-from functools import partial
-
 import jax
 import jax.numpy as jnp
 from jax import lax
@@ -83,17 +81,163 @@
     return (grad - mean_grad - unit * mean_dot) * inv
 
 
-def attn_forward_kernel(
-    live_ref, x_ref, cot_ref, mod_ref, taps_ref, wqkv_ref, wout_ref,
-    u_ref, qkv_ref, probs_ref, ctx_ref, att_ref, x1_ref, h2_ref, h2t_ref, db_ref,
-    base, shifted,
+def narrow_peers(here):
+    return [here ^ 2, here ^ 3, here ^ 1]
+
+
+def remote(src, dst, sems, at, wide, narrow):
+    return pltpu.make_async_remote_copy(
+        src_ref=src,
+        dst_ref=dst,
+        send_sem=sems.at[0, at],
+        recv_sem=sems.at[1, at],
+        device_id=(wide, narrow),
+        device_id_type=pl.DeviceIdType.MESH,
+    )
+
+
+class Gather:
+    def __init__(self, src, dst, sems, local_sem, first, wide, here):
+        half_rows = src.shape[0] // 2
+        half = wide % 2
+        mine, other = ds(half * half_rows, half_rows), ds((1 - half) * half_rows, half_rows)
+        far, near = here ^ 2, here ^ 1
+        self.own = pltpu.make_async_copy(src, dst.at[here], local_sem)
+        self.near = remote(src, dst.at[here], sems, first, wide, near)
+        self.far = remote(src.at[mine], dst.at[here, mine], sems, first + 1, wide, far)
+        got, swapped = dst.at[far, mine], dst.at[far, other]
+        self.share = remote(got, got, sems, first + 2, wide, near)
+        self.swap = remote(got, got, sems, first + 3, wide ^ 1, here)
+        self.share_swapped = remote(swapped, swapped, sems, first + 4, wide, near)
+
+    def start_near(self):
+        self.own.start()
+        self.near.start()
+
+    def start_far(self):
+        self.far.start()
+
+    def forward(self):
+        self.far.wait_recv()
+        self.swap.start()
+        self.share.start()
+
+    def forward_swapped(self):
+        self.swap.wait_recv()
+        self.share_swapped.start()
+
+    def finish(self):
+        self.own.wait()
+        self.near.wait()
+        self.far.wait_send()
+        self.swap.wait_send()
+        self.share.wait()
+        self.share_swapped.wait()
+
+
+def group_permutation(rows):
+    out = lax.broadcasted_iota(jnp.int32, (rows, rows), 0)
+    source = lax.broadcasted_iota(jnp.int32, (rows, rows), 1)
+    per_group = rows // 4
+    group, rest = out // per_group, out % per_group
+    line = 2 * (rest // HALF) + group // 2
+    wanted = line * SIDE + 2 * (rest % HALF) + group % 2
+    return jnp.where(source == wanted, 1.0, 0.0).astype(BF16)
+
+
+class Exchange:
+    def __init__(self, sent, got, sems, local_sem, first, wide, here):
+        self.own = pltpu.make_async_copy(sent.at[here], got.at[:, here], local_sem)
+        self.copies = [
+            remote(sent.at[peer], got.at[:, here], sems, first + at, wide, peer)
+            for at, peer in enumerate(narrow_peers(here))
+        ]
+
+    def start(self):
+        for copy in self.copies:
+            copy.start()
+        self.own.start()
+
+    def wait(self):
+        self.own.wait()
+        for copy in self.copies:
+            copy.wait()
+
+
+def front_kernel(
+    live_ref, silu_ref, taps_ref, tokens_hbm, cot_hbm, ada_hbm, wqkv_src, wout_src, wup_src, wdown_src, ktaps_src,
+    x_ref, cot_ref, mod_ref, u_ref, qkv_ref, probs_ref, ctx_ref, att_ref, x1_ref, h2_ref, h2t_ref, db_ref,
+    wqkv_ref, wout_ref, wup_ref, wdown_ref, ktaps_ref,
+    base, shifted, shards, sent, sent_cot, got, ada, sems, local_sems, in_sems,
 ):
-    width = x_ref.shape[1]
-    rows_all = x_ref.shape[0]
+    width = u_ref.shape[1]
+    rows_all = u_ref.shape[0]
+    latents, shard_rows = shards.shape[:2]
+    wide, here = lax.axis_index("wide"), lax.axis_index("narrow")
+    load_tokens = pltpu.make_async_copy(tokens_hbm, shards, in_sems.at[0])
+    load_tokens.start()
+    load_ada = pltpu.make_async_copy(ada_hbm, ada, in_sems.at[1])
+    load_ada.start()
+
+    barrier = pltpu.get_barrier_semaphore()
+    partners = [(wide, peer) for peer in narrow_peers(here)] + [(wide ^ 1, here)]
+    for partner in partners:
+        pl.semaphore_signal(
+            barrier, inc=1, device_id=partner, device_id_type=pl.DeviceIdType.MESH
+        )
+    permutation = group_permutation(shard_rows)
+    load_tokens.wait()
+
+    def permute(to):
+        def one(at, carry):
+            moved = mm(permutation, shards[at], NN).astype(BF16)
+            for group in range(4):
+                to[at, group] = moved[group * (shard_rows // 4) : (group + 1) * (shard_rows // 4)]
+            return carry
+
+        lax.fori_loop(0, latents, one, 0)
+
+    permute(sent)
+    pl.semaphore_wait(barrier, len(partners))
+    exchange = Exchange(sent, got, sems, local_sems.at[0], 0, wide, here)
+    exchange_cot = Exchange(sent_cot, cot_ref, sems, local_sems.at[1], 3, wide, here)
+    gathers = [
+        Gather(src, dst, sems, local_sems.at[2 + at], 6 + 5 * at, wide, here)
+        for at, (src, dst) in enumerate(
+            (
+                (wqkv_src, wqkv_ref),
+                (wout_src, wout_ref),
+                (wup_src, wup_ref),
+                (wdown_src, wdown_ref),
+                (ktaps_src, ktaps_ref),
+            )
+        )
+    ]
+    g_qkv, g_out, g_up, g_down, g_taps = gathers
+    exchange.start()
+    load_cot = pltpu.make_async_copy(cot_hbm, shards, in_sems.at[0])
+    load_cot.start()
+    for one in gathers:
+        one.start_near()
+
+    load_ada.wait()
+    for part in range(6):
+        mod_ref[part : part + 1, :] = mm(
+            silu_ref[...], ada[:, part * width : (part + 1) * width], NN
+        )[0:1, :]
+    load_cot.wait()
+    permute(sent_cot)
     shift_one, scale_one, gate_one = mod_ref[0:1, :], mod_ref[1:2, :], mod_ref[2:3, :]
     shift_two, scale_two, gate_two = mod_ref[3:4, :], mod_ref[4:5, :], mod_ref[5:6, :]
     clear_edges(base)
     clear_edges(shifted)
+    exchange.wait()
+    g_qkv.start_far()
+    g_out.start_far()
+    for group in range(4):
+        for source in range(latents):
+            start = group * PHASE + source * ROWS
+            x_ref[start : start + ROWS, :] = got[group, source]
 
     def norm_step(step, carry):
         group, part = step // (PHASE // ROWS), step % (PHASE // ROWS)
@@ -122,12 +266,23 @@
         return lax.fori_loop(0, PHASE // ROWS, rows_step, carry)
 
     lax.fori_loop(0, width // LANES, conv_step, 0)
+    g_qkv.forward()
+    g_out.forward()
+    g_up.start_far()
+    g_taps.start_far()
+    g_qkv.forward_swapped()
+    g_out.forward_swapped()
+    g_qkv.finish()
+    shards_here = wqkv_ref.shape[0]
+    slab = wqkv_ref.shape[1]
 
     def project_step(step, carry):
         rows = ds(step * PHASE, PHASE)
         for part in range(3):
-            cols = slice(part * width, (part + 1) * width)
-            qkv_ref[rows, cols] = mm(u_ref[rows, :], wqkv_ref[:, cols], NT).astype(BF16)
+            for shard in range(shards_here):
+                weight = wqkv_ref[shard, :, part * width : (part + 1) * width]
+                cols = slice(part * width + shard * slab, part * width + (shard + 1) * slab)
+                qkv_ref[rows, cols] = mm(u_ref[rows, :], weight, NT).astype(BF16)
         return carry
 
     lax.fori_loop(0, 4, project_step, 0)
@@ -154,11 +309,25 @@
         ctx_ref[rows, ds(pair * LANES, LANES)] = jnp.where(first, found[0], found[1]).astype(BF16)
         return carry
 
-    lax.fori_loop(0, 4 * pairs, attend_step, 0)
+    lax.fori_loop(0, pairs, attend_step, 0)
+    g_up.forward()
+    g_taps.forward()
+    exchange_cot.start()
+    lax.fori_loop(pairs, 3 * pairs, attend_step, 0)
+    g_up.forward_swapped()
+    g_taps.forward_swapped()
+    exchange_cot.wait()
+    g_down.start_far()
+    lax.fori_loop(3 * pairs, 4 * pairs, attend_step, 0)
+    g_out.finish()
 
     def out_step(step, carry):
         rows = ds(step * PHASE, PHASE)
-        att_ref[rows, :] = mm(ctx_ref[rows, :], wout_ref[...], NN)
+        total = None
+        for shard in range(shards_here):
+            one = mm(ctx_ref[rows, shard * slab : (shard + 1) * slab], wout_ref[shard], NN)
+            total = one if total is None else total + one
+        att_ref[rows, :] = total
         return carry
 
     lax.fori_loop(0, 4, out_step, 0)
@@ -170,27 +339,38 @@
         x1_ref[rows, :] = after
         unit, _ = normed(after)
         h2_ref[rows, :] = (unit * (1.0 + scale_two) + shift_two).astype(BF16)
-        db_ref[rows, :] = (cot_ref[rows, :].astype(F32) * live * gate_two).astype(BF16)
+        group, source = step // (PHASE // ROWS), step % (PHASE // ROWS)
+        db_ref[rows, :] = (cot_ref[group, source].astype(F32) * live * gate_two).astype(BF16)
         return carry
 
     lax.fori_loop(0, rows_all // ROWS, second_step, 0)
+    g_down.forward()
     for part in range(4):
         h2t_ref[:, part * PHASE : (part + 1) * PHASE] = h2_ref[
             part * PHASE : (part + 1) * PHASE, :
         ].T
+    g_down.forward_swapped()
+    for one in (g_up, g_taps, g_down):
+        one.finish()
 
 
 def whole(memory=pltpu.VMEM):
     return pl.BlockSpec(memory_space=memory)
 
 
-def attn_forward(live, x, cot, mod, taps, wqkv, wout):
-    rows, width = x.shape
+def front(live, silu_row, taps, tokens, cot, w_ada, wqkv, wout, wup, wdown, ktaps):
+    latents, shard_rows, width = tokens.shape
+    rows = latents * shard_rows
     steps = 4 * (width // LANES)
     shape = jax.ShapeDtypeStruct
+    full = lambda shard: shape((latents,) + shard.shape, BF16)
+    moved = (latents, 4, shard_rows // 4, width)
     return pl.pallas_call(
-        attn_forward_kernel,
+        front_kernel,
         out_shape=(
+            shape((rows, width), BF16),
+            shape((4, latents, shard_rows // 4, width), BF16),
+            shape((6, width), F32),
             shape((rows, width), BF16),
             shape((rows, 3 * width), BF16),
             shape((steps, PHASE, 2 * PHASE), BF16),
@@ -200,13 +380,31 @@
             shape((rows, width), BF16),
             shape((width, rows), BF16),
             shape((rows, width), BF16),
+            full(wqkv),
+            full(wout),
+            full(wup),
+            full(wdown),
+            full(ktaps),
         ),
-        in_specs=[whole(pltpu.SMEM)] + [whole()] * 6,
-        out_specs=(whole(),) * 9,
-        scratch_shapes=[pltpu.VMEM((4, PAD, width), F32), pltpu.VMEM((4, PAD, width), F32)],
-        compiler_params=pltpu.CompilerParams(vmem_limit_bytes=56 * MIB),
+        in_specs=[whole(pltpu.SMEM)] + [whole()] * 2 + [whole(pl.ANY)] * 8,
+        out_specs=(whole(),) * 14 + (whole(pl.ANY),) * 3,
+        scratch_shapes=[
+            pltpu.VMEM((4, PAD, width), F32),
+            pltpu.VMEM((4, PAD, width), F32),
+            pltpu.VMEM((latents, shard_rows, width), BF16),
+            pltpu.VMEM(moved, BF16),
+            pltpu.VMEM(moved, BF16),
+            pltpu.VMEM((4, latents, shard_rows // 4, width), BF16),
+            pltpu.VMEM(w_ada.shape, BF16),
+            pltpu.SemaphoreType.DMA((2, 6 + 5 * 5)),
+            pltpu.SemaphoreType.DMA((7,)),
+            pltpu.SemaphoreType.DMA((2,)),
+        ],
+        compiler_params=pltpu.CompilerParams(
+            vmem_limit_bytes=60 * MIB, collective_id=0, has_side_effects=True
+        ),
         name="attn_forward",
-    )(live, x, cot, mod, taps, wqkv, wout)
+    )(live, silu_row, taps, tokens, cot, w_ada, wqkv, wout, wup, wdown, ktaps)
 
 
 def ffn_kernel(
@@ -555,34 +753,27 @@
     here = lax.axis_index("narrow")
     rows_all = shard_rows * lat_dev
     local = w_up.shape[1]
-    gather = partial(lax.all_gather, axis_name="narrow")
-
-    def latent_in(shard):
-        return lax.all_to_all(to_groups(shard), "narrow", 0, 2, tiled=True).reshape(rows_all, width)
 
     def latent_out(latent):
         parts = latent.reshape(1, 4, rows_all // 4, width)
         return from_groups(lax.all_to_all(parts, "narrow", 2, 0, tiled=True))
 
-    x = latent_in(tokens)
-    cot = latent_in(cotangent)
     qkv_t = w_qkv.transpose(2, 1, 0).reshape(w_qkv.shape[2], 3 * width)
-    wqkv = gather(qkv_t, tiled=True)
-    wout = gather(w_out, tiled=True)
-    wup = gather(w_up)
-    wdown = gather(w_down)
-    ffn_taps = gather(k_ffn.reshape(9, local)).astype(F32)
+    ktaps_own = jnp.pad(k_ffn.reshape(9, local), ((0, 23), (0, 0)))
     attn_taps = k_attn.reshape(9, width).astype(F32)
 
     cond_f = condition.astype(F32)
     silu_low = jax.nn.silu(cond_f).astype(BF16)
-    own_silu = lax.dynamic_slice_in_dim(silu_low, here, 1, 0)
-    mod = mm(own_silu, w_ada, NN).reshape(6, width)
+    own_silu = jnp.broadcast_to(lax.dynamic_slice_in_dim(silu_low, here, 1, 0), (16, width))
     live = (here < counts[0]).astype(F32).reshape(1, 1)
 
-    u, qkv, probs, ctx, att, x1, h2, h2t, db = attn_forward(
-        live, x, cot, mod, attn_taps, wqkv, wout
+    (x, cot, mod, u, qkv, probs, ctx, att, x1, h2, h2t, db, wqkv, wout, wup, wdown, ktaps) = front(
+        live, own_silu, attn_taps, tokens, cotangent, w_ada, qkv_t, w_out, w_up, w_down, ktaps_own
     )
+    cot = cot.reshape(rows_all, width)
+    wqkv = wqkv.reshape(width, 3 * width)
+    wout = wout.reshape(width, width)
+    ffn_taps = ktaps[:, :9].astype(F32)
     branch, dh2, dwup, dwdown, dffn_taps = ffn(h2, h2t, db, wup, wdown, ffn_taps)
     block_g, dx1, dctx, dwout, dmod_mid = mid(live, x1, cot, branch, dh2, att, ctx, mod, wout)
     dqkv, dwqkv = attn_backward(u, qkv, probs, dctx)

time: 619 us -> 593 us (0.958)
  Pallas kernels: 220 us -> 292 us
  waiting for transfers between devices: 168 us -> 122 us
  blocking collectives: 109 us -> 87.4 us
  local copies, waits for them, and re-layouts: 56 us -> 38.3 us
  starting transfers between devices: 15.4 us -> 7.6 us
    pallas_call x1, Pallas kernels: 49.9 us -> 121 us  [front(): pl.pallas_call(front_kernel, out_shape=(shape((rows, width), BF16), shape...]
    all_gather x4 -> x0, waiting for transfers between devices: 24.2 us -> none  [the longest x1 24.2 us: per_device(): wdown = gather(w_down)]
    all_to_all x2 -> x0, waiting for transfers between devices: 21.4 us -> none  [latent_in(): lax.all_to_all(to_groups(shard), 'narrow', 0, 2, tiled=True)]
    all_gather x1 -> x0, blocking collectives: 20.7 us -> none  [per_device(): ffn_taps = gather(k_ffn.reshape(9, local)).astype(F32)]
    unnamed x28 -> x21, local copies, waits for them, and re-layouts: 17.2 us -> 6.92 us
    all_to_all x2 -> x0, starting transfers between devices: 7.83 us -> none  [latent_in(): lax.all_to_all(to_groups(shard), 'narrow', 0, 2, tiled=True)]
    reshape x4 -> x1, local copies, waits for them, and re-layouts: 7.02 us -> 0.75 us  [per_device(): ktaps_own = jnp.pad(k_ffn.reshape(9, local), ((0, 23), (0, 0)))]
    dot_general x3 -> x2, matrix products: 17.8 us -> 12.9 us  [mm(): return lax.dot_general(left, right, dims, preferred_element_type=F32)]
  transfers between devices with their start and end apart: 11 -> 5, of which waited for: 5 -> 3; matrix products, arithmetic and copies ran while one was open for 11% -> 6% of each run, Pallas kernels for 12% -> 4%
where the time goes in v2:
time: 593 us; the launch traced here: 592 us
  Pallas kernels  292 us (49%)
  waiting for transfers between devices  122 us (21%)
  blocking collectives  87.4 us (15%)
  local copies, waits for them, and re-layouts  38.3 us (6%)
  other arithmetic  17 us (3%)
  between operations  14.6 us (2%)
  matrix products  12.9 us (2%)
  starting transfers between devices  7.6 us (1%)
    reduce_scatter x2, waiting for transfers between devices, reduce(): lax.psum_scatter(parts, 'narrow', scatter_dimension=0, tiled=True)  122 us
    pallas_call x1, Pallas kernels, front(): pl.pallas_call(front_kernel, out_shape=(shape((rows, width), BF16), shape...  121 us
    pallas_call x1, Pallas kernels, ffn(): pl.pallas_call(ffn_kernel, grid=(shards * per,), out_shape=(shape((rows,...  97.1 us
    all_gather x1, blocking collectives, per_device(): small_all = lax.all_gather(small, ('wide', 'narrow'))  56.6 us
    pallas_call x1, Pallas kernels, attn_backward(): pl.pallas_call(attn_backward_kernel, out_shape=(shape((rows, 3 * width),...  34.9 us
    all_gather x1, blocking collectives, per_device(): silu_all = lax.all_gather(silu_low, 'wide', tiled=True)  30.8 us
    pallas_call x1, Pallas kernels, input_backward(): pl.pallas_call(input_backward_kernel, out_shape=(shape((rows, width), BF1...  23 us
    pallas_call x1, Pallas kernels, mid(): pl.pallas_call(mid_kernel, out_shape=(shape((rows, width), BF16), shape((...  15.8 us
  transfers between devices with their start and end apart: 5, of which 3 were waited for; matrix products, arithmetic and copies ran while one was open for 6% of the time, Pallas kernels for 4%

profile of v2, /device:TPU:0, one launch (start us, length us, event | category | flops | bytes accessed | tf_op | source)
XLA Modules:
  0.0 591.6 jit_solution(5873355158775365794)
XLA Ops:
  8.6 1.4 reshape.160.taps_ref
  10.0 2.1 copy.47
  14.1 120.7 %attn_forward.1 = (bf16[1024,768]{1,0:T(8,128)(2,1)}, bf16[4,4,64,768]{3,2,1,0:T(8,128)(2,1)}, f32[6,768]{1,0:T(8,128)}, bf16[1024,768]{1,0:T(8,128)(2,1)}, bf16...) custom-call(f32[1,1]{1,0:T(1,128)} %bitcast.1.live_ref, ...), custom_call_target="tpu_custom_call" | custom-call | tf_op jit(solution)/shard_map/attn_forward/pallas_call | solution.py:368
  134.9 1.6 slice_convert_fusion.taps_ref
  136.4 97.1 %feed_forward.1 = (f32[1024,768]{1,0:T(8,128)}, f32[1024,768]{1,0:T(8,128)}, bf16[4,768,768]{2,1,0:T(8,128)(2,1)}, bf16[4,768,768]{2,1,0:T(8,128)(2,1)}, f32[4,9,768]{2,1,0:T(8,128)}) custom-call(bf16[1024,768]{1,0:T(8,128)(2,1)} %get-tuple-element.44.h2_ref, bf16[768,1024]{1,0:T(8,128)(2,1)} %get-tuple-element.45.h2t_ref, ...), custom_call_target="tpu_custom_call" | custom-call | tf_op jit(solution)/shard_map/feed_forward/pallas_call | solution.py:508
  233.5 15.8 %residual_backward.1 = (bf16[1024,768]{1,0:T(8,128)(2,1)}, f32[1024,768]{1,0:T(8,128)}, bf16[1024,768]{1,0:T(8,128)(2,1)}, bf16[768,768]{1,0:T(8,128)(2,1)}, f32[4,768]{1,0:T(4,128)}) custom-call(f32[1,1]{1,0:T(1,128)} %bitcast.1.live_ref, f32[1024,768]{1,0:T(8,128)} %get-tuple-element.42.x1_ref, bf16[1024,768]{1,0:T(8,128)(2,1)} %bitcast.58, ...), custom_call_target="tpu_custom_call" | custom-call | tf_op jit(solution)/shard_map/residual_backward/pallas_call | solution.py:586
  249.3 34.9 %attn_backward.1 = (bf16[1024,2304]{1,0:T(8,128)(2,1)}, bf16[768,2304]{1,0:T(8,128)(2,1)}) custom-call(bf16[1024,768]{1,0:T(8,128)(2,1)} %get-tuple-element.59.u_ref, bf16[1024,2304]{1,0:T(8,128)(2,1)} %get-tuple-element.60.qkv_ref, bf16[24,256,512]{2,1,0:T(8,128)(2,1)} %get-tuple-element.61.probs_ref, bf16[1024,768]{1,0:T(8,128)(2,1)} %get-tuple-element.62.dctx_ref), custom_call_target="tpu_custom_call" | custom-call | tf_op jit(solution)/shard_map/attn_backward/pallas_call | solution.py:656
  284.2 5.1 reshape.153
  289.3 3.7 pad_maximum_fusion
  293.9 9.2 %fusion.1 = bf16[4,1552,768]{2,1,0:T(8,128)(2,1)} fusion(bf16[4,9,768]{2,1,0:T(8,128)(2,1)S(1)} %convert.27, bf16[4,768,768]{2,1,0:T(8,128)(2,1)} %get-tuple-element.72, bf16[4,768,768]{2,1,0:T(8,128)(2,1)} %get-tuple-element.71), kind=kLoop, calls=%fused_computation.2 | loop fusion | flops 38141952 | bytes 19027968 | tf_op jit(solution)/shard_map/concatenate | solution.py:788
  303.2 39.6 %reduce-scatter.3.cloned.1.call-done = bf16[768,768]{1,0:T(8,128)(2,1)} async-done(((bf16[3072,768]{1,0:T(8,128)(2,1)}), bf16[768,768]{1,0:T(8,128)(2,1)}) %reduce-scatter.3.cloned.1.call-update) | async-done | bytes 1179664 | tf_op jit(solution)/shard_map/reduce_scatter | solution.py:786
  342.8 82.4 %reduce-scatter.5.cloned.1.call-done = bf16[1552,768]{1,0:T(8,128)(2,1)} async-done(((bf16[6208,768]{1,0:T(8,128)(2,1)}), bf16[1552,768]{1,0:T(8,128)(2,1)}) %reduce-scatter.5.cloned.1.call-update) | async-done | bytes 2383888 | tf_op jit(solution)/shard_map/reduce_scatter | solution.py:786
  425.3 23.0 %input_backward.1 = (bf16[1024,768]{1,0:T(8,128)(2,1)}, f32[2,768]{1,0:T(2,128)}, f32[9,768]{1,0:T(8,128)}) custom-call(bf16[1024,768]{1,0:T(8,128)(2,1)} %get-tuple-element.57.x_ref, f32[1024,768]{1,0:T(8,128)} %get-tuple-element.58.dx1_ref, bf16[1024,2304]{1,0:T(8,128)(2,1)} %get-tuple-element.63.dqkv_ref, f32[6,768]{1,0:T(8,128)} %get-tuple-element.54.mod_ref, ...), custom_call_target="tpu_custom_call" | custom-call | tf_op jit(solution)/shard_map/input_backward/pallas_call | solution.py:726
  448.3 3.8 copy.38
  452.1 3.7 all-to-all-start.1
  456.1 56.6 %all_gather.7 = bf16[32,16,768]{2,1,0:T(8,128)(2,1)S(1)} all-gather(bf16[1,16,768]{2,1,0:T(8,128)(2,1)S(1)} %maximum_maximum_fusion), channel_id=1, replica_groups=mesh['wide'=8,'narrow'=4] {'wide','narrow'}, dimensions={0}, use_global_device_ids=true | all-gather | bytes 811008 | tf_op jit(solution)/shard_map/all_gather | solution.py:804
  512.7 0.9 copy-done.1
  513.7 30.8 %all-gather = bf16[8,4,768]{2,1,0:T(4,128)(2,1)S(1)} all-gather(bf16[1,4,768]{2,1,0:T(4,128)(2,1)S(1)} %fusion.18), channel_id=1, replica_groups=mesh['wide'=8,'narrow'=4] {'wide'}, dimensions={0}, use_global_device_ids=true | all-gather | bytes 55296 | tf_op jit(solution)/shard_map/all_gather | solution.py:805
  544.5 2.4 copy.34
  546.9 3.8 all-to-all-start
  550.7 1.4 convert_reduce_fusion
  552.7 5.6 fusion.9
  558.3 7.3 %fusion.14 = f32[768,4608]{1,0:T(8,128)} fusion(bf16[32,768]{1,0:T(8,128)(2,1)S(1)} %reshape.165, bf16[32,4608]{1,0:T(8,128)(2,1)S(1)} %bitcast.60), kind=kOutput, calls=%fused_computation.25 | convolution fusion | flops 226492416 | bytes 14499840 | tf_op jit(solution)/shard_map/dot_general | solution.py:29
  566.1 2.0 copy.41
  568.2 2.2 copy.43
  570.7 1.2 copy.37
  571.9 1.3 copy.42
  573.3 2.6 slice.34
  575.9 1.8 slice.35
  577.7 2.5 fusion.13
  580.3 2.6 reshape.155
  582.9 1.5 copy.44
  (45 shorter events, 6.2 us)
Async XLA Ops:
  7.2 335.7 %reduce-scatter.3.cloned.1.call-start = ((), (), s32[]{:S(2)}) async-start(), calls=%async_computation.4 | async-start | bytes 5898240 | tf_op jit(solution)/shard_map/reduce_scatter | solution.py:786
  293.0 0.9 copy-start.3
  293.0 132.3 %reduce-scatter.5.cloned.1.call-start = ((), (), s32[]{:S(2)}) async-start(), calls=%async_computation.5 | async-start | bytes 11919360 | tf_op jit(solution)/shard_map/reduce_scatter | solution.py:786
  303.2 270.1 %all-reduce.5.cloned.1.call-start = ((), (), s32[]{:S(2)}) async-start(), calls=%async_computation.6 | async-start | bytes 7127040 | tf_op jit(solution)/shard_map/psum | solution.py:786
  448.3 7.5 %copy-start.6 = (f32[4,768]{1,0:T(4,128)S(1)}, f32[4,768]{1,0:T(4,128)}, u32[]{:S(2)}) copy-start(f32[4,768]{1,0:T(4,128)} %get-tuple-element.67) | copy-start | bytes 36868
  448.3 7.6 %copy-start.7 = (f32[2,768]{1,0:T(2,128)S(1)}, f32[2,768]{1,0:T(2,128)}, u32[]{:S(2)}) copy-start(f32[2,768]{1,0:T(2,128)} %get-tuple-element.66) | copy-start | bytes 18436
  448.3 7.7 %copy-start.5 = (f32[9,768]{1,0:T(8,128)S(1)}, f32[9,768]{1,0:T(8,128)}, u32[]{:S(2)}) copy-start(f32[9,768]{1,0:T(8,128)} %get-tuple-element.68) | copy-start | bytes 82948
  452.1 61.5 %copy-start.4 = (bf16[4,768]{1,0:T(4,128)(2,1)S(1)}, bf16[4,768]{1,0:T(4,128)(2,1)}, u32[]{:S(2)}) copy-start(bf16[4,768]{1,0:T(4,128)(2,1)} %param.12) | copy-start | bytes 18436
  452.1 92.4 %copy-start.2 = (bf16[1024,768]{1,0:T(8,128)(2,1)S(1)}, bf16[1024,768]{1,0:T(8,128)(2,1)}, u32[]{:S(2)}) copy-start(bf16[1024,768]{1,0:T(8,128)(2,1)} %get-tuple-element.56) | copy-start | bytes 4718596
  452.1 94.7 %all-to-all-start.1 = ((bf16[1,4,256,768]{3,1,0,2:T(4,128)(2,1)}), bf16[1,4,256,768]{3,1,0,2:T(4,128)(2,1)S(1)}, u32[]{:S(2)}, u32[]{:S(2)}) async-start(bf16[1,4,256,768]{3,1,0,2:T(4,128)(2,1)} %copy.38), calls=%async_computation.1 | async-start | bytes 3145728 | tf_op jit(solution)/shard_map/all_to_all | solution.py:759
  512.7 0.9 copy-start.1
  546.9 23.6 %all-to-all-start = ((bf16[1,4,256,768]{3,1,0,2:T(4,128)(2,1)}), bf16[1,4,256,768]{3,1,0,2:T(4,128)(2,1)S(1)}, u32[]{:S(2)}, u32[]{:S(2)}) async-start(bf16[1,4,256,768]{3,1,0,2:T(4,128)(2,1)} %copy.34), calls=%async_computation | async-start | bytes 3145728 | tf_op jit(solution)/shard_map/all_to_all | solution.py:759
  573.3 4.5 copy-start
Sparse Core Ops, SparseCore 0:
  293.1 49.6 reduce-scatter.2
  346.2 79.0 reduce-scatter.4
  429.5 142.5 all-reduce.4

commit v3 on v2

--- a/solution.py
+++ b/solution.py
@@ -1,3 +1,5 @@
+from functools import partial
+
 import jax
 import jax.numpy as jnp
 from jax import lax
@@ -102,13 +104,12 @@
         half = wide % 2
         mine, other = ds(half * half_rows, half_rows), ds((1 - half) * half_rows, half_rows)
         far, near = here ^ 2, here ^ 1
-        self.own = pltpu.make_async_copy(src, dst.at[here], local_sem)
-        self.near = remote(src, dst.at[here], sems, first, wide, near)
-        self.far = remote(src.at[mine], dst.at[here, mine], sems, first + 1, wide, far)
-        got, swapped = dst.at[far, mine], dst.at[far, other]
-        self.share = remote(got, got, sems, first + 2, wide, near)
-        self.swap = remote(got, got, sems, first + 3, wide ^ 1, here)
-        self.share_swapped = remote(swapped, swapped, sems, first + 4, wide, near)
+        self.own = pltpu.make_async_copy(src, dst.at[0], local_sem)
+        self.near = remote(src, dst.at[1], sems, first, wide, near)
+        self.far = remote(src.at[mine], dst.at[2, mine], sems, first + 1, wide, far)
+        self.share = remote(dst.at[2, mine], dst.at[3, mine], sems, first + 2, wide, near)
+        self.swap = remote(dst.at[2, mine], dst.at[2, mine], sems, first + 3, wide ^ 1, here)
+        self.share_swapped = remote(dst.at[2, other], dst.at[3, other], sems, first + 4, wide, near)
 
     def start_near(self):
         self.own.start()
@@ -162,6 +163,133 @@
         self.own.wait()
         for copy in self.copies:
             copy.wait()
+
+
+class Return:
+    def __init__(self, sent, got, sems, local_sem, first, wide, here):
+        self.own = pltpu.make_async_copy(sent.at[:, here], got.at[here], local_sem)
+        self.copies = [
+            remote(sent.at[:, peer], got.at[here], sems, first + at, wide, peer)
+            for at, peer in enumerate(narrow_peers(here))
+        ]
+
+    start = Exchange.start
+    wait = Exchange.wait
+
+
+HALVINGS = 3
+
+
+class WideSum:
+    def __init__(self, source, work, full, got, sems, first, wide, here, n_wide, done=0):
+        self.source, self.work, self.full, self.got = source, work, full, got
+        self.rows = work.shape[0]
+        self.levels = min(HALVINGS, n_wide.bit_length() - 1)
+        self.extra = n_wide.bit_length() - 1 - self.levels
+        self.done = done
+        self.wide, self.here, self.sems, self.first = wide, here, sems, first
+        self.offsets = [0]
+        for level in range(self.levels):
+            bit = (wide // 2**level) % 2
+            self.offsets.append(self.offsets[-1] + bit * (self.rows >> (level + 1)))
+        self.waiting = []
+
+    def size(self, level):
+        return self.rows >> level
+
+    def at(self, ref, offset, size):
+        return ref.at[ds(offset, size, 16)]
+
+    def half_copy(self, level):
+        size, base = self.size(level + 1), self.offsets[level]
+        send = base + size - (self.offsets[level + 1] - base)
+        source = self.source if level == self.done else self.work
+        landing = self.rows - self.size(level)
+        return remote(
+            self.at(source, send, size), self.got.at[landing : landing + size],
+            self.sems, self.first + level, self.wide ^ (1 << level), self.here,
+        )
+
+    def start_half(self, level):
+        self.half_copy(level).start()
+
+    def finish_half(self, level):
+        self.half_copy(level).wait_recv()
+        size, landing = self.size(level + 1), self.rows - self.size(level)
+        rows = ds(self.offsets[level + 1], size, 16)
+        source = self.source if level == self.done else self.work
+        self.work[rows, :] = (
+            source[rows, :].astype(F32) + self.got[landing : landing + size, :].astype(F32)
+        ).astype(BF16)
+
+    def extras(self):
+        size = self.size(self.levels)
+        rows = ds(self.offsets[self.levels], size, 16)
+        source = self.source if self.done == self.levels else self.work
+        self.full[rows, :] = source[rows, :]
+        for at in range(self.extra):
+            landing = self.rows - size + at * size
+            copy = remote(
+                self.full.at[rows], self.got.at[landing : landing + size],
+                self.sems, self.first + 2 * self.levels + at,
+                self.wide ^ (1 << (self.levels + at)), self.here,
+            )
+            copy.start()
+            copy.wait()
+            self.full[rows, :] = (
+                self.full[rows, :].astype(F32) + self.got[landing : landing + size, :].astype(F32)
+            ).astype(BF16)
+
+    def spread_copy(self, level):
+        part = self.at(self.full, self.offsets[level + 1], self.size(level + 1))
+        return remote(
+            part, part, self.sems, self.first + self.levels + level, self.wide ^ (1 << level), self.here
+        )
+
+    def actions(self):
+        acts = []
+        for level in range(self.done, self.levels):
+            acts.append([partial(self.start_half, level)])
+            if level > self.done:
+                acts[-1].insert(0, partial(self.finish_half, level - 1))
+        tail = [self.extras]
+        if self.done < self.levels:
+            tail.insert(0, partial(self.finish_half, self.levels - 1))
+        for level in reversed(range(self.levels)):
+            acts.append(tail + [lambda level=level: self.spread_copy(level).start()])
+            tail = [lambda level=level: self.spread_copy(level).wait_recv()]
+        acts.append(tail)
+        return acts
+
+    def wait_sends(self):
+        for level in range(self.done, self.levels):
+            self.half_copy(level).wait_send()
+        for level in range(self.levels):
+            self.spread_copy(level).wait_send()
+
+
+def greet(partners):
+    barrier = pltpu.get_barrier_semaphore()
+    for partner in partners:
+        pl.semaphore_signal(
+            barrier, inc=1, device_id=partner, device_id_type=pl.DeviceIdType.MESH
+        )
+    pl.semaphore_wait(barrier, len(partners))
+
+
+def wide_partners(wide, here, n_wide):
+    return [(wide ^ (1 << level), here) for level in range(n_wide.bit_length() - 1)]
+
+
+def sum_semaphores(n_wide):
+    levels = n_wide.bit_length() - 1
+    return levels + min(levels, HALVINGS)
+
+
+def sum_landing(rows, n_wide):
+    levels = n_wide.bit_length() - 1
+    last = rows >> min(levels, HALVINGS)
+    return rows - last + max(levels - HALVINGS, 0) * last
 
 
 def front_kernel(
@@ -327,7 +455,8 @@
         for shard in range(shards_here):
             one = mm(ctx_ref[rows, shard * slab : (shard + 1) * slab], wout_ref[shard], NN)
             total = one if total is None else total + one
-        att_ref[rows, :] = total
+        att_ref[rows, :] = total.astype(BF16)
+        x1_ref[rows, :] = x_ref[rows, :].astype(F32) + gate_one * total
         return carry
 
     lax.fori_loop(0, 4, out_step, 0)
@@ -335,9 +464,7 @@
 
     def second_step(step, carry):
         rows = ds(step * ROWS, ROWS)
-        after = x_ref[rows, :].astype(F32) + gate_one * att_ref[rows, :]
-        x1_ref[rows, :] = after
-        unit, _ = normed(after)
+        unit, _ = normed(x1_ref[rows, :])
         h2_ref[rows, :] = (unit * (1.0 + scale_two) + shift_two).astype(BF16)
         group, source = step // (PHASE // ROWS), step % (PHASE // ROWS)
         db_ref[rows, :] = (cot_ref[group, source].astype(F32) * live * gate_two).astype(BF16)
@@ -375,7 +502,7 @@
             shape((rows, 3 * width), BF16),
             shape((steps, PHASE, 2 * PHASE), BF16),
             shape((rows, width), BF16),
-            shape((rows, width), F32),
+            shape((rows, width), BF16),
             shape((rows, width), F32),
             shape((rows, width), BF16),
             shape((width, rows), BF16),
@@ -408,18 +535,36 @@
 
 
 def ffn_kernel(
-    h2_ref, h2t_ref, db_ref, wup_ref, wdown_ref, taps_ref,
-    branch_ref, dh2_ref, dwup_ref, dwdown_ref, dtaps_ref,
-    hid, hid_moved, grad, grad_moved, slope, act, dhid,
+    live_ref, h2_ref, h2t_ref, db_ref, x1_ref, cot_ref, att_ref, mod_ref, wup_ref, wdown_ref, taps_ref,
+    block_ref, dx1_ref, datt_ref, dmod_ref, sums_ref,
+    hid, hid_moved, grad, grad_moved, slope, act, dhid, branch, dh2, dtaps, work, chip_sum, got_near, got_far,
+    sems,
 ):
-    rows_all = h2_ref.shape[0]
-
-    @pl.when(pl.program_id(0) == 0)
+    rows_all, width = h2_ref.shape
+    wide, here = lax.axis_index("wide"), lax.axis_index("narrow")
+    step, steps = pl.program_id(0), pl.num_programs(0)
+    part, turn, odd = (step // 2) % (steps // 4), step // 2, step % 2
+    early = step < steps // 2
+
+    def to_near(at):
+        return remote(work.at[at % 2], got_near.at[at], sems, at, wide, here ^ 1)
+
+    def to_far(at):
+        return remote(chip_sum.at[at], got_far.at[at], sems, steps // 2 + at, wide, here ^ 2)
+
+    @pl.when(step == 0)
     def _():
+        barrier = pltpu.get_barrier_semaphore()
+        for partner in (here ^ 1, here ^ 2):
+            pl.semaphore_signal(
+                barrier, inc=1, device_id=(wide, partner), device_id_type=pl.DeviceIdType.MESH
+            )
         for ref in (hid, hid_moved, grad, grad_moved):
             clear_edges(ref)
-        branch_ref[...] = jnp.zeros_like(branch_ref)
-        dh2_ref[...] = jnp.zeros_like(dh2_ref)
+        branch[...] = jnp.zeros_like(branch)
+        dh2[...] = jnp.zeros_like(dh2)
+        dtaps[...] = jnp.zeros_like(dtaps)
+        pl.semaphore_wait(barrier, 2)
 
     def up_step(group, carry):
         rows = ds(group * PHASE, PHASE)
@@ -433,18 +578,18 @@
         shift_cols(hid, hid_moved, lanes)
         taps = [taps_ref[0, t : t + 1, lanes] for t in range(9)]
 
-        def act_step(step, carry):
+        def act_step(at, carry):
             for group in range(4):
                 total = jnp.zeros((ROWS, LANES), F32)
                 for tap in range(9):
                     total += taps[tap] * tap_value(
-                        hid, hid_moved, group, tap // 3, tap % 3, step * ROWS, lanes
+                        hid, hid_moved, group, tap // 3, tap % 3, at * ROWS, lanes
                     )
                 square = total * total
-                turn = jnp.tanh(total * (square * (GELU_C * GELU_A) + GELU_C))
-                half = 0.5 * turn + 0.5
+                turned = jnp.tanh(total * (square * (GELU_C * GELU_A) + GELU_C))
+                half = 0.5 * turned + 0.5
                 bend = total * (half - half * half)
-                rows = ds(group * PHASE + step * ROWS, ROWS)
+                rows = ds(group * PHASE + at * ROWS, ROWS)
                 act[rows, lanes] = (total * half).astype(BF16)
                 slope[rows, lanes] = half + bend * (
                     square * (6.0 * GELU_C * GELU_A) + 2.0 * GELU_C
@@ -465,17 +610,78 @@
         lanes = slice(block * LANES, (block + 1) * LANES)
         shift_cols(grad, grad_moved, lanes)
         conv_back(grad, grad_moved, hid, lanes, [taps_ref[0, t : t + 1, lanes] for t in range(9)],
-                  dtaps_ref.at[0], dhid)
+                  dtaps, dhid)
 
     def final_step(group, carry):
         rows = ds(group * PHASE, PHASE)
-        branch_ref[rows, :] += mm(act[rows, :], wdown_ref[0], NN)
-        dh2_ref[rows, :] += mm(dhid[rows, :], wup_ref[0], NT)
+        branch[rows, :] += mm(act[rows, :], wdown_ref[0], NN)
+        dh2[rows, :] += mm(dhid[rows, :], wup_ref[0], NT)
         return carry
 
     lax.fori_loop(0, 4, final_step, 0)
-    dwup_ref[0] = mm(h2t_ref[...], dhid[...], NN).astype(BF16)
-    dwdown_ref[0] = mm(act[...], db_ref[...], TN).astype(BF16)
+
+    @pl.when(jnp.logical_and(odd == 0, turn >= 2))
+    def _():
+        to_near(turn - 2).wait_send()
+
+    slot = work.at[jnp.where(odd == 0, turn % 2, 2)]
+    slot[:width, :] = mm(h2t_ref[...], dhid[...], NN).astype(BF16)
+    down = mm(act[...], db_ref[...], TN).astype(BF16)
+    for block in range(width // CHUNK):
+        rows = slice(width + block * CHUNK, width + (block + 1) * CHUNK)
+        slot[rows, :] = down[:, block * CHUNK : (block + 1) * CHUNK]
+    slot[2 * width :, :] = dtaps[...].astype(BF16)
+
+    @pl.when(odd == 0)
+    def _():
+        to_near(turn).start()
+
+    @pl.when(odd == 1)
+    def _():
+        to_near(turn).wait_recv()
+
+    @pl.when(jnp.logical_and(odd == 1, early))
+    def _():
+        chip_sum[part] = (work[2].astype(F32) + got_near[turn].astype(F32)).astype(BF16)
+        to_far(part).start()
+
+    @pl.when(jnp.logical_and(odd == 1, jnp.logical_not(early)))
+    def _():
+        to_far(part).wait_recv()
+        sums_ref[part] = (
+            work[2].astype(F32) + got_near[turn].astype(F32) + got_far[part].astype(F32)
+        ).astype(BF16)
+
+    @pl.when(step == steps - 1)
+    def _():
+        gate_one, scale_two, gate_two = mod_ref[2:3, :], mod_ref[4:5, :], mod_ref[5:6, :]
+        live = live_ref[0, 0]
+
+        def fold(value):
+            return value.reshape(ROWS // 8, 8, width).sum(axis=0)
+
+        def rows_step(at, sums):
+            rows = ds(at * ROWS, ROWS)
+            after = x1_ref[rows, :]
+            dout = cot_ref[rows, :].astype(F32) * live
+            branch_rows = branch[rows, :]
+            block_ref[rows, :] = ((after + gate_two * branch_rows) * live).astype(BF16)
+            unit, inv = normed(after)
+            dh2_rows = dh2[rows, :]
+            dx1 = dout + norm_back(unit, inv, dh2_rows * (1.0 + scale_two))
+            dx1_ref[rows, :] = dx1
+            datt_ref[rows, :] = (dx1 * gate_one).astype(BF16)
+            found = (dx1 * att_ref[rows, :].astype(F32), dh2_rows, dh2_rows * unit, dout * branch_rows)
+            return tuple(total + fold(one) for total, one in zip(sums, found))
+
+        start = tuple(jnp.zeros((8, width), F32) for _ in range(4))
+        sums = lax.fori_loop(0, rows_all // ROWS, rows_step, start)
+        for at in range(4):
+            dmod_ref[at : at + 1, :] = jnp.sum(sums[at], axis=0, keepdims=True)
+        for at in (steps // 2 - 2, steps // 2 - 1):
+            to_near(at).wait_send()
+        for at in range(steps // 4):
+            to_far(at).wait_send()
 
 
 def conv_back(grad, grad_moved, source, lanes, taps, dtaps_ref, out_ref):
@@ -499,129 +705,153 @@
         dtaps_ref[tap : tap + 1, lanes] = jnp.sum(sums[tap], axis=0, keepdims=True)
 
 
-def ffn(h2, h2t, db, wup, wdown, taps):
+def ffn(live, h2, h2t, db, x1, cot, att, mod, wup, wdown, taps):
     rows, width = h2.shape
     shards, _, local = wup.shape
     per = local // CHUNK
+    parcel = (2 * width + 16, CHUNK)
     shape = jax.ShapeDtypeStruct
-    keep = lambda *block: pl.BlockSpec(block, lambda c: (0,) * len(block))
+    keep = lambda *block: pl.BlockSpec(
+        block, lambda c: (0,) * len(block), pipeline_mode=pl.Buffered(1)
+    )
+    slot_of = lambda c: jnp.where(c < 2 * per, 3, 1) - c % 2
+    part_of = lambda c: (c // 2) % per
     return pl.pallas_call(
         ffn_kernel,
         grid=(shards * per,),
         out_shape=(
+            shape((rows, width), BF16),
             shape((rows, width), F32),
-            shape((rows, width), F32),
-            shape(wup.shape, BF16),
-            shape(wdown.shape, BF16),
-            shape(taps.shape, F32),
+            shape((rows, width), BF16),
+            shape((4, width), F32),
+            shape((per,) + parcel, BF16),
         ),
         in_specs=[
+            whole(pltpu.SMEM),
             keep(rows, width),
             keep(width, rows),
             keep(rows, width),
-            pl.BlockSpec((1, width, CHUNK), lambda c: (c // per, 0, c % per)),
-            pl.BlockSpec((1, CHUNK, width), lambda c: (c // per, c % per, 0)),
-            pl.BlockSpec((1, 9, CHUNK), lambda c: (c // per, 0, c % per)),
+            keep(rows, width),
+            keep(rows, width),
+            keep(rows, width),
+            keep(6, width),
+            pl.BlockSpec((1, width, CHUNK), lambda c: (slot_of(c), 0, part_of(c))),
+            pl.BlockSpec((1, CHUNK, width), lambda c: (slot_of(c), part_of(c), 0)),
+            pl.BlockSpec((1, 9, CHUNK), lambda c: (slot_of(c), 0, part_of(c))),
         ],
         out_specs=(
             keep(rows, width),
             keep(rows, width),
-            pl.BlockSpec((1, width, CHUNK), lambda c: (c // per, 0, c % per)),
-            pl.BlockSpec((1, CHUNK, width), lambda c: (c // per, c % per, 0)),
-            pl.BlockSpec((1, 9, CHUNK), lambda c: (c // per, 0, c % per)),
+            keep(rows, width),
+            keep(4, width),
+            keep(per, *parcel),
         ),
         scratch_shapes=[pltpu.VMEM((4, PAD, CHUNK), F32)] * 4
         + [pltpu.VMEM((rows, CHUNK), F32)]
-        + [pltpu.VMEM((rows, CHUNK), BF16)] * 2,
-        compiler_params=pltpu.CompilerParams(vmem_limit_bytes=56 * MIB),
+        + [pltpu.VMEM((rows, CHUNK), BF16)] * 2
+        + [pltpu.VMEM((rows, width), F32)] * 2
+        + [
+            pltpu.VMEM((16, CHUNK), F32),
+            pltpu.VMEM((3,) + parcel, BF16),
+            pltpu.VMEM((per,) + parcel, BF16),
+            pltpu.VMEM((2 * per,) + parcel, BF16),
+            pltpu.VMEM((per,) + parcel, BF16),
+            pltpu.SemaphoreType.DMA((2, 3 * per)),
+        ],
+        compiler_params=pltpu.CompilerParams(
+            vmem_limit_bytes=60 * MIB, collective_id=1, has_side_effects=True
+        ),
         name="feed_forward",
-    )(h2, h2t, db, wup, wdown, taps)
-
-
-def mid_kernel(
-    live_ref, x1_ref, cot_ref, branch_ref, dh2_ref, att_ref, ctx_ref, mod_ref, wout_ref,
-    block_ref, dx1_ref, dctx_ref, dwout_ref, dmod_ref,
-    datt,
-):
-    rows_all, width = x1_ref.shape
-    gate_one, scale_two, gate_two = mod_ref[2:3, :], mod_ref[4:5, :], mod_ref[5:6, :]
-    live = live_ref[0, 0]
-
-    def fold(value):
-        return value.reshape(ROWS // 8, 8, width).sum(axis=0)
-
-    def rows_step(step, sums):
-        rows = ds(step * ROWS, ROWS)
-        after = x1_ref[rows, :]
-        dout = cot_ref[rows, :].astype(F32) * live
-        branch = branch_ref[rows, :]
-        block_ref[rows, :] = ((after + gate_two * branch) * live).astype(BF16)
-        unit, inv = normed(after)
-        dh2 = dh2_ref[rows, :]
-        dx1 = dout + norm_back(unit, inv, dh2 * (1.0 + scale_two))
-        dx1_ref[rows, :] = dx1
-        datt[rows, :] = (dx1 * gate_one).astype(BF16)
-        found = (dx1 * att_ref[rows, :], dh2, dh2 * unit, dout * branch)
-        return tuple(total + fold(one) for total, one in zip(sums, found))
-
-    start = tuple(jnp.zeros((8, width), F32) for _ in range(4))
-    sums = lax.fori_loop(0, rows_all // ROWS, rows_step, start)
-    for at in range(4):
-        dmod_ref[at : at + 1, :] = jnp.sum(sums[at], axis=0, keepdims=True)
-
-    def ctx_step(step, carry):
-        rows = ds(step * PHASE, PHASE)
-        dctx_ref[rows, :] = mm(datt[rows, :], wout_ref[...], NT).astype(BF16)
-        return carry
-
-    lax.fori_loop(0, 4, ctx_step, 0)
-    for part in range(3):
-        cols = slice(part * PHASE, (part + 1) * PHASE)
-        dwout_ref[cols, :] = mm(ctx_ref[:, cols], datt[...], TN).astype(BF16)
-
-
-def mid(live, x1, cot, branch, dh2, att, ctx, mod, wout):
-    rows, width = x1.shape
-    shape = jax.ShapeDtypeStruct
-    return pl.pallas_call(
-        mid_kernel,
-        out_shape=(
-            shape((rows, width), BF16),
-            shape((rows, width), F32),
-            shape((rows, width), BF16),
-            shape(wout.shape, BF16),
-            shape((4, width), F32),
-        ),
-        in_specs=[whole(pltpu.SMEM)] + [whole()] * 8,
-        out_specs=(whole(),) * 5,
-        scratch_shapes=[pltpu.VMEM((rows, width), BF16)],
-        compiler_params=pltpu.CompilerParams(vmem_limit_bytes=56 * MIB),
-        name="residual_backward",
-    )(live, x1, cot, branch, dh2, att, ctx, mod, wout)
+    )(live, h2, h2t, db, x1, cot, att, mod, wup, wdown, taps)
 
 
 def attn_backward_kernel(
-    u_ref, qkv_ref, probs_ref, dctx_ref, dqkv_ref, dw_ref
+    n_wide, datt_ref, ctx_ref, u_ref, wout_ref, block_in, parcels, qkv_hbm, probs_hbm,
+    dqkv_ref, block_ref, own_ref, gup_ref, gdown_ref, gtaps_ref,
+    dctx, probs_buf, weights, got_near, chip_sum, got_far, got_block, work, full, got_sums, taps_sum, taps_got,
+    sems, local_sems, in_sems, sum_sems,
 ):
     rows_all, width = u_ref.shape
+    wide, here = lax.axis_index("wide"), lax.axis_index("narrow")
     pairs = width // LANES
+    half_pairs = pairs // 2
+    steps = 4 * pairs
+    load_qkv = pltpu.make_async_copy(qkv_hbm, dqkv_ref, in_sems.at[2])
+    load_qkv.start()
+
+    def pair_of(step):
+        return (half_pairs + step // 4) % pairs
+
+    def load_probs(step):
+        return pltpu.make_async_copy(
+            probs_hbm.at[(step % 4) * pairs + pair_of(step)], probs_buf.at[step % 2], in_sems.at[step % 2]
+        )
+
+    load_probs(0).start()
+    greet([(wide, peer) for peer in narrow_peers(here)] + wide_partners(wide, here, n_wide))
+    back = Return(block_in, got_block, sems, local_sems.at[0], 0, wide, here)
+    back.start()
+    pieces = full.shape[0]
+    rows = full.shape[1]
+    per_sum = sum_semaphores(n_wide)
+    sums = [
+        WideSum(parcels.at[at, :rows], work.at[at], full.at[at], got_sums.at[at], sum_sems, at * per_sum,
+                wide, here, n_wide)
+        for at in range(pieces)
+    ]
+    levels = n_wide.bit_length() - 1
+
+    def taps_copy(level):
+        return remote(taps_sum.at[level], taps_got.at[level], sems, 6 + level, wide ^ (1 << level), here)
+
+    def taps_add(level):
+        taps_copy(level).wait_recv()
+        taps_sum[level + 1] = taps_sum[level] + taps_got[level]
+        if level + 1 < levels:
+            taps_copy(level + 1).start()
+
+    for at in range(pieces):
+        taps_sum[0, :, at * CHUNK : (at + 1) * CHUNK] = parcels[at, rows:, :].astype(F32)
+    acts = [one.actions() for one in sums]
+    for act in acts[0][0]:
+        act()
+    taps_copy(0).start()
+
+    def ctx_step(step, carry):
+        span = ds(step * PHASE, PHASE)
+        slab = wout_ref.shape[1]
+        for slot in range(4):
+            dctx[span, slot * slab : (slot + 1) * slab] = mm(
+                datt_ref[span, :], wout_ref[slot], NT
+            ).astype(BF16)
+        return carry
+
+    lax.fori_loop(0, 4, ctx_step, 0)
+    load_qkv.wait()
+
     first = lax.broadcasted_iota(jnp.int32, (PHASE, LANES), 1) < HEAD_DIM
     zero = jnp.zeros((PHASE, LANES), BF16)
     scale = HEAD_DIM**-0.5
 
     def attend_step(step, carry):
-        group, pair = step // pairs, step % pairs
-        rows = ds(group * PHASE, PHASE)
-        query = qkv_ref[rows, ds(pair * LANES, LANES)]
-        key = qkv_ref[rows, ds(width + pair * LANES, LANES)]
-        value = qkv_ref[rows, ds(2 * width + pair * LANES, LANES)]
-        dctx = dctx_ref[rows, ds(pair * LANES, LANES)]
+        group, pair = step % 4, pair_of(step)
+        load_probs(step).wait()
+
+        @pl.when(step + 1 < steps)
+        def _():
+            load_probs(step + 1).start()
+
+        span = ds(group * PHASE, PHASE)
+        query = dqkv_ref[span, ds(pair * LANES, LANES)]
+        key = dqkv_ref[span, ds(width + pair * LANES, LANES)]
+        value = dqkv_ref[span, ds(2 * width + pair * LANES, LANES)]
+        dctx_pair = dctx[span, ds(pair * LANES, LANES)]
         dq, dk, dv = [], None, None
         for head in range(2):
-            own = lambda full: jnp.where(first, full, zero) if head == 0 else jnp.where(first, zero, full)
-            probs = probs_ref[step, :, head * PHASE : (head + 1) * PHASE]
+            own = lambda both: jnp.where(first, both, zero) if head == 0 else jnp.where(first, zero, both)
+            probs = probs_buf[step % 2, :, head * PHASE : (head + 1) * PHASE]
             probs_f = probs.astype(F32)
-            dctx_own, query_own = own(dctx), own(query)
+            dctx_own, query_own = own(dctx_pair), own(query)
             dprobs = mm(value, dctx_own, NT)
             inner = jnp.sum(dprobs * probs_f, axis=0, keepdims=True)
             dscores = (probs_f * (dprobs - inner)).astype(BF16)
@@ -630,46 +860,169 @@
             dv = dv_one if dv is None else dv + dv_one
             dk = dk_one if dk is None else dk + dk_one
             dq.append(mm(dscores, key, TN))
-        dqkv_ref[rows, ds(pair * LANES, LANES)] = (
+        dqkv_ref[span, ds(pair * LANES, LANES)] = (
             jnp.where(first, dq[0], dq[1]) * scale
         ).astype(BF16)
-        dqkv_ref[rows, ds(width + pair * LANES, LANES)] = (dk * scale).astype(BF16)
-        dqkv_ref[rows, ds(2 * width + pair * LANES, LANES)] = dv.astype(BF16)
-        return carry
-
-    lax.fori_loop(0, 4 * pairs, attend_step, 0)
-    for part in range(3):
-        cols = slice(part * width, (part + 1) * width)
-
-        def weight_step(block, carry, cols=cols, part=part):
-            out_rows = ds(block * PHASE, PHASE)
-            left = dqkv_ref[:, ds(part * width + block * PHASE, PHASE)]
-            dw_ref[out_rows, cols] = mm(left, u_ref[...], TN).astype(BF16)
-            return carry
-
-        lax.fori_loop(0, width // PHASE, weight_step, 0)
-
-
-def attn_backward(u, qkv, probs, dctx):
+        dqkv_ref[span, ds(width + pair * LANES, LANES)] = (dk * scale).astype(BF16)
+        dqkv_ref[span, ds(2 * width + pair * LANES, LANES)] = dv.astype(BF16)
+        return carry
+
+    def run(acts_now):
+        for act in acts_now:
+            act()
+
+    def weight_grads(half):
+        span = width // 2
+        slab = span // 2
+        for part in range(4):
+            cols = slice(half * span, (half + 1) * span)
+            if part < 3:
+                left = dqkv_ref[:, part * width + half * span : part * width + (half + 1) * span]
+                found = mm(left, u_ref[...], TN).astype(BF16)
+            else:
+                found = mm(ctx_ref[:, cols], datt_ref[...], TN).astype(BF16)
+            for one in range(2):
+                weights[2 * half + one, part * slab : (part + 1) * slab, :] = found[
+                    one * slab : (one + 1) * slab
+                ]
+
+    near_early = remote(weights.at[3], got_near.at[0], sems, 3, wide, here ^ 1)
+    near_late = remote(weights.at[1], got_near.at[1], sems, 4, wide, here ^ 1)
+    far = remote(chip_sum, got_far, sems, 5, wide, here ^ 2)
+
+    third = steps // 6
+    lax.fori_loop(0, third, attend_step, 0)
+    run(acts[0][1] + acts[1][0])
+    taps_add(0)
+    lax.fori_loop(third, 2 * third, attend_step, 0)
+    run(acts[0][2])
+    taps_add(1)
+    lax.fori_loop(2 * third, 3 * third, attend_step, 0)
+    run(acts[0][3] + acts[1][1] + acts[2][0])
+    weight_grads(1)
+    near_early.start()
+    run(acts[0][4] + acts[1][2])
+    near_early.wait_recv()
+    chip_sum[...] = (weights[2].astype(F32) + got_near[0].astype(F32)).astype(BF16)
+    far.start()
+    lax.fori_loop(3 * third, 4 * third, attend_step, 0)
+    run(acts[0][5] + acts[1][3] + acts[2][1])
+    back.wait()
+    permutation = group_permutation(got_block.shape[1] * got_block.shape[2])
+
+    def unpermute(at, carry):
+        groups = jnp.concatenate([got_block[at, group] for group in range(4)], axis=0)
+        block_ref[at] = mm(permutation, groups, TN).astype(BF16)
+        return carry
+
+    lax.fori_loop(0, got_block.shape[0], unpermute, 0)
+    lax.fori_loop(4 * third, 5 * third, attend_step, 0)
+    run(acts[1][4] + acts[2][2])
+    lax.fori_loop(5 * third, 6 * third, attend_step, 0)
+    run(acts[0][6] + acts[1][5] + acts[2][3])
+    weight_grads(0)
+    near_late.start()
+    for level in range(2, levels):
+        taps_add(level)
+    gtaps_ref[...] = taps_sum[levels]
+
+    def put(at):
+        cols = slice(at * CHUNK, (at + 1) * CHUNK)
+        gup_ref[:, cols] = full[at, :width, :].astype(F32)
+        for block in range(width // CHUNK):
+            span = slice(width + block * CHUNK, width + (block + 1) * CHUNK)
+            gdown_ref[cols, block * CHUNK : (block + 1) * CHUNK] = full[at, span, :].astype(F32)
+
+    run(acts[2][4])
+    put(0)
+    near_late.wait_recv()
+    run(acts[1][6] + acts[2][5])
+    put(1)
+    far.wait_recv()
+    own_ref[...] = (
+        weights[0].astype(F32) + got_near[1].astype(F32) + got_far[...].astype(F32)
+    ).astype(BF16)
+    run(acts[2][6])
+    put(2)
+    for one in sums:
+        one.wait_sends()
+    for level in range(levels):
+        taps_copy(level).wait_send()
+    near_early.wait_send()
+    near_late.wait_send()
+    far.wait_send()
+
+
+def attn_backward(n_wide, datt, ctx, u, wout, block, parcels, qkv, probs):
     rows, width = u.shape
+    slots, slab, _ = wout.shape
+    pieces, parcel_rows, _ = parcels.shape
+    sum_rows = parcel_rows - 16
     shape = jax.ShapeDtypeStruct
+    levels = n_wide.bit_length() - 1
+    per_sum = sum_semaphores(n_wide)
     return pl.pallas_call(
-        attn_backward_kernel,
-        out_shape=(shape((rows, 3 * width), BF16), shape((width, 3 * width), BF16)),
-        in_specs=[whole()] * 4,
-        out_specs=(whole(),) * 2,
-        compiler_params=pltpu.CompilerParams(vmem_limit_bytes=56 * MIB),
+        partial(attn_backward_kernel, n_wide),
+        out_shape=(
+            shape((rows, 3 * width), BF16),
+            shape((slots, rows // slots, width), BF16),
+            shape((4 * slab, width), BF16),
+            shape((width, pieces * CHUNK), F32),
+            shape((pieces * CHUNK, width), F32),
+            shape((16, pieces * CHUNK), F32),
+        ),
+        in_specs=[whole()] * 6 + [whole(pl.ANY)] * 2,
+        out_specs=(whole(),) * 6,
+        scratch_shapes=[
+            pltpu.VMEM((rows, width), BF16),
+            pltpu.VMEM((2, PHASE, 2 * PHASE), BF16),
+            pltpu.VMEM((slots, 4 * slab, width), BF16),
+            pltpu.VMEM((2, 4 * slab, width), BF16),
+            pltpu.VMEM((4 * slab, width), BF16),
+            pltpu.VMEM((4 * slab, width), BF16),
+            pltpu.VMEM((slots, 4, rows // (4 * slots), width), BF16),
+            pltpu.VMEM((pieces, sum_rows, CHUNK), BF16),
+            pltpu.VMEM((pieces, sum_rows, CHUNK), BF16),
+            pltpu.VMEM((pieces, sum_landing(sum_rows, n_wide), CHUNK), BF16),
+            pltpu.VMEM((levels + 1, 16, pieces * CHUNK), F32),
+            pltpu.VMEM((levels, 16, pieces * CHUNK), F32),
+            pltpu.SemaphoreType.DMA((2, 6 + levels)),
+            pltpu.SemaphoreType.DMA((1,)),
+            pltpu.SemaphoreType.DMA((3,)),
+            pltpu.SemaphoreType.DMA((2, pieces * per_sum)),
+        ],
+        compiler_params=pltpu.CompilerParams(
+            vmem_limit_bytes=60 * MIB, collective_id=2, has_side_effects=True
+        ),
         name="attn_backward",
-    )(u, qkv, probs, dctx)
+    )(datt, ctx, u, wout, block, parcels, qkv, probs)
 
 
 def input_backward_kernel(
-    x_ref, dx1_ref, dqkv_ref, mod_ref, taps_ref, wqkv_ref,
-    dx_ref, dmod_ref, dtaps_ref,
-    base, shifted, first_in, dh1,
+    n_wide, x_ref, dx1_ref, dqkv_ref, mod_ref, taps_ref, wqkv_ref, own_ref,
+    dx_ref, dmod_ref, dtaps_ref, gattn_ref,
+    base, shifted, first_in, dh1, dx, got_dx, work, full, got_sums, sems, local_sems, sum_sems,
 ):
     rows_all, width = x_ref.shape
+    wide, here = lax.axis_index("wide"), lax.axis_index("narrow")
     shift_one, scale_one = mod_ref[0:1, :], mod_ref[1:2, :]
+    greet([(wide, peer) for peer in narrow_peers(here)] + wide_partners(wide, here, n_wide))
+    pieces = full.shape[0]
+    rows = full.shape[1]
+    per_sum = sum_semaphores(n_wide)
+    sums = [
+        WideSum(own_ref.at[at * rows : (at + 1) * rows], work.at[at], full.at[at], got_sums.at[at], sum_sems,
+                at * per_sum, wide, here, n_wide)
+        for at in range(pieces)
+    ]
+    acts = [one.actions() for one in sums]
+
+    def run(*some):
+        for act in some:
+            for one in act:
+                one()
+
+    run(acts[0][0])
     clear_edges(base)
     clear_edges(shifted)
 
@@ -681,18 +1034,23 @@
         return carry
 
     lax.fori_loop(0, rows_all // ROWS, norm_step, 0)
+    slab = wqkv_ref.shape[1]
 
     def du_step(group, carry):
-        rows = ds(group * PHASE, PHASE)
+        span = ds(group * PHASE, PHASE)
         total = None
         for part in range(3):
-            cols = slice(part * width, (part + 1) * width)
-            one = mm(dqkv_ref[rows, cols], wqkv_ref[:, cols], NN)
-            total = one if total is None else total + one
+            for slot in range(4):
+                cols = slice(part * width + slot * slab, part * width + (slot + 1) * slab)
+                weight = wqkv_ref[slot, :, part * width : (part + 1) * width]
+                one = mm(dqkv_ref[span, cols], weight, NN)
+                total = one if total is None else total + one
         base[group, HALF : HALF + PHASE, :] = total
         return carry
 
+    run(acts[0][1], acts[1][0])
     lax.fori_loop(0, 4, du_step, 0)
+    run(acts[0][2], acts[1][1])
 
     def conv_step(block, carry):
         lanes = ds(block * LANES, LANES)
@@ -701,49 +1059,82 @@
                   dtaps_ref, dh1)
         return carry
 
-    lax.fori_loop(0, width // LANES, conv_step, 0)
+    lax.fori_loop(0, width // (2 * LANES), conv_step, 0)
+    run(acts[0][3], acts[1][2])
+    lax.fori_loop(width // (2 * LANES), width // LANES, conv_step, 0)
+    run(acts[0][4], acts[1][3])
 
     def fold(value):
         return value.reshape(ROWS // 8, 8, width).sum(axis=0)
 
     def rows_step(step, sums):
-        rows = ds(step * ROWS, ROWS)
-        unit, inv = normed(x_ref[rows, :].astype(F32))
-        grad = dh1[rows, :]
-        dx = dx1_ref[rows, :] + norm_back(unit, inv, grad * (1.0 + scale_one))
-        dx_ref[rows, :] = dx.astype(BF16)
+        span = ds(step * ROWS, ROWS)
+        group, source = step // (PHASE // ROWS), step % (PHASE // ROWS)
+        unit, inv = normed(x_ref[span, :].astype(F32))
+        grad = dh1[span, :]
+        dx[group, source] = (
+            dx1_ref[span, :] + norm_back(unit, inv, grad * (1.0 + scale_one))
+        ).astype(BF16)
         return tuple(total + fold(one) for total, one in zip(sums, (grad, grad * unit)))
 
     start = tuple(jnp.zeros((8, width), F32) for _ in range(2))
-    sums = lax.fori_loop(0, rows_all // ROWS, rows_step, start)
+    found = lax.fori_loop(0, rows_all // ROWS, rows_step, start)
     for at in range(2):
-        dmod_ref[at : at + 1, :] = jnp.sum(sums[at], axis=0, keepdims=True)
-
-
-def input_backward(x, dx1, dqkv, mod, taps, wqkv):
+        dmod_ref[at : at + 1, :] = jnp.sum(found[at], axis=0, keepdims=True)
+    back = Return(dx, got_dx, sems, local_sems.at[0], 0, wide, here)
+    back.start()
+    run(acts[0][5], acts[1][4])
+    run(acts[0][6], acts[1][5])
+    gattn_ref[:rows, :] = full[0].astype(F32)
+    permutation = group_permutation(got_dx.shape[1] * got_dx.shape[2])
+    back.wait()
+
+    def unpermute(at, carry):
+        groups = jnp.concatenate([got_dx[at, group] for group in range(4)], axis=0)
+        dx_ref[at] = mm(permutation, groups, TN)
+        return carry
+
+    lax.fori_loop(0, got_dx.shape[0], unpermute, 0)
+    run(acts[1][6])
+    gattn_ref[rows:, :] = full[1].astype(F32)
+    for one in sums:
+        one.wait_sends()
+
+
+def input_backward(n_wide, x, dx1, dqkv, mod, taps, wqkv, own):
     rows, width = x.shape
+    slots = wqkv.shape[0]
+    pieces = 2
+    sum_rows = own.shape[0] // pieces
     shape = jax.ShapeDtypeStruct
+    per_sum = sum_semaphores(n_wide)
     return pl.pallas_call(
-        input_backward_kernel,
-        out_shape=(shape((rows, width), BF16), shape((2, width), F32), shape((9, width), F32)),
-        in_specs=[whole()] * 6,
-        out_specs=(whole(),) * 3,
-        scratch_shapes=[pltpu.VMEM((4, PAD, width), F32)] * 3 + [pltpu.VMEM((rows, width), F32)],
-        compiler_params=pltpu.CompilerParams(vmem_limit_bytes=56 * MIB),
+        partial(input_backward_kernel, n_wide),
+        out_shape=(
+            shape((slots, rows // slots, width), F32),
+            shape((2, width), F32),
+            shape((16, width), F32),
+            shape(own.shape, F32),
+        ),
+        in_specs=[whole()] * 7,
+        out_specs=(whole(),) * 4,
+        scratch_shapes=[pltpu.VMEM((4, PAD, width), F32)] * 3
+        + [
+            pltpu.VMEM((rows, width), F32),
+            pltpu.VMEM((4, slots, rows // (4 * slots), width), BF16),
+            pltpu.VMEM((slots, 4, rows // (4 * slots), width), BF16),
+            pltpu.VMEM((pieces, sum_rows, width), BF16),
+            pltpu.VMEM((pieces, sum_rows, width), BF16),
+            pltpu.VMEM((pieces, sum_landing(sum_rows, n_wide), width), BF16),
+            pltpu.SemaphoreType.DMA((2, 3)),
+            pltpu.SemaphoreType.DMA((1,)),
+            pltpu.SemaphoreType.DMA((2, pieces * per_sum)),
+        ],
+        compiler_params=pltpu.CompilerParams(
+            vmem_limit_bytes=60 * MIB, collective_id=3, has_side_effects=True
+        ),
         name="input_backward",
-    )(x, dx1, dqkv, mod, taps, wqkv)
-
-
-def to_groups(shard):
-    latents, rows, width = shard.shape
-    split = shard.reshape(latents, rows // (2 * SIDE), 2, HALF, 2, width)
-    return split.transpose(0, 2, 4, 1, 3, 5).reshape(latents, 4, rows // 4, width)
-
-
-def from_groups(groups):
-    latents, _, rows, width = groups.shape
-    split = groups.reshape(latents, 2, 2, rows // HALF, HALF, width)
-    return split.transpose(0, 3, 1, 4, 2, 5).reshape(latents, 4 * rows, width)
+    )(x, dx1, dqkv, mod, taps, wqkv, own)
 
 
 def per_device(
@@ -754,10 +1145,7 @@
     rows_all = shard_rows * lat_dev
     local = w_up.shape[1]
 
-    def latent_out(latent):
-        parts = latent.reshape(1, 4, rows_all // 4, width)
-        return from_groups(lax.all_to_all(parts, "narrow", 2, 0, tiled=True))
-
+    n_wide = lax.axis_size("wide")
     qkv_t = w_qkv.transpose(2, 1, 0).reshape(w_qkv.shape[2], 3 * width)
     ktaps_own = jnp.pad(k_ffn.reshape(9, local), ((0, 23), (0, 0)))
     attn_taps = k_attn.reshape(9, width).astype(F32)
@@ -771,36 +1159,25 @@
         live, own_silu, attn_taps, tokens, cotangent, w_ada, qkv_t, w_out, w_up, w_down, ktaps_own
     )
     cot = cot.reshape(rows_all, width)
-    wqkv = wqkv.reshape(width, 3 * width)
-    wout = wout.reshape(width, width)
     ffn_taps = ktaps[:, :9].astype(F32)
-    branch, dh2, dwup, dwdown, dffn_taps = ffn(h2, h2t, db, wup, wdown, ffn_taps)
-    block_g, dx1, dctx, dwout, dmod_mid = mid(live, x1, cot, branch, dh2, att, ctx, mod, wout)
-    dqkv, dwqkv = attn_backward(u, qkv, probs, dctx)
-    dx, dmod_first, dattn_taps = input_backward(x, dx1, dqkv, mod, attn_taps, wqkv)
-
-    block = latent_out(block_g)
-    grad_tokens = latent_out(dx).astype(F32)
-
-    def reduce(parts):
-        return lax.psum(lax.psum_scatter(parts, "narrow", scatter_dimension=0, tiled=True), "wide")
-
-    shared = jnp.concatenate(
-        [dwup, dwdown, jnp.pad(dffn_taps, ((0, 0), (0, 7), (0, 0))).astype(BF16)], axis=1
-    ).reshape(lat_dev * (2 * width + 16), local)
-    late = jnp.concatenate(
-        [dwout.reshape(lat_dev, -1, width), dwqkv.reshape(lat_dev, -1, width)], axis=1
-    ).reshape(-1, width)
-    shared = reduce(shared).astype(F32)
-    late = reduce(late).astype(F32)
-    grad_w_up, grad_w_down = shared[:width], shared[width : 2 * width]
-    grad_k_ffn = shared[2 * width : 2 * width + 9].reshape(3, 3, local)
+    block_g, dx1, datt, dmod_mid, parcels = ffn(
+        live, h2, h2t, db, x1, cot, att, mod, wup, wdown, ffn_taps
+    )
+    block_g = block_g.reshape(4, lat_dev, shard_rows // 4, width)
+    dqkv, block, own, grad_w_up, grad_w_down, gtaps = attn_backward(
+        n_wide, datt, ctx, u, wout, block_g, parcels, qkv, probs
+    )
+    grad_tokens, dmod_first, dattn_taps, gattn = input_backward(
+        n_wide, x, dx1, dqkv, mod, attn_taps, wqkv, own
+    )
+    grad_k_ffn = gtaps[:9].reshape(3, 3, local)
     heads_width = w_out.shape[0]
-    grad_w_out = late[:heads_width]
-    grad_w_qkv = late[heads_width:].reshape(heads_width, 3, width).transpose(2, 1, 0)
+    gattn = gattn.reshape(4, heads_width, width)
+    grad_w_qkv = gattn[:3].transpose(2, 0, 1)
+    grad_w_out = gattn[3]
 
     dmod = jnp.concatenate([dmod_first, dmod_mid], axis=0)
-    small = jnp.concatenate([dmod, dattn_taps, jnp.zeros((1, width), F32)], axis=0).astype(BF16)
+    small = jnp.concatenate([dmod, dattn_taps[:9], jnp.zeros((1, width), F32)], axis=0).astype(BF16)
     small_all = lax.all_gather(small, ("wide", "narrow"))
     silu_all = lax.all_gather(silu_low, "wide", tiled=True)
     mod_all = small_all[:, :6].reshape(-1, 6 * width)

time: 593 us -> 481 us (0.81)
  waiting for transfers between devices: 122 us -> 0 us
  Pallas kernels: 292 us -> 371 us
  local copies, waits for them, and re-layouts: 38.3 us -> 20.5 us
  blocking collectives: 87.4 us -> 70 us
  other arithmetic: 17 us -> 3.34 us
  between operations: 14.6 us -> 1.41 us
  starting transfers between devices: 7.6 us -> 0 us
    reduce_scatter x2 -> x0, waiting for transfers between devices: 122 us -> none  [reduce(): lax.psum_scatter(parts, 'narrow', scatter_dimension=0, tiled=True)]
    pallas_call x3 -> x2, Pallas kernels: 73.7 us -> 141 us  [the longest x1 82.1 us: attn_backward(): pl.pallas_call(partial(attn_backward_kernel, n_wide), out_shape=(shape((r...]
    all_gather x1, blocking collectives: 56.6 us -> 39.1 us  [per_device(): small_all = lax.all_gather(small, ('wide', 'narrow'))]
    reshape x5 -> x1, local copies, waits for them, and re-layouts: 14.5 us -> 0.63 us  [per_device(): grad_k_ffn = gtaps[:9].reshape(3, 3, local)]
    pallas_call x1, Pallas kernels: 97.1 us -> 110 us  [ffn(): pl.pallas_call(ffn_kernel, grid=(shards * per,), out_shape=(shape((rows,...]
    concatenate x6 -> x3, other arithmetic: 13 us -> 0.78 us  [per_device(): jnp.concatenate([dmod, dattn_taps[:9], jnp.zeros((1, width), F32)], axis=0)]
    all_to_all x2 -> x0, starting transfers between devices: 7.48 us -> none  [latent_out(): return from_groups(lax.all_to_all(parts, 'narrow', 2, 0, tiled=True))]
  transfers between devices with their start and end apart: 5 -> 0, of which waited for: 3 -> 0; matrix products, arithmetic and copies ran while one was open for 6% -> 0% of each run, Pallas kernels for 4% -> 0%
where the time goes in v3:
time: 481 us; the launch traced here: 479 us
  Pallas kernels  371 us (77%)
  blocking collectives  70 us (15%)
  local copies, waits for them, and re-layouts  20.5 us (4%)
  matrix products  13 us (3%)
    pallas_call x1, Pallas kernels, front(): pl.pallas_call(front_kernel, out_shape=(shape((rows, width), BF16), shape...  120 us
    pallas_call x1, Pallas kernels, ffn(): pl.pallas_call(ffn_kernel, grid=(shards * per,), out_shape=(shape((rows,...  110 us
    pallas_call x1, Pallas kernels, attn_backward(): pl.pallas_call(partial(attn_backward_kernel, n_wide), out_shape=(shape((r...  82.1 us
    pallas_call x1, Pallas kernels, input_backward(): pl.pallas_call(partial(input_backward_kernel, n_wide), out_shape=(shape((...  59 us
    all_gather x1, blocking collectives, per_device(): small_all = lax.all_gather(small, ('wide', 'narrow'))  39.1 us
    all_gather x1, blocking collectives, per_device(): silu_all = lax.all_gather(silu_low, 'wide', tiled=True)  30.9 us
    dot_general x2, matrix products, mm(): return lax.dot_general(left, right, dims, preferred_element_type=F32)  13 us

profile of v3, /device:TPU:0, one launch (start us, length us, event | category | flops | bytes accessed | tf_op | source)
XLA Modules:
  0.0 479.4 jit_solution(10515582331361247069)
XLA Ops:
  0.6 0.7 fusion.6
  1.4 0.6 broadcast_in_dim.11.silu_ref
  2.7 1.4 reshape.116.taps_ref
  4.0 2.1 copy.24
  6.2 0.7 reshape.108
  6.9 0.6 pad.4.ktaps_src
  7.5 120.2 %attn_forward.1 = (bf16[1024,768]{1,0:T(8,128)(2,1)}, bf16[4,4,64,768]{3,2,1,0:T(8,128)(2,1)}, f32[6,768]{1,0:T(8,128)}, bf16[1024,768]{1,0:T(8,128)(2,1)}, bf16...) custom-call(f32[1,1]{1,0:T(1,128)} %bitcast.1.live_ref, ...), custom_call_target="tpu_custom_call" | custom-call | tf_op jit(solution)/shard_map/attn_forward/pallas_call | solution.py:495
  127.8 1.6 slice_convert_fusion.taps_ref
  129.4 109.8 %feed_forward.1 = (bf16[1024,768]{1,0:T(8,128)(2,1)}, f32[1024,768]{1,0:T(8,128)}, bf16[1024,768]{1,0:T(8,128)(2,1)}, f32[4,768]{1,0:T(4,128)}, bf16[3,1552,256]{2,1,0:T(8,128)(2,1)}) custom-call(f32[1,1]{1,0:T(1,128)} %bitcast.1.live_ref, bf16[1024,768]{1,0:T(8,128)(2,1)} %get-tuple-element.42.h2_ref, bf16[768,1024]{1,0:T(8,128)(2,1)} %get-tuple-element.43.h2t_ref, ...), custom_call_target="tpu_custom_call" | custom-call | tf_op jit(solution)/shard_map/feed_forward/pallas_call | solution.py:719
  239.2 82.1 %attn_backward.1 = (bf16[1024,2304]{1,0:T(8,128)(2,1)}, bf16[4,256,768]{2,1,0:T(8,128)(2,1)}, bf16[768,768]{1,0:T(8,128)(2,1)}, f32[768,768]{1,0:T(8,128)}, f32[768,768]{1,0:T(8,128)}, /*index=5*/f32[16,768]{1,0:T(8,128)}) custom-call(bf16[1024,768]{1,0:T(8,128)(2,1)} %get-tuple-element.52.datt_ref, bf16[1024,768]{1,0:T(8,128)(2,1)} %get-tuple-element.53.ctx_ref, ...), custom_call_target="tpu_custom_call" | custom-call | tf_op jit(solution)/shard_map/attn_backward/pallas_call | solution.py:964
  321.3 59.0 %input_backward.1 = (f32[4,256,768]{2,1,0:T(8,128)}, f32[2,768]{1,0:T(2,128)}, f32[16,768]{1,0:T(8,128)}, f32[768,768]{1,0:T(8,128)}) custom-call(bf16[1024,768]{1,0:T(8,128)(2,1)} %get-tuple-element.61.x_ref, f32[1024,768]{1,0:T(8,128)} %get-tuple-element.62.dx1_ref, bf16[1024,2304]{1,0:T(8,128)(2,1)} %get-tuple-element.63.dqkv_ref, ...), custom_call_target="tpu_custom_call" | custom-call | tf_op jit(solution)/shard_map/input_backward/pallas_call | solution.py:1111
  380.2 0.0 copy-start.4
  380.3 0.8 fusion.2
  381.1 0.7 convert_bitcast_fusion.1
  381.8 0.1 pad.8.clone
  381.9 0.1 maximum_maximum_fusion
  381.9 39.1 %all_gather.7 = bf16[32,16,768]{2,1,0:T(8,128)(2,1)S(1)} all-gather(bf16[1,16,768]{2,1,0:T(8,128)(2,1)S(1)} %maximum_maximum_fusion), channel_id=1, replica_groups=mesh['wide'=8,'narrow'=4] {'wide','narrow'}, dimensions={0}, use_global_device_ids=true | all-gather | bytes 811008 | tf_op jit(solution)/shard_map/all_gather | solution.py:1181
  421.1 0.1 copy.25
  421.2 30.9 %all-gather = bf16[8,4,768]{2,1,0:T(4,128)(2,1)S(1)} all-gather(bf16[1,4,768]{2,1,0:T(4,128)(2,1)S(1)} %fusion.16), channel_id=1, replica_groups=mesh['wide'=8,'narrow'=4] {'wide'}, dimensions={0}, use_global_device_ids=true | all-gather | bytes 55296 | tf_op jit(solution)/shard_map/all_gather | solution.py:1182
  452.1 7.3 %fusion.12 = f32[768,4608]{1,0:T(8,128)} fusion(bf16[32,768]{1,0:T(8,128)(2,1)S(1)} %reshape.118, bf16[32,4608]{1,0:T(8,128)(2,1)S(1)} %bitcast.31), kind=kOutput, calls=%fused_computation.21 | convolution fusion | flops 226492416 | bytes 14499840 | tf_op jit(solution)/shard_map/dot_general | solution.py:31
  459.4 5.7 %fusion.8 = f32[4,768]{1,0:T(4,128)} fusion(bf16[4,768]{1,0:T(4,128)(2,1)S(1)} %copy-done.4, bf16[768,4608]{1,0:T(8,128)(2,1)} %ada_hbm.1, bf16[32,4608]{1,0:T(8,128)(2,1)S(1)} %bitcast.32, s32[]{:T(128)S(6)} %select_n.7), kind=kOutput, calls=%fused_computation.16 | convolution fusion | flops 28342272 | bytes 7133188 | tf_op jit(solution)/shard_map/dot_general | solution.py:31
  465.1 0.2 convert_reduce_fusion
  465.4 0.6 reshape.112
  466.0 1.3 slice.30
  467.3 2.1 slice.32
  469.4 0.6 reshape.113
  470.0 2.7 copy.31
  472.7 1.7 copy.32
  474.3 1.1 copy-done.3
  475.5 1.4 copy.33
  476.9 1.1 copy-done.2
  478.0 1.4 copy.34
  (16 shorter events, 0.1 us)
Async XLA Ops:
  321.2 60.5 %copy-start.6 = (f32[4,768]{1,0:T(4,128)S(1)}, f32[4,768]{1,0:T(4,128)}, u32[]{:S(2)}) copy-start(f32[4,768]{1,0:T(4,128)} %get-tuple-element.68) | copy-start | bytes 36868
  380.2 40.9 %copy-start.4 = (bf16[4,768]{1,0:T(4,128)(2,1)S(1)}, bf16[4,768]{1,0:T(4,128)(2,1)}, u32[]{:S(2)}) copy-start(bf16[4,768]{1,0:T(4,128)(2,1)} %param.12) | copy-start | bytes 18436
  459.4 6.6 %copy-start.1 = (f32[768,768]{1,0:T(8,128)S(1)}, f32[768,768]{1,0:T(8,128)}, u32[]{:S(2)}) copy-start(f32[768,768]{1,0:T(8,128)} %get-tuple-element.70) | copy-start | bytes 7077892
  466.0 3.4 copy-start.5
  467.3 5.4 %copy-start = (f32[4,256,768]{2,1,0:T(8,128)S(1)}, f32[4,256,768]{2,1,0:T(8,128)}, u32[]{:S(2)}) copy-start(f32[4,256,768]{2,1,0:T(8,128)} %get-tuple-element.85) | copy-start | bytes 9437188
  472.7 2.8 copy-start.3
  475.5 2.5 copy-start.2

commit v4 on v3

--- a/solution.py
+++ b/solution.py
@@ -100,16 +100,22 @@
 
 class Gather:
     def __init__(self, src, dst, sems, local_sem, first, wide, here):
-        half_rows = src.shape[0] // 2
+        count = src.shape[0]
+        half_rows = count // 2
         half = wide % 2
-        mine, other = ds(half * half_rows, half_rows), ds((1 - half) * half_rows, half_rows)
         far, near = here ^ 2, here ^ 1
-        self.own = pltpu.make_async_copy(src, dst.at[0], local_sem)
-        self.near = remote(src, dst.at[1], sems, first, wide, near)
-        self.far = remote(src.at[mine], dst.at[2, mine], sems, first + 1, wide, far)
-        self.share = remote(dst.at[2, mine], dst.at[3, mine], sems, first + 2, wide, near)
-        self.swap = remote(dst.at[2, mine], dst.at[2, mine], sems, first + 3, wide ^ 1, here)
-        self.share_swapped = remote(dst.at[2, other], dst.at[3, other], sems, first + 4, wide, near)
+
+        def at(slot, which=None):
+            if which is None:
+                return dst.at[slot * count : (slot + 1) * count]
+            return dst.at[ds(slot * count + which * half_rows, half_rows, 16)]
+
+        self.own = pltpu.make_async_copy(src, at(0), local_sem)
+        self.near = remote(src, at(1), sems, first, wide, near)
+        self.far = remote(src.at[ds(half * half_rows, half_rows, 16)], at(2, half), sems, first + 1, wide, far)
+        self.share = remote(at(2, half), at(3, half), sems, first + 2, wide, near)
+        self.swap = remote(at(2, half), at(2, half), sems, first + 3, wide ^ 1, here)
+        self.share_swapped = remote(at(2, 1 - half), at(3, 1 - half), sems, first + 4, wide, near)
 
     def start_near(self):
         self.own.start()
@@ -266,6 +272,10 @@
             self.half_copy(level).wait_send()
         for level in range(self.levels):
             self.spread_copy(level).wait_send()
+
+
+def halvings_ahead(pieces, levels):
+    return [min(levels, pieces - at) for at in range(pieces)]
 
 
 def greet(partners):
@@ -401,16 +411,12 @@
     g_qkv.forward_swapped()
     g_out.forward_swapped()
     g_qkv.finish()
-    shards_here = wqkv_ref.shape[0]
-    slab = wqkv_ref.shape[1]
 
     def project_step(step, carry):
         rows = ds(step * PHASE, PHASE)
         for part in range(3):
-            for shard in range(shards_here):
-                weight = wqkv_ref[shard, :, part * width : (part + 1) * width]
-                cols = slice(part * width + shard * slab, part * width + (shard + 1) * slab)
-                qkv_ref[rows, cols] = mm(u_ref[rows, :], weight, NT).astype(BF16)
+            cols = slice(part * width, (part + 1) * width)
+            qkv_ref[rows, cols] = mm(u_ref[rows, :], wqkv_ref[:, cols], NT).astype(BF16)
         return carry
 
     lax.fori_loop(0, 4, project_step, 0)
@@ -451,10 +457,7 @@
 
     def out_step(step, carry):
         rows = ds(step * PHASE, PHASE)
-        total = None
-        for shard in range(shards_here):
-            one = mm(ctx_ref[rows, shard * slab : (shard + 1) * slab], wout_ref[shard], NN)
-            total = one if total is None else total + one
+        total = mm(ctx_ref[rows, :], wout_ref[...], NN)
         att_ref[rows, :] = total.astype(BF16)
         x1_ref[rows, :] = x_ref[rows, :].astype(F32) + gate_one * total
         return carry
@@ -490,7 +493,7 @@
     rows = latents * shard_rows
     steps = 4 * (width // LANES)
     shape = jax.ShapeDtypeStruct
-    full = lambda shard: shape((latents,) + shard.shape, BF16)
+    full = lambda shard: shape((latents * shard.shape[0],) + shard.shape[1:], BF16)
     moved = (latents, 4, shard_rows // 4, width)
     return pl.pallas_call(
         front_kernel,
@@ -535,125 +538,182 @@
 
 
 def ffn_kernel(
-    live_ref, h2_ref, h2t_ref, db_ref, x1_ref, cot_ref, att_ref, mod_ref, wup_ref, wdown_ref, taps_ref,
+    n_wide, live_ref, h2_ref, h2t_ref, db_ref, x1_ref, cot_ref, att_ref, mod_ref,
+    wup_before, wup_even, wup_odd, wup_after, wdown_even, wdown_odd, taps_even, taps_odd,
     block_ref, dx1_ref, datt_ref, dmod_ref, sums_ref,
-    hid, hid_moved, grad, grad_moved, slope, act, dhid, branch, dh2, dtaps, work, chip_sum, got_near, got_far,
-    sems,
+    hid_even, hid_odd, hid_moved, grad, grad_moved, slope, act, act_t, dhid, branch, dtaps,
+    work, chip_sum, got_near, got_far, got_sums, sems, sum_sems,
 ):
     rows_all, width = h2_ref.shape
+    dh2 = dx1_ref
     wide, here = lax.axis_index("wide"), lax.axis_index("narrow")
     step, steps = pl.program_id(0), pl.num_programs(0)
-    part, turn, odd = (step // 2) % (steps // 4), step // 2, step % 2
-    early = step < steps // 2
+    quarters = [slice(q * PHASE, (q + 1) * PHASE) for q in range(4)]
+    inside = slice(HALF, HALF + PHASE)
+    lane_blocks = [slice(at * LANES, (at + 1) * LANES) for at in range(CHUNK // LANES)]
+    col = lax.broadcasted_iota(jnp.int32, (ROWS, LANES), 0) % HALF
+
+    partners = [(wide, here ^ 1), (wide, here ^ 2)] + wide_partners(wide, here, n_wide)[:HALVINGS]
+    pieces, sum_rows = got_sums.shape[0], got_sums.shape[1]
+    sums = [
+        WideSum(sums_ref.at[at, : 2 * width], sums_ref.at[at, : 2 * width], None, got_sums.at[at], sum_sems,
+                at * HALVINGS, wide, here, n_wide)
+        for at in range(pieces)
+    ]
+    schedule = halvings_ahead(pieces, sums[0].levels)
 
     def to_near(at):
         return remote(work.at[at % 2], got_near.at[at], sems, at, wide, here ^ 1)
 
     def to_far(at):
-        return remote(chip_sum.at[at], got_far.at[at], sems, steps // 2 + at, wide, here ^ 2)
+        return remote(chip_sum.at[at], got_far.at[at], sems, steps + at, wide, here ^ 2)
 
     @pl.when(step == 0)
     def _():
         barrier = pltpu.get_barrier_semaphore()
-        for partner in (here ^ 1, here ^ 2):
+        for partner in partners:
             pl.semaphore_signal(
-                barrier, inc=1, device_id=(wide, partner), device_id_type=pl.DeviceIdType.MESH
+                barrier, inc=1, device_id=partner, device_id_type=pl.DeviceIdType.MESH
             )
-        for ref in (hid, hid_moved, grad, grad_moved):
+        for ref in (hid_even, hid_odd, hid_moved, grad, grad_moved):
             clear_edges(ref)
         branch[...] = jnp.zeros_like(branch)
         dh2[...] = jnp.zeros_like(dh2)
         dtaps[...] = jnp.zeros_like(dtaps)
-        pl.semaphore_wait(barrier, 2)
-
-    def up_step(group, carry):
-        rows = ds(group * PHASE, PHASE)
-        hid[group, HALF : HALF + PHASE, :] = mm(h2_ref[rows, :], wup_ref[0], NN)
-        return carry
-
-    lax.fori_loop(0, 4, up_step, 0)
-
-    for block in range(CHUNK // LANES):
-        lanes = slice(block * LANES, (block + 1) * LANES)
-        shift_cols(hid, hid_moved, lanes)
-        taps = [taps_ref[0, t : t + 1, lanes] for t in range(9)]
-
-        def act_step(at, carry):
+        dhid[...] = jnp.zeros_like(dhid)
+        full = mm(h2_ref[...], wup_even[...], NN)
+        for q in range(4):
+            hid_even[q, inside, :] = full[quarters[q]]
+        pl.semaphore_wait(barrier, len(partners))
+
+    def moved_cols(group, value):
+        if group % 2:
+            return jnp.where(col == 0, 0.0, pltpu.roll(value, 1, 0))
+        return jnp.where(col == HALF - 1, 0.0, pltpu.roll(value, ROWS - 1, 0))
+
+    def static_tap(base, shifted, group, tap_row, tap_col, start, lanes):
+        src_row, row_move = tap_source(group // 2, tap_row)
+        src_col, col_move = tap_source(group % 2, tap_col)
+        ref = base if col_move == 0 else shifted
+        first = HALF + row_move * HALF + start
+        return ref[2 * src_row + src_col, first : first + ROWS, lanes]
+
+    def weights_back(q, wup_last, slot):
+        dh2[quarters[q], :] += mm(dhid[quarters[q], :], wup_last[...], NT)
+        if q < width // PHASE:
+            slot[quarters[q], :] = mm(h2t_ref[quarters[q], :], dhid[...], NN).astype(BF16)
+
+    def forward(hid, wdown, taps_ref, wup_last, slot):
+        taps = [[taps_ref[0, t : t + 1, lanes] for t in range(9)] for lanes in lane_blocks]
+        for part in range(PHASE // ROWS):
+            rows = slice(HALF + part * ROWS, HALF + (part + 1) * ROWS)
             for group in range(4):
-                total = jnp.zeros((ROWS, LANES), F32)
-                for tap in range(9):
-                    total += taps[tap] * tap_value(
-                        hid, hid_moved, group, tap // 3, tap % 3, at * ROWS, lanes
+                for lanes in lane_blocks:
+                    hid_moved[group, rows, lanes] = moved_cols(group, hid[group, rows, lanes])
+        for part in range(PHASE // ROWS):
+            grad[part, inside, :] = mm(db_ref[quarters[part], :], wdown[...], NT)
+            weights_back(part, wup_last, slot)
+            for group in range(4):
+                for at, lanes in enumerate(lane_blocks):
+                    total = jnp.zeros((ROWS, LANES), F32)
+                    for tap in range(9):
+                        total += taps[at][tap] * static_tap(
+                            hid, hid_moved, group, tap // 3, tap % 3, part * ROWS, lanes
+                        )
+                    square = total * total
+                    turned = jnp.tanh(total * (square * (GELU_C * GELU_A) + GELU_C))
+                    half = 0.5 * turned + 0.5
+                    bend = total * (half - half * half)
+                    start = group * PHASE + part * ROWS
+                    act[start : start + ROWS, lanes] = (total * half).astype(BF16)
+                    slope[start : start + ROWS, lanes] = half + bend * (
+                        square * (6.0 * GELU_C * GELU_A) + 2.0 * GELU_C
                     )
-                square = total * total
-                turned = jnp.tanh(total * (square * (GELU_C * GELU_A) + GELU_C))
-                half = 0.5 * turned + 0.5
-                bend = total * (half - half * half)
-                rows = ds(group * PHASE + at * ROWS, ROWS)
-                act[rows, lanes] = (total * half).astype(BF16)
-                slope[rows, lanes] = half + bend * (
-                    square * (6.0 * GELU_C * GELU_A) + 2.0 * GELU_C
-                )
-            return carry
-
-        lax.fori_loop(0, PHASE // ROWS, act_step, 0)
-
-    def dact_step(group, carry):
-        rows = ds(group * PHASE, PHASE)
-        dact = mm(db_ref[rows, :], wdown_ref[0], NT)
-        grad[group, HALF : HALF + PHASE, :] = dact * slope[rows, :]
-        return carry
-
-    lax.fori_loop(0, 4, dact_step, 0)
-
-    for block in range(CHUNK // LANES):
-        lanes = slice(block * LANES, (block + 1) * LANES)
-        shift_cols(grad, grad_moved, lanes)
-        conv_back(grad, grad_moved, hid, lanes, [taps_ref[0, t : t + 1, lanes] for t in range(9)],
-                  dtaps, dhid)
-
-    def final_step(group, carry):
-        rows = ds(group * PHASE, PHASE)
-        branch[rows, :] += mm(act[rows, :], wdown_ref[0], NN)
-        dh2[rows, :] += mm(dhid[rows, :], wup_ref[0], NT)
-        return carry
-
-    lax.fori_loop(0, 4, final_step, 0)
-
-    @pl.when(jnp.logical_and(odd == 0, turn >= 2))
+
+    def backward(hid, hid_next, wdown, wup_next, taps_ref, slot):
+        taps = [[taps_ref[0, t : t + 1, lanes] for t in range(9)] for lanes in lane_blocks]
+        act_t[...] = act[...].T
+        for part in range(PHASE // ROWS):
+            rows = slice(HALF + part * ROWS, HALF + (part + 1) * ROWS)
+            for group in range(4):
+                start = group * PHASE + part * ROWS
+                for lanes in lane_blocks:
+                    value = grad[group, rows, lanes] * slope[start : start + ROWS, lanes]
+                    grad[group, rows, lanes] = value
+                    grad_moved[group, rows, lanes] = moved_cols(group, value)
+        sums = [[jnp.zeros((8, LANES), F32) for _ in range(9)] for _ in lane_blocks]
+        for part in range(PHASE // ROWS):
+            hid_next[part, inside, :] = mm(h2_ref[quarters[part], :], wup_next[...], NN)
+            branch[quarters[part], :] += mm(act[quarters[part], :], wdown[...], NN)
+            if part < width // CHUNK:
+                block = slice(part * CHUNK, (part + 1) * CHUNK)
+                slot[width + part * CHUNK : width + (part + 1) * CHUNK, :] = mm(
+                    act_t[...], db_ref[:, block], NN
+                ).astype(BF16)
+            for group in range(4):
+                start = group * PHASE + part * ROWS
+                for at, lanes in enumerate(lane_blocks):
+                    own = hid[group, HALF + part * ROWS : HALF + (part + 1) * ROWS, lanes]
+                    total = jnp.zeros((ROWS, LANES), F32)
+                    for tap in range(9):
+                        moved = static_tap(
+                            grad, grad_moved, group, 2 - tap // 3, 2 - tap % 3, part * ROWS, lanes
+                        )
+                        total += taps[at][tap] * moved
+                        sums[at][tap] += (own * moved).reshape(ROWS // 8, 8, LANES).sum(axis=0)
+                    dhid[start : start + ROWS, lanes] = total.astype(BF16)
+        for at, lanes in enumerate(lane_blocks):
+            for tap in range(9):
+                dtaps[tap : tap + 1, lanes] = jnp.sum(sums[at][tap], axis=0, keepdims=True)
+        slot[2 * width :, :] = dtaps[...].astype(BF16)
+
+    def settle(pair):
+        to_near(pair).wait_recv()
+
+        @pl.when(pair < steps // 2)
+        def _():
+            chip_sum[pair] = (work[2].astype(F32) + got_near[pair].astype(F32)).astype(BF16)
+            to_far(pair).start()
+
+        @pl.when(pair >= steps // 2)
+        def _():
+            part = pair - steps // 2
+            to_far(part).wait_recv()
+            sums_ref[part] = (
+                work[2].astype(F32) + got_near[pair].astype(F32) + got_far[part].astype(F32)
+            ).astype(BF16)
+
+        for part in range(pieces):
+
+            @pl.when(pair == steps // 2 + part)
+            def _():
+                for at in range(part):
+                    sums[at].finish_half(part - at - 1)
+                for at in range(part + 1):
+                    if part - at < schedule[at]:
+                        sums[at].start_half(part - at)
+
+    forward(hid_even, wdown_even, taps_even, wup_before, work.at[2])
+
+    @pl.when(step >= 1)
     def _():
-        to_near(turn - 2).wait_send()
-
-    slot = work.at[jnp.where(odd == 0, turn % 2, 2)]
-    slot[:width, :] = mm(h2t_ref[...], dhid[...], NN).astype(BF16)
-    down = mm(act[...], db_ref[...], TN).astype(BF16)
-    for block in range(width // CHUNK):
-        rows = slice(width + block * CHUNK, width + (block + 1) * CHUNK)
-        slot[rows, :] = down[:, block * CHUNK : (block + 1) * CHUNK]
-    slot[2 * width :, :] = dtaps[...].astype(BF16)
-
-    @pl.when(odd == 0)
+        settle(step - 1)
+
+    @pl.when(step >= 2)
     def _():
-        to_near(turn).start()
-
-    @pl.when(odd == 1)
-    def _():
-        to_near(turn).wait_recv()
-
-    @pl.when(jnp.logical_and(odd == 1, early))
-    def _():
-        chip_sum[part] = (work[2].astype(F32) + got_near[turn].astype(F32)).astype(BF16)
-        to_far(part).start()
-
-    @pl.when(jnp.logical_and(odd == 1, jnp.logical_not(early)))
-    def _():
-        to_far(part).wait_recv()
-        sums_ref[part] = (
-            work[2].astype(F32) + got_near[turn].astype(F32) + got_far[part].astype(F32)
-        ).astype(BF16)
+        to_near(step - 2).wait_send()
+
+    even_slot = work.at[step % 2]
+    backward(hid_even, hid_odd, wdown_even, wup_odd, taps_even, even_slot)
+    forward(hid_odd, wdown_odd, taps_odd, wup_even, even_slot)
+    to_near(step).start()
+    backward(hid_odd, hid_even, wdown_odd, wup_after, taps_odd, work.at[2])
 
     @pl.when(step == steps - 1)
     def _():
+        for q in range(4):
+            weights_back(q, wup_odd, work.at[2])
+        settle(step)
         gate_one, scale_two, gate_two = mod_ref[2:3, :], mod_ref[4:5, :], mod_ref[5:6, :]
         live = live_ref[0, 0]
 
@@ -675,13 +735,17 @@
             return tuple(total + fold(one) for total, one in zip(sums, found))
 
         start = tuple(jnp.zeros((8, width), F32) for _ in range(4))
-        sums = lax.fori_loop(0, rows_all // ROWS, rows_step, start)
+        totals = lax.fori_loop(0, rows_all // ROWS, rows_step, start)
         for at in range(4):
-            dmod_ref[at : at + 1, :] = jnp.sum(sums[at], axis=0, keepdims=True)
-        for at in (steps // 2 - 2, steps // 2 - 1):
+            dmod_ref[at : at + 1, :] = jnp.sum(totals[at], axis=0, keepdims=True)
+        for at in (steps - 2, steps - 1):
             to_near(at).wait_send()
-        for at in range(steps // 4):
+        for at in range(steps // 2):
             to_far(at).wait_send()
+        for at in range(pieces):
+            sums[at].finish_half(schedule[at] - 1)
+            for level in range(schedule[at]):
+                sums[at].half_copy(level).wait_send()
 
 
 def conv_back(grad, grad_moved, source, lanes, taps, dtaps_ref, out_ref):
@@ -705,20 +769,43 @@
         dtaps_ref[tap : tap + 1, lanes] = jnp.sum(sums[tap], axis=0, keepdims=True)
 
 
-def ffn(live, h2, h2t, db, x1, cot, att, mod, wup, wdown, taps):
+def ffn(n_wide, live, h2, h2t, db, x1, cot, att, mod, wup, wdown, taps):
     rows, width = h2.shape
-    shards, _, local = wup.shape
+    shards, _, local = taps.shape
     per = local // CHUNK
+    steps = shards * per // 2
     parcel = (2 * width + 16, CHUNK)
     shape = jax.ShapeDtypeStruct
     keep = lambda *block: pl.BlockSpec(
         block, lambda c: (0,) * len(block), pipeline_mode=pl.Buffered(1)
     )
-    slot_of = lambda c: jnp.where(c < 2 * per, 3, 1) - c % 2
-    part_of = lambda c: (c // 2) % per
+
+    def slot_and_part(step, odd):
+        return jnp.where(step < per, 3, 1) - odd, step % per
+
+    def up_block(move, odd):
+        def index(step):
+            return slot_and_part(jnp.clip(step + move, 0, steps - 1), odd)
+
+        return pl.BlockSpec((width, CHUNK), index)
+
+    def down_block(odd):
+        def index(step):
+            slot, part = slot_and_part(step, odd)
+            return slot * per + part, 0
+
+        return pl.BlockSpec((CHUNK, width), index)
+
+    def taps_block(odd):
+        def index(step):
+            slot, part = slot_and_part(step, odd)
+            return slot, 0, part
+
+        return pl.BlockSpec((1, 9, CHUNK), index)
+
     return pl.pallas_call(
-        ffn_kernel,
-        grid=(shards * per,),
+        partial(ffn_kernel, n_wide),
+        grid=(steps,),
         out_shape=(
             shape((rows, width), BF16),
             shape((rows, width), F32),
@@ -735,9 +822,14 @@
             keep(rows, width),
             keep(rows, width),
             keep(6, width),
-            pl.BlockSpec((1, width, CHUNK), lambda c: (slot_of(c), 0, part_of(c))),
-            pl.BlockSpec((1, CHUNK, width), lambda c: (slot_of(c), part_of(c), 0)),
-            pl.BlockSpec((1, 9, CHUNK), lambda c: (slot_of(c), 0, part_of(c))),
+            up_block(-1, 1),
+            up_block(0, 0),
+            up_block(0, 1),
+            up_block(1, 0),
+            down_block(0),
+            down_block(1),
+            taps_block(0),
+            taps_block(1),
         ],
         out_specs=(
             keep(rows, width),
@@ -746,30 +838,34 @@
             keep(4, width),
             keep(per, *parcel),
         ),
-        scratch_shapes=[pltpu.VMEM((4, PAD, CHUNK), F32)] * 4
-        + [pltpu.VMEM((rows, CHUNK), F32)]
-        + [pltpu.VMEM((rows, CHUNK), BF16)] * 2
-        + [pltpu.VMEM((rows, width), F32)] * 2
+        scratch_shapes=[pltpu.VMEM((4, PAD, CHUNK), F32)] * 5
         + [
+            pltpu.VMEM((rows, CHUNK), F32),
+            pltpu.VMEM((rows, CHUNK), BF16),
+            pltpu.VMEM((CHUNK, rows), BF16),
+            pltpu.VMEM((rows, CHUNK), BF16),
+            pltpu.VMEM((rows, width), F32),
             pltpu.VMEM((16, CHUNK), F32),
             pltpu.VMEM((3,) + parcel, BF16),
             pltpu.VMEM((per,) + parcel, BF16),
-            pltpu.VMEM((2 * per,) + parcel, BF16),
+            pltpu.VMEM((steps,) + parcel, BF16),
             pltpu.VMEM((per,) + parcel, BF16),
-            pltpu.SemaphoreType.DMA((2, 3 * per)),
+            pltpu.VMEM((per, sum_landing(2 * width, n_wide), CHUNK), BF16),
+            pltpu.SemaphoreType.DMA((2, steps + per)),
+            pltpu.SemaphoreType.DMA((2, per * HALVINGS)),
         ],
         compiler_params=pltpu.CompilerParams(
-            vmem_limit_bytes=60 * MIB, collective_id=1, has_side_effects=True
+            vmem_limit_bytes=62 * MIB, collective_id=1, has_side_effects=True
         ),
         name="feed_forward",
-    )(live, h2, h2t, db, x1, cot, att, mod, wup, wdown, taps)
+    )(live, h2, h2t, db, x1, cot, att, mod, wup, wup, wup, wup, wdown, wdown, taps, taps)
 
 
 def attn_backward_kernel(
-    n_wide, datt_ref, ctx_ref, u_ref, wout_ref, block_in, parcels, qkv_hbm, probs_hbm,
-    dqkv_ref, block_ref, own_ref, gup_ref, gdown_ref, gtaps_ref,
-    dctx, probs_buf, weights, got_near, chip_sum, got_far, got_block, work, full, got_sums, taps_sum, taps_got,
-    sems, local_sems, in_sems, sum_sems,
+    n_wide, datt_ref, ctx_ref, u_ref, wout_ref, parcels, qkv_hbm, probs_hbm,
+    dqkv_ref, own_ref, full, gtaps_ref,
+    dctx, probs_buf, weights, got_near, chip_sum, got_far, work, got_sums, taps_sum, taps_got,
+    sems, in_sems, sum_sems,
 ):
     rows_all, width = u_ref.shape
     wide, here = lax.axis_index("wide"), lax.axis_index("narrow")
@@ -788,21 +884,27 @@
         )
 
     load_probs(0).start()
-    greet([(wide, peer) for peer in narrow_peers(here)] + wide_partners(wide, here, n_wide))
-    back = Return(block_in, got_block, sems, local_sems.at[0], 0, wide, here)
-    back.start()
+    greet([(wide, here ^ 2), (wide, here ^ 1)] + wide_partners(wide, here, n_wide))
     pieces = full.shape[0]
     rows = full.shape[1]
     per_sum = sum_semaphores(n_wide)
+    ahead = halvings_ahead(pieces, min(HALVINGS, n_wide.bit_length() - 1))
     sums = [
         WideSum(parcels.at[at, :rows], work.at[at], full.at[at], got_sums.at[at], sum_sems, at * per_sum,
-                wide, here, n_wide)
+                wide, here, n_wide, done=ahead[at])
         for at in range(pieces)
     ]
     levels = n_wide.bit_length() - 1
+    queues = [one.actions() for one in sums]
+
+    def advance(*which):
+        for at in which:
+            if queues[at]:
+                for act in queues[at].pop(0):
+                    act()
 
     def taps_copy(level):
-        return remote(taps_sum.at[level], taps_got.at[level], sems, 6 + level, wide ^ (1 << level), here)
+        return remote(taps_sum.at[level], taps_got.at[level], sems, 3 + level, wide ^ (1 << level), here)
 
     def taps_add(level):
         taps_copy(level).wait_recv()
@@ -812,18 +914,12 @@
 
     for at in range(pieces):
         taps_sum[0, :, at * CHUNK : (at + 1) * CHUNK] = parcels[at, rows:, :].astype(F32)
-    acts = [one.actions() for one in sums]
-    for act in acts[0][0]:
-        act()
     taps_copy(0).start()
+    advance(2, 0, 1)
 
     def ctx_step(step, carry):
         span = ds(step * PHASE, PHASE)
-        slab = wout_ref.shape[1]
-        for slot in range(4):
-            dctx[span, slot * slab : (slot + 1) * slab] = mm(
-                datt_ref[span, :], wout_ref[slot], NT
-            ).astype(BF16)
+        dctx[span, :] = mm(datt_ref[span, :], wout_ref[...], NT).astype(BF16)
         return carry
 
     lax.fori_loop(0, 4, ctx_step, 0)
@@ -833,7 +929,7 @@
     zero = jnp.zeros((PHASE, LANES), BF16)
     scale = HEAD_DIM**-0.5
 
-    def attend_step(step, carry):
+    def attend(step):
         group, pair = step % 4, pair_of(step)
         load_probs(step).wait()
 
@@ -865,11 +961,15 @@
         ).astype(BF16)
         dqkv_ref[span, ds(width + pair * LANES, LANES)] = (dk * scale).astype(BF16)
         dqkv_ref[span, ds(2 * width + pair * LANES, LANES)] = dv.astype(BF16)
-        return carry
-
-    def run(acts_now):
-        for act in acts_now:
-            act()
+
+    def attend_loop(begin, end, plan):
+        def body(step, carry):
+            for at, what in plan:
+                pl.when(step == at)(what)
+            attend(step)
+            return carry
+
+        lax.fori_loop(begin, end, body, 0)
 
     def weight_grads(half):
         span = width // 2
@@ -886,64 +986,37 @@
                     one * slab : (one + 1) * slab
                 ]
 
-    near_early = remote(weights.at[3], got_near.at[0], sems, 3, wide, here ^ 1)
-    near_late = remote(weights.at[1], got_near.at[1], sems, 4, wide, here ^ 1)
-    far = remote(chip_sum, got_far, sems, 5, wide, here ^ 2)
-
-    third = steps // 6
-    lax.fori_loop(0, third, attend_step, 0)
-    run(acts[0][1] + acts[1][0])
-    taps_add(0)
-    lax.fori_loop(third, 2 * third, attend_step, 0)
-    run(acts[0][2])
-    taps_add(1)
-    lax.fori_loop(2 * third, 3 * third, attend_step, 0)
-    run(acts[0][3] + acts[1][1] + acts[2][0])
+    near_early = remote(weights.at[3], got_near.at[0], sems, 0, wide, here ^ 1)
+    near_late = remote(weights.at[1], got_near.at[1], sems, 1, wide, here ^ 1)
+    far = remote(chip_sum, got_far, sems, 2, wide, here ^ 2)
+
+    later = lambda *which: partial(advance, *which)
+    attend_loop(
+        0, steps // 2,
+        [(2, later(2, 0)), (5, later(1)), (7, partial(taps_add, 0)), (8, later(2, 0)), (11, later(1))],
+    )
     weight_grads(1)
     near_early.start()
-    run(acts[0][4] + acts[1][2])
+    advance(2)
     near_early.wait_recv()
     chip_sum[...] = (weights[2].astype(F32) + got_near[0].astype(F32)).astype(BF16)
     far.start()
-    lax.fori_loop(3 * third, 4 * third, attend_step, 0)
-    run(acts[0][5] + acts[1][3] + acts[2][1])
-    back.wait()
-    permutation = group_permutation(got_block.shape[1] * got_block.shape[2])
-
-    def unpermute(at, carry):
-        groups = jnp.concatenate([got_block[at, group] for group in range(4)], axis=0)
-        block_ref[at] = mm(permutation, groups, TN).astype(BF16)
-        return carry
-
-    lax.fori_loop(0, got_block.shape[0], unpermute, 0)
-    lax.fori_loop(4 * third, 5 * third, attend_step, 0)
-    run(acts[1][4] + acts[2][2])
-    lax.fori_loop(5 * third, 6 * third, attend_step, 0)
-    run(acts[0][6] + acts[1][5] + acts[2][3])
+    attend_loop(
+        steps // 2, steps,
+        [(13, later(1, 0)), (14, partial(taps_add, 1)), (16, later(2))],
+    )
     weight_grads(0)
     near_late.start()
     for level in range(2, levels):
         taps_add(level)
     gtaps_ref[...] = taps_sum[levels]
-
-    def put(at):
-        cols = slice(at * CHUNK, (at + 1) * CHUNK)
-        gup_ref[:, cols] = full[at, :width, :].astype(F32)
-        for block in range(width // CHUNK):
-            span = slice(width + block * CHUNK, width + (block + 1) * CHUNK)
-            gdown_ref[cols, block * CHUNK : (block + 1) * CHUNK] = full[at, span, :].astype(F32)
-
-    run(acts[2][4])
-    put(0)
     near_late.wait_recv()
-    run(acts[1][6] + acts[2][5])
-    put(1)
+    while any(queues):
+        advance(0, 1, 2)
     far.wait_recv()
     own_ref[...] = (
         weights[0].astype(F32) + got_near[1].astype(F32) + got_far[...].astype(F32)
     ).astype(BF16)
-    run(acts[2][6])
-    put(2)
     for one in sums:
         one.wait_sends()
     for level in range(levels):
@@ -953,9 +1026,10 @@
     far.wait_send()
 
 
-def attn_backward(n_wide, datt, ctx, u, wout, block, parcels, qkv, probs):
+def attn_backward(n_wide, datt, ctx, u, wout, parcels, qkv, probs):
     rows, width = u.shape
-    slots, slab, _ = wout.shape
+    slots = lax.axis_size("narrow")
+    slab = wout.shape[0] // slots
     pieces, parcel_rows, _ = parcels.shape
     sum_rows = parcel_rows - 16
     shape = jax.ShapeDtypeStruct
@@ -965,14 +1039,12 @@
         partial(attn_backward_kernel, n_wide),
         out_shape=(
             shape((rows, 3 * width), BF16),
-            shape((slots, rows // slots, width), BF16),
             shape((4 * slab, width), BF16),
-            shape((width, pieces * CHUNK), F32),
-            shape((pieces * CHUNK, width), F32),
+            shape((pieces, sum_rows, CHUNK), BF16),
             shape((16, pieces * CHUNK), F32),
         ),
-        in_specs=[whole()] * 6 + [whole(pl.ANY)] * 2,
-        out_specs=(whole(),) * 6,
+        in_specs=[whole()] * 5 + [whole(pl.ANY)] * 2,
+        out_specs=(whole(),) * 4,
         scratch_shapes=[
             pltpu.VMEM((rows, width), BF16),
             pltpu.VMEM((2, PHASE, 2 * PHASE), BF16),
@@ -980,28 +1052,34 @@
             pltpu.VMEM((2, 4 * slab, width), BF16),
             pltpu.VMEM((4 * slab, width), BF16),
             pltpu.VMEM((4 * slab, width), BF16),
-            pltpu.VMEM((slots, 4, rows // (4 * slots), width), BF16),
-            pltpu.VMEM((pieces, sum_rows, CHUNK), BF16),
             pltpu.VMEM((pieces, sum_rows, CHUNK), BF16),
             pltpu.VMEM((pieces, sum_landing(sum_rows, n_wide), CHUNK), BF16),
             pltpu.VMEM((levels + 1, 16, pieces * CHUNK), F32),
             pltpu.VMEM((levels, 16, pieces * CHUNK), F32),
-            pltpu.SemaphoreType.DMA((2, 6 + levels)),
-            pltpu.SemaphoreType.DMA((1,)),
+            pltpu.SemaphoreType.DMA((2, 3 + levels)),
             pltpu.SemaphoreType.DMA((3,)),
             pltpu.SemaphoreType.DMA((2, pieces * per_sum)),
         ],
         compiler_params=pltpu.CompilerParams(
-            vmem_limit_bytes=60 * MIB, collective_id=2, has_side_effects=True
+            vmem_limit_bytes=56 * MIB, collective_id=2, has_side_effects=True
         ),
         name="attn_backward",
-    )(datt, ctx, u, wout, block, parcels, qkv, probs)
+    )(datt, ctx, u, wout, parcels, qkv, probs)
+
+
+def one_hot(rows, columns, wanted):
+    row = lax.broadcasted_iota(jnp.int32, (rows, columns), 0)
+    column = lax.broadcasted_iota(jnp.int32, (rows, columns), 1)
+    return jnp.where(column == wanted(row), 1.0, 0.0).astype(BF16)
+
+
+SMALL = 16
 
 
 def input_backward_kernel(
-    n_wide, x_ref, dx1_ref, dqkv_ref, mod_ref, taps_ref, wqkv_ref, own_ref,
-    dx_ref, dmod_ref, dtaps_ref, gattn_ref,
-    base, shifted, first_in, dh1, dx, got_dx, work, full, got_sums, sems, local_sems, sum_sems,
+    n_wide, x_ref, dx1_ref, dqkv_ref, mod_ref, taps_ref, wqkv_ref, own_ref, silu_ref, dmod_ref, block_in,
+    got_dx, got_block, full, small, dtaps_ref,
+    base, shifted, first_in, dh1, dx, work, got_sums, tap_sums, tap_got, sems, local_sems, sum_sems, small_sems,
 ):
     rows_all, width = x_ref.shape
     wide, here = lax.axis_index("wide"), lax.axis_index("narrow")
@@ -1015,14 +1093,17 @@
                 at * per_sum, wide, here, n_wide)
         for at in range(pieces)
     ]
-    acts = [one.actions() for one in sums]
-
-    def run(*some):
-        for act in some:
-            for one in act:
-                one()
-
-    run(acts[0][0])
+    queues = [one.actions() for one in sums]
+
+    def advance(*which):
+        for at in which:
+            if queues[at]:
+                for act in queues[at].pop(0):
+                    act()
+
+    advance(0, 1)
+    block_back = Return(block_in, got_block, sems, local_sems.at[1], 3, wide, here)
+    block_back.start()
     clear_edges(base)
     clear_edges(shifted)
 
@@ -1034,23 +1115,20 @@
         return carry
 
     lax.fori_loop(0, rows_all // ROWS, norm_step, 0)
-    slab = wqkv_ref.shape[1]
 
     def du_step(group, carry):
         span = ds(group * PHASE, PHASE)
         total = None
         for part in range(3):
-            for slot in range(4):
-                cols = slice(part * width + slot * slab, part * width + (slot + 1) * slab)
-                weight = wqkv_ref[slot, :, part * width : (part + 1) * width]
-                one = mm(dqkv_ref[span, cols], weight, NN)
-                total = one if total is None else total + one
+            cols = slice(part * width, (part + 1) * width)
+            one = mm(dqkv_ref[span, cols], wqkv_ref[:, cols], NN)
+            total = one if total is None else total + one
         base[group, HALF : HALF + PHASE, :] = total
         return carry
 
-    run(acts[0][1], acts[1][0])
-    lax.fori_loop(0, 4, du_step, 0)
-    run(acts[0][2], acts[1][1])
+    lax.fori_loop(0, 3, du_step, 0)
+    advance(0)
+    lax.fori_loop(3, 4, du_step, 0)
 
     def conv_step(block, carry):
         lanes = ds(block * LANES, LANES)
@@ -1059,17 +1137,22 @@
                   dtaps_ref, dh1)
         return carry
 
-    lax.fori_loop(0, width // (2 * LANES), conv_step, 0)
-    run(acts[0][3], acts[1][2])
-    lax.fori_loop(width // (2 * LANES), width // LANES, conv_step, 0)
-    run(acts[0][4], acts[1][3])
+    for block in range(width // LANES):
+        if block % 2:
+            advance(0)
+        else:
+            advance(1)
+        lax.fori_loop(block, block + 1, conv_step, 0)
 
     def fold(value):
         return value.reshape(ROWS // 8, 8, width).sum(axis=0)
 
-    def rows_step(step, sums):
-        span = ds(step * ROWS, ROWS)
-        group, source = step // (PHASE // ROWS), step % (PHASE // ROWS)
+    back = Return(dx, got_dx, sems, local_sems.at[0], 0, wide, here)
+
+    def rows_step(at, sums):
+        source = (at // 4 + 2) % 4 ^ here
+        group = at % 4
+        span = ds(group * PHASE + source * ROWS, ROWS)
         unit, inv = normed(x_ref[span, :].astype(F32))
         grad = dh1[span, :]
         dx[group, source] = (
@@ -1077,64 +1160,201 @@
         ).astype(BF16)
         return tuple(total + fold(one) for total, one in zip(sums, (grad, grad * unit)))
 
-    start = tuple(jnp.zeros((8, width), F32) for _ in range(2))
-    found = lax.fori_loop(0, rows_all // ROWS, rows_step, start)
-    for at in range(2):
-        dmod_ref[at : at + 1, :] = jnp.sum(found[at], axis=0, keepdims=True)
-    back = Return(dx, got_dx, sems, local_sems.at[0], 0, wide, here)
-    back.start()
-    run(acts[0][5], acts[1][4])
-    run(acts[0][6], acts[1][5])
-    gattn_ref[:rows, :] = full[0].astype(F32)
-    permutation = group_permutation(got_dx.shape[1] * got_dx.shape[2])
+    found = tuple(jnp.zeros((8, width), F32) for _ in range(2))
+    for at in range(4):
+        found = lax.fori_loop(4 * at, 4 * at + 4, rows_step, found)
+        if at < 2:
+            back.copies[at].start()
+        elif at == 3:
+            back.copies[2].start()
+    back.own.start()
+    dmod = [jnp.sum(one, axis=0, keepdims=True) for one in found]
+    dmod += [dmod_ref[at : at + 1, :] for at in range(4)]
+
+    partners = wide_partners(wide, here, n_wide)[::-1] + [(wide, here ^ 2), (wide, here ^ 1)]
+    levels = len(partners)
+    stack = jnp.concatenate([silu_ref[0:1, :].astype(F32)] + dmod + [jnp.zeros((SMALL - 7, width), F32)])
+    small[0] = stack.astype(BF16)
+    tap_sums[0, :9, :] = dtaps_ref[:9, :]
+    tap_sums[0, 9:, :] = jnp.zeros((7, width), F32)
+
+    def small_copies(level):
+        have = 1 << level
+        return (
+            remote(small.at[:have], small.at[have : 2 * have], small_sems, 2 * level, *partners[level]),
+            remote(tap_sums.at[level], tap_got.at[level], small_sems, 2 * level + 1, *partners[level]),
+        )
+
+    def small_start(level):
+        for copy in small_copies(level):
+            copy.start()
+
+    def small_finish(level):
+        for copy in small_copies(level):
+            copy.wait_recv()
+        tap_sums[level + 1] = tap_sums[level] + tap_got[level]
+
+    small_start(0)
+    advance(0, 1)
+    for level in range(levels):
+        small_finish(level)
+        if level + 1 < levels:
+            small_start(level + 1)
+        if level == 1:
+            advance(0, 1)
+    dtaps_ref[...] = tap_sums[levels]
+    while any(queues):
+        advance(0, 1)
+    block_back.wait()
     back.wait()
-
-    def unpermute(at, carry):
-        groups = jnp.concatenate([got_dx[at, group] for group in range(4)], axis=0)
-        dx_ref[at] = mm(permutation, groups, TN)
-        return carry
-
-    lax.fori_loop(0, got_dx.shape[0], unpermute, 0)
-    run(acts[1][6])
-    gattn_ref[rows:, :] = full[1].astype(F32)
+    for level in range(levels):
+        for copy in small_copies(level):
+            copy.wait_send()
     for one in sums:
         one.wait_sends()
 
 
-def input_backward(n_wide, x, dx1, dqkv, mod, taps, wqkv, own):
+def input_backward(n_wide, x, dx1, dqkv, mod, taps, wqkv, own, silu_row, dmod, block):
     rows, width = x.shape
-    slots = wqkv.shape[0]
+    slots = lax.axis_size("narrow")
     pieces = 2
     sum_rows = own.shape[0] // pieces
     shape = jax.ShapeDtypeStruct
     per_sum = sum_semaphores(n_wide)
+    levels = (n_wide * slots).bit_length() - 1
+    back = shape((slots, 4, rows // (4 * slots), width), BF16)
     return pl.pallas_call(
         partial(input_backward_kernel, n_wide),
         out_shape=(
-            shape((slots, rows // slots, width), F32),
-            shape((2, width), F32),
-            shape((16, width), F32),
-            shape(own.shape, F32),
+            back,
+            back,
+            shape((pieces, sum_rows, width), BF16),
+            shape((1 << levels, SMALL, width), BF16),
+            shape((SMALL, width), F32),
         ),
-        in_specs=[whole()] * 7,
-        out_specs=(whole(),) * 4,
+        in_specs=[whole()] * 10,
+        out_specs=(whole(),) * 5,
         scratch_shapes=[pltpu.VMEM((4, PAD, width), F32)] * 3
         + [
             pltpu.VMEM((rows, width), F32),
             pltpu.VMEM((4, slots, rows // (4 * slots), width), BF16),
-            pltpu.VMEM((slots, 4, rows // (4 * slots), width), BF16),
-            pltpu.VMEM((pieces, sum_rows, width), BF16),
             pltpu.VMEM((pieces, sum_rows, width), BF16),
             pltpu.VMEM((pieces, sum_landing(sum_rows, n_wide), width), BF16),
-            pltpu.SemaphoreType.DMA((2, 3)),
-            pltpu.SemaphoreType.DMA((1,)),
+            pltpu.VMEM((levels + 1, SMALL, width), F32),
+            pltpu.VMEM((levels, SMALL, width), F32),
+            pltpu.SemaphoreType.DMA((2, 6)),
+            pltpu.SemaphoreType.DMA((2,)),
             pltpu.SemaphoreType.DMA((2, pieces * per_sum)),
+            pltpu.SemaphoreType.DMA((2, 2 * levels)),
         ],
         compiler_params=pltpu.CompilerParams(
-            vmem_limit_bytes=60 * MIB, collective_id=3, has_side_effects=True
+            vmem_limit_bytes=56 * MIB, collective_id=3, has_side_effects=True
         ),
         name="input_backward",
-    )(x, dx1, dqkv, mod, taps, wqkv, own)
+    )(x, dx1, dqkv, mod, taps, wqkv, own, silu_row, dmod, block)
+
+
+def outputs_kernel(
+    dx_in, block_in, attn_sum, ffn_sum, small, cond_ref, ada_hbm,
+    gada_hbm, dx_hbm, block_hbm, gqkv_hbm, gout_hbm, gup_hbm, gdown_hbm, gcond_ref,
+    ada, gada, dx, block, gqkv, gout, gup, gdown, sems, in_sem,
+):
+    width = small.shape[-1]
+    here = lax.axis_index("narrow")
+    load_ada = pltpu.make_async_copy(ada_hbm, ada, in_sem.at[0])
+    load_ada.start()
+    started = []
+
+    def put(src, dst):
+        copy = pltpu.make_async_copy(src, dst, sems.at[len(started)])
+        copy.start()
+        started.append(copy)
+
+    devices = small.shape[0]
+    shares = small[...].reshape(devices * SMALL, width)
+    pick = lambda row: mm(
+        one_hot(devices, devices * SMALL, lambda at: at * SMALL + row), shares, NN
+    ).astype(BF16)
+    silu_all = pick(0)
+    for part in range(6):
+        gada[part] = mm(silu_all, pick(1 + part), TN)
+        put(gada.at[part], gada_hbm.at[:, part * width : (part + 1) * width])
+    slab = attn_sum.shape[1] // 2
+    for part in range(3):
+        gqkv[part] = attn_sum[part // 2, (part % 2) * slab : (part % 2 + 1) * slab, :].astype(F32).T
+        put(gqkv.at[part], gqkv_hbm.at[part])
+    gout[...] = attn_sum[1, slab:, :].astype(F32)
+    put(gout, gout_hbm)
+    permutation = group_permutation(dx_in.shape[1] * dx_in.shape[2])
+    for at in range(dx_in.shape[0]):
+        for source, held, out in ((dx_in, dx, dx_hbm), (block_in, block, block_hbm)):
+            groups = jnp.concatenate([source[at, group] for group in range(4)], axis=0)
+            held[at] = mm(permutation, groups, TN).astype(held.dtype)
+            put(held.at[at], out.at[at])
+    for at in range(ffn_sum.shape[0]):
+        cols = slice(at * CHUNK, (at + 1) * CHUNK)
+        gup[:, cols] = ffn_sum[at, :width, :].astype(F32)
+        for part in range(width // CHUNK):
+            span = slice(width + part * CHUNK, width + (part + 1) * CHUNK)
+            gdown[cols, part * CHUNK : (part + 1) * CHUNK] = ffn_sum[at, span, :].astype(F32)
+        put(gdown.at[cols], gdown_hbm.at[cols])
+    put(gup, gup_hbm)
+
+    def own_column(row, part):
+        away = row ^ here
+        place = ((away // 2) % 2) * (devices // 4) + (away % 2) * (devices // 2)
+        return jnp.where(row < cond_ref.shape[0], place * SMALL + 1 + part, -1)
+
+    load_ada.wait()
+    grad_silu = jnp.zeros((16, width), F32)
+    for part in range(6):
+        own = mm(
+            one_hot(16, devices * SMALL, lambda row, part=part: own_column(row, part)), shares, NN
+        ).astype(BF16)
+        grad_silu += mm(own, ada[:, part * width : (part + 1) * width], NT)
+    cond = cond_ref[...].astype(F32)
+    gate = 1.0 / (1.0 + jnp.exp(-cond))
+    gcond_ref[...] = grad_silu[: cond_ref.shape[0]] * (gate * (1.0 + cond * (1.0 - gate)))
+    for copy in started:
+        copy.wait()
+
+
+def outputs(dx, block, attn_sum, ffn_sum, small, cond, w_ada):
+    slots, _, quarter, width = dx.shape
+    slab = attn_sum.shape[1] // 2
+    pieces = ffn_sum.shape[0]
+    local = pieces * CHUNK
+    shape = jax.ShapeDtypeStruct
+    tokens = (slots, 4 * quarter, width)
+    return pl.pallas_call(
+        outputs_kernel,
+        out_shape=(
+            shape(w_ada.shape, F32),
+            shape(tokens, F32),
+            shape(tokens, BF16),
+            shape((3, width, slab), F32),
+            shape((slab, width), F32),
+            shape((width, local), F32),
+            shape((local, width), F32),
+            shape(cond.shape, F32),
+        ),
+        in_specs=[whole()] * 6 + [whole(pl.ANY)],
+        out_specs=(whole(pl.ANY),) * 7 + (whole(),),
+        scratch_shapes=[
+            pltpu.VMEM(w_ada.shape, BF16),
+            pltpu.VMEM((6, width, width), F32),
+            pltpu.VMEM(tokens, F32),
+            pltpu.VMEM(tokens, BF16),
+            pltpu.VMEM((3, width, slab), F32),
+            pltpu.VMEM((slab, width), F32),
+            pltpu.VMEM((width, local), F32),
+            pltpu.VMEM((local, width), F32),
+            pltpu.SemaphoreType.DMA((6 + 3 + 1 + 2 * slots + pieces + 1,)),
+            pltpu.SemaphoreType.DMA((1,)),
+        ],
+        compiler_params=pltpu.CompilerParams(vmem_limit_bytes=56 * MIB),
+        name="outputs",
+    )(dx, block, attn_sum, ffn_sum, small, cond, w_ada)
 
 
 def per_device(
@@ -1159,34 +1379,21 @@
         live, own_silu, attn_taps, tokens, cotangent, w_ada, qkv_t, w_out, w_up, w_down, ktaps_own
     )
     cot = cot.reshape(rows_all, width)
-    ffn_taps = ktaps[:, :9].astype(F32)
+    ffn_taps = ktaps.reshape(lat_dev, -1, local)[:, :9].astype(F32)
     block_g, dx1, datt, dmod_mid, parcels = ffn(
-        live, h2, h2t, db, x1, cot, att, mod, wup, wdown, ffn_taps
+        n_wide, live, h2, h2t, db, x1, cot, att, mod, wup, wdown, ffn_taps
     )
     block_g = block_g.reshape(4, lat_dev, shard_rows // 4, width)
-    dqkv, block, own, grad_w_up, grad_w_down, gtaps = attn_backward(
-        n_wide, datt, ctx, u, wout, block_g, parcels, qkv, probs
+    dqkv, own, ffn_sum, gtaps = attn_backward(n_wide, datt, ctx, u, wout, parcels, qkv, probs)
+    got_dx, got_block, attn_sum, small, dattn_taps = input_backward(
+        n_wide, x, dx1, dqkv, mod, attn_taps, wqkv, own, own_silu, dmod_mid, block_g
     )
-    grad_tokens, dmod_first, dattn_taps, gattn = input_backward(
-        n_wide, x, dx1, dqkv, mod, attn_taps, wqkv, own
+    grad_w_ada, grad_tokens, block, gqkv, grad_w_out, grad_w_up, grad_w_down, grad_condition = outputs(
+        got_dx, got_block, attn_sum, ffn_sum, small, condition, w_ada
     )
     grad_k_ffn = gtaps[:9].reshape(3, 3, local)
-    heads_width = w_out.shape[0]
-    gattn = gattn.reshape(4, heads_width, width)
-    grad_w_qkv = gattn[:3].transpose(2, 0, 1)
-    grad_w_out = gattn[3]
-
-    dmod = jnp.concatenate([dmod_first, dmod_mid], axis=0)
-    small = jnp.concatenate([dmod, dattn_taps[:9], jnp.zeros((1, width), F32)], axis=0).astype(BF16)
-    small_all = lax.all_gather(small, ("wide", "narrow"))
-    silu_all = lax.all_gather(silu_low, "wide", tiled=True)
-    mod_all = small_all[:, :6].reshape(-1, 6 * width)
-    grad_k_attn = small_all[:, 6:15].astype(F32).sum(axis=0).reshape(3, 3, width)
-    grad_w_ada = mm(silu_all, mod_all, TN)
-    mod_low = lax.dynamic_slice_in_dim(mod_all, lax.axis_index("wide") * lat_dev, lat_dev, 0)
-    grad_silu = mm(mod_low, w_ada, NT)
-    _, pull_silu = jax.vjp(jax.nn.silu, cond_f)
-    (grad_condition,) = pull_silu(grad_silu)
+    grad_k_attn = dattn_taps[:9].reshape(3, 3, width)
+    grad_w_qkv = gqkv.transpose(1, 0, 2)
     return (
         block,
         grad_tokens,

time: 481 us -> 376 us (0.78)
  blocking collectives: 70 us -> 0 us
  Pallas kernels: 371 us -> 356 us
  matrix products: 13 us -> 0 us
  local copies, waits for them, and re-layouts: 20.5 us -> 10.5 us
    all_gather x2 -> x0, blocking collectives: 70 us -> none  [the longest x1 39.1 us: per_device(): small_all = lax.all_gather(small, ('wide', 'narrow'))]
    pallas_call x1, Pallas kernels: 82.1 us -> 63.1 us  [attn_backward(): pl.pallas_call(partial(attn_backward_kernel, n_wide), out_shape=(shape((r...]
    dot_general x2 -> x0, matrix products: 13 us -> none  [mm(): return lax.dot_general(left, right, dims, preferred_element_type=F32)]
    unnamed x20 -> x3, local copies, waits for them, and re-layouts: 9.46 us -> 2.92 us
    pallas_call x2 -> x3, Pallas kernels: 169 us -> 174 us  [the longest x1 90 us: ffn(): pl.pallas_call(partial(ffn_kernel, n_wide), grid=(steps,), out_shape=(sha...]
where the time goes in v4:
time: 376 us; the launch traced here: 371 us
  Pallas kernels  356 us (95%)
  local copies, waits for them, and re-layouts  10.5 us (3%)
    pallas_call x1, Pallas kernels, front(): pl.pallas_call(front_kernel, out_shape=(shape((rows, width), BF16), shape...  119 us
    pallas_call x1, Pallas kernels, ffn(): pl.pallas_call(partial(ffn_kernel, n_wide), grid=(steps,), out_shape=(sha...  90 us
    pallas_call x1, Pallas kernels, input_backward(): pl.pallas_call(partial(input_backward_kernel, n_wide), out_shape=(back, b...  66.4 us
    pallas_call x1, Pallas kernels, attn_backward(): pl.pallas_call(partial(attn_backward_kernel, n_wide), out_shape=(shape((r...  63.1 us
    pallas_call x1, Pallas kernels, outputs(): pl.pallas_call(outputs_kernel, out_shape=(shape(w_ada.shape, F32), shape(...  17.8 us

profile of v4, /device:TPU:0, one launch (start us, length us, event | category | flops | bytes accessed | tf_op | source)
XLA Modules:
  0.0 370.8 jit_solution(18172123106650934490)
XLA Ops:
  1.3 0.7 convert_element_type.17
  2.0 0.6 broadcast_in_dim.8.silu_ref
  2.7 0.7 reshape.52
  3.4 0.6 pad.4.ktaps_src
  4.0 1.4 reshape.60.taps_ref
  5.4 2.1 copy.25
  7.5 118.9 %attn_forward.1 = (bf16[1024,768]{1,0:T(8,128)(2,1)}, bf16[4,4,64,768]{3,2,1,0:T(8,128)(2,1)}, f32[6,768]{1,0:T(8,128)}, bf16[1024,768]{1,0:T(8,128)(2,1)}, bf16...) custom-call(f32[1,1]{1,0:T(1,128)} %bitcast.1.live_ref, ...), custom_call_target="tpu_custom_call" | custom-call | tf_op jit(solution)/shard_map/attn_forward/pallas_call | solution.py:498
  126.4 1.6 slice_convert_fusion.taps_even.taps_odd
  128.0 90.0 %feed_forward.1 = (bf16[1024,768]{1,0:T(8,128)(2,1)}, f32[1024,768]{1,0:T(8,128)}, bf16[1024,768]{1,0:T(8,128)(2,1)}, f32[4,768]{1,0:T(4,128)}, bf16[3,1552,256]{2,1,0:T(8,128)(2,1)}) custom-call(f32[1,1]{1,0:T(1,128)} %bitcast.1.live_ref, bf16[1024,768]{1,0:T(8,128)(2,1)} %get-tuple-element.50.h2_ref, bf16[768,1024]{1,0:T(8,128)(2,1)} %get-tuple-element.51.h2t_ref, ...), custom_call_target="tpu_custom_call" | custom-call | tf_op jit(solution)/shard_map/feed_forward/pallas_call | solution.py:806
  218.1 63.1 %attn_backward.1 = (bf16[1024,2304]{1,0:T(8,128)(2,1)}, bf16[768,768]{1,0:T(8,128)(2,1)}, bf16[3,1536,256]{2,1,0:T(8,128)(2,1)}, f32[16,768]{1,0:T(8,128)}) custom-call(bf16[1024,768]{1,0:T(8,128)(2,1)} %get-tuple-element.61.datt_ref, bf16[1024,768]{1,0:T(8,128)(2,1)} %get-tuple-element.62.ctx_ref, bf16[1024,768]{1,0:T(8,128)(2,1)} %get-tuple-element.63.u_ref, ...), custom_call_target="tpu_custom_call" | custom-call | tf_op jit(solution)/shard_map/attn_backward/pallas_call | solution.py:1038
  281.2 0.0 copy-start
  281.2 66.4 %input_backward.1 = (bf16[4,4,64,768]{3,2,1,0:T(8,128)(2,1)}, bf16[4,4,64,768]{3,2,1,0:T(8,128)(2,1)}, bf16[2,384,768]{2,1,0:T(8,128)(2,1)}, bf16[32,16,768]{2,1,0:T(8,128)(2,1)}, f32[16,768]{1,0:T(8,128)}) custom-call(bf16[1024,768]{1,0:T(8,128)(2,1)} %get-tuple-element.49.x_ref, f32[1024,768]{1,0:T(8,128)} %get-tuple-element.60.dx1_ref, ...), custom_call_target="tpu_custom_call" | custom-call | tf_op jit(solution)/shard_map/input_backward/pallas_call | solution.py:1226
  347.6 1.4 reshape.56
  349.0 0.0 copy-done
  349.0 0.6 reshape.57
  349.7 17.8 %outputs.1 = (f32[768,4608]{1,0:T(8,128)}, f32[4,256,768]{2,1,0:T(8,128)}, bf16[4,256,768]{2,1,0:T(8,128)(2,1)}, f32[3,768,192]{2,1,0:T(8,128)}, f32[192,768]{1,...) custom-call(bf16[4,4,64,768]{3,2,1,0:T(8,128)(2,1)} %get-tuple-element.73.dx_in, ...), custom_call_target="tpu_custom_call" | custom-call | tf_op jit(solution)/shard_map/outputs/pallas_call | solution.py:1329
  367.4 2.9 copy.24
  (1 shorter events, 0.0 us)
Async XLA Ops:
  281.2 67.9 %copy-start = (f32[16,768]{1,0:T(8,128)S(1)}, f32[16,768]{1,0:T(8,128)}, u32[]{:S(2)}) copy-start(f32[16,768]{1,0:T(8,128)} %get-tuple-element.86) | copy-start | bytes 147460

commit v5 on v4

--- a/solution.py
+++ b/solution.py
@@ -99,23 +99,44 @@
 
 
 class Gather:
+    COPIES = 11
+
     def __init__(self, src, dst, sems, local_sem, first, wide, here):
         count = src.shape[0]
-        half_rows = count // 2
-        half = wide % 2
+        quarter = count // 4
+        front = -(-quarter // 32) * 16
+        mine = wide % 4
         far, near = here ^ 2, here ^ 1
 
-        def at(slot, which=None):
-            if which is None:
-                return dst.at[slot * count : (slot + 1) * count]
-            return dst.at[ds(slot * count + which * half_rows, half_rows, 16)]
-
-        self.own = pltpu.make_async_copy(src, at(0), local_sem)
-        self.near = remote(src, at(1), sems, first, wide, near)
-        self.far = remote(src.at[ds(half * half_rows, half_rows, 16)], at(2, half), sems, first + 1, wide, far)
-        self.share = remote(at(2, half), at(3, half), sems, first + 2, wide, near)
-        self.swap = remote(at(2, half), at(2, half), sems, first + 3, wide ^ 1, here)
-        self.share_swapped = remote(at(2, 1 - half), at(3, 1 - half), sems, first + 4, wide, near)
+        def slot(k):
+            return dst.at[k * count : (k + 1) * count]
+
+        def at(k, which, start=0, size=quarter):
+            return dst.at[ds(k * count + which * quarter + start, size, 16)]
+
+        def send(number, source, target, wide_to, narrow_to):
+            return remote(source, target, sems, first + number, wide_to, narrow_to)
+
+        def same(number, which, wide_to, start=0, size=quarter):
+            return send(number, at(2, which, start, size), at(2, which, start, size), wide_to, here)
+
+        def share(number, which, start=0, size=quarter):
+            return send(number, at(2, which, start, size), at(3, which, start, size), wide, near)
+
+        own_part = src.at[ds(mine * quarter, quarter, 16)]
+        rest = quarter - front
+        self.own = pltpu.make_async_copy(src, slot(0), local_sem)
+        self.near = send(0, src, slot(1), wide, near)
+        self.far = send(1, own_part, at(2, mine), wide, far)
+        self.swaps = [same(2, mine, wide ^ 1), same(3, mine, wide ^ 2)]
+        self.corners = [same(4, mine ^ 1, wide ^ 2, 0, front), same(5, mine ^ 2, wide ^ 1, front, rest)]
+        self.shares = [
+            share(6, mine),
+            share(7, mine ^ 1),
+            share(8, mine ^ 2),
+            share(9, mine ^ 3, 0, front),
+            share(10, mine ^ 3, front, rest),
+        ]
 
     def start_near(self):
         self.own.start()
@@ -124,22 +145,31 @@
     def start_far(self):
         self.far.start()
 
-    def forward(self):
+    def swap(self):
         self.far.wait_recv()
-        self.swap.start()
-        self.share.start()
-
-    def forward_swapped(self):
-        self.swap.wait_recv()
-        self.share_swapped.start()
+        self.swaps[0].start()
+        self.swaps[1].start()
+        self.shares[0].start()
+
+    def corner(self):
+        for which in range(2):
+            self.swaps[which].wait_recv()
+            self.corners[which].start()
+            self.shares[1 + which].start()
+
+    def share_corner(self):
+        for which in range(2):
+            self.corners[which].wait_recv()
+            self.shares[3 + which].start()
 
     def finish(self):
         self.own.wait()
         self.near.wait()
         self.far.wait_send()
-        self.swap.wait_send()
-        self.share.wait()
-        self.share_swapped.wait()
+        for copy in self.swaps + self.corners:
+            copy.wait_send()
+        for copy in self.shares:
+            copy.wait()
 
 
 def group_permutation(rows):
@@ -306,7 +336,7 @@
     live_ref, silu_ref, taps_ref, tokens_hbm, cot_hbm, ada_hbm, wqkv_src, wout_src, wup_src, wdown_src, ktaps_src,
     x_ref, cot_ref, mod_ref, u_ref, qkv_ref, probs_ref, ctx_ref, att_ref, x1_ref, h2_ref, h2t_ref, db_ref,
     wqkv_ref, wout_ref, wup_ref, wdown_ref, ktaps_ref,
-    base, shifted, shards, sent, sent_cot, got, ada, sems, local_sems, in_sems,
+    base, shifted, shards, sent, sent_cot, got, ada, up_own, down_own, sems, local_sems, in_sems,
 ):
     width = u_ref.shape[1]
     rows_all = u_ref.shape[0]
@@ -316,9 +346,13 @@
     load_tokens.start()
     load_ada = pltpu.make_async_copy(ada_hbm, ada, in_sems.at[1])
     load_ada.start()
+    load_up = pltpu.make_async_copy(wup_src, up_own, in_sems.at[2])
+    load_up.start()
+    load_down = pltpu.make_async_copy(wdown_src, down_own, in_sems.at[3])
+    load_down.start()
 
     barrier = pltpu.get_barrier_semaphore()
-    partners = [(wide, peer) for peer in narrow_peers(here)] + [(wide ^ 1, here)]
+    partners = [(wide, peer) for peer in narrow_peers(here)] + [(wide ^ 1, here), (wide ^ 2, here)]
     for partner in partners:
         pl.semaphore_signal(
             barrier, inc=1, device_id=partner, device_id_type=pl.DeviceIdType.MESH
@@ -340,23 +374,32 @@
     exchange = Exchange(sent, got, sems, local_sems.at[0], 0, wide, here)
     exchange_cot = Exchange(sent_cot, cot_ref, sems, local_sems.at[1], 3, wide, here)
     gathers = [
-        Gather(src, dst, sems, local_sems.at[2 + at], 6 + 5 * at, wide, here)
+        Gather(src, dst, sems, local_sems.at[2 + at], 9 + Gather.COPIES * at, wide, here)
         for at, (src, dst) in enumerate(
             (
                 (wqkv_src, wqkv_ref),
                 (wout_src, wout_ref),
-                (wup_src, wup_ref),
-                (wdown_src, wdown_ref),
-                (ktaps_src, ktaps_ref),
+                (up_own, wup_ref),
+                (down_own, wdown_ref),
             )
         )
     ]
-    g_qkv, g_out, g_up, g_down, g_taps = gathers
+    g_qkv, g_out, g_up, g_down = gathers
+    taps_own = pltpu.make_async_copy(ktaps_src, ktaps_ref.at[0], local_sems.at[6])
+    taps_sends = [
+        remote(ktaps_src, ktaps_ref.at[peer ^ here], sems, 6 + at, wide, peer)
+        for at, peer in enumerate(narrow_peers(here))
+    ]
     exchange.start()
     load_cot = pltpu.make_async_copy(cot_hbm, shards, in_sems.at[0])
     load_cot.start()
+    load_up.wait()
+    load_down.wait()
     for one in gathers:
         one.start_near()
+    taps_own.start()
+    for one in taps_sends:
+        one.start()
 
     load_ada.wait()
     for part in range(6):
@@ -385,6 +428,9 @@
         return carry
 
     lax.fori_loop(0, rows_all // ROWS, norm_step, 0)
+    g_qkv.swap()
+    g_out.swap()
+    g_up.start_far()
 
     def conv_step(block, carry):
         lanes = ds(block * LANES, LANES)
@@ -403,13 +449,14 @@
 
         return lax.fori_loop(0, PHASE // ROWS, rows_step, carry)
 
-    lax.fori_loop(0, width // LANES, conv_step, 0)
-    g_qkv.forward()
-    g_out.forward()
-    g_up.start_far()
-    g_taps.start_far()
-    g_qkv.forward_swapped()
-    g_out.forward_swapped()
+    blocks = width // LANES
+    lax.fori_loop(0, 2 * blocks // 3, conv_step, 0)
+    g_qkv.corner()
+    g_out.corner()
+    g_up.swap()
+    exchange_cot.start()
+    lax.fori_loop(2 * blocks // 3, blocks, conv_step, 0)
+    g_qkv.share_corner()
     g_qkv.finish()
 
     def project_step(step, carry):
@@ -443,15 +490,14 @@
         ctx_ref[rows, ds(pair * LANES, LANES)] = jnp.where(first, found[0], found[1]).astype(BF16)
         return carry
 
+    g_up.corner()
+    g_out.share_corner()
     lax.fori_loop(0, pairs, attend_step, 0)
-    g_up.forward()
-    g_taps.forward()
-    exchange_cot.start()
-    lax.fori_loop(pairs, 3 * pairs, attend_step, 0)
-    g_up.forward_swapped()
-    g_taps.forward_swapped()
+    g_up.share_corner()
     exchange_cot.wait()
     g_down.start_far()
+    lax.fori_loop(pairs, 3 * pairs, attend_step, 0)
+    g_down.swap()
     lax.fori_loop(3 * pairs, 4 * pairs, attend_step, 0)
     g_out.finish()
 
@@ -473,15 +519,18 @@
         db_ref[rows, :] = (cot_ref[group, source].astype(F32) * live * gate_two).astype(BF16)
         return carry
 
+    g_down.corner()
     lax.fori_loop(0, rows_all // ROWS, second_step, 0)
-    g_down.forward()
+    g_down.share_corner()
     for part in range(4):
         h2t_ref[:, part * PHASE : (part + 1) * PHASE] = h2_ref[
             part * PHASE : (part + 1) * PHASE, :
         ].T
-    g_down.forward_swapped()
-    for one in (g_up, g_taps, g_down):
-        one.finish()
+    g_up.finish()
+    g_down.finish()
+    taps_own.wait()
+    for one in taps_sends:
+        one.wait()
 
 
 def whole(memory=pltpu.VMEM):
@@ -514,10 +563,10 @@
             full(wout),
             full(wup),
             full(wdown),
-            full(ktaps),
+            shape((latents,) + ktaps.shape, BF16),
         ),
-        in_specs=[whole(pltpu.SMEM)] + [whole()] * 2 + [whole(pl.ANY)] * 8,
-        out_specs=(whole(),) * 14 + (whole(pl.ANY),) * 3,
+        in_specs=[whole(pltpu.SMEM)] + [whole()] * 2 + [whole(pl.ANY)] * 3 + [whole()] * 2 + [whole(pl.ANY)] * 2 + [whole()],
+        out_specs=(whole(),) * 14 + (whole(pl.ANY),) * 2 + (whole(),),
         scratch_shapes=[
             pltpu.VMEM((4, PAD, width), F32),
             pltpu.VMEM((4, PAD, width), F32),
@@ -526,9 +575,11 @@
             pltpu.VMEM(moved, BF16),
             pltpu.VMEM((4, latents, shard_rows // 4, width), BF16),
             pltpu.VMEM(w_ada.shape, BF16),
-            pltpu.SemaphoreType.DMA((2, 6 + 5 * 5)),
+            pltpu.VMEM(wup.shape, BF16),
+            pltpu.VMEM(wdown.shape, BF16),
+            pltpu.SemaphoreType.DMA((2, 9 + 4 * Gather.COPIES)),
             pltpu.SemaphoreType.DMA((7,)),
-            pltpu.SemaphoreType.DMA((2,)),
+            pltpu.SemaphoreType.DMA((4,)),
         ],
         compiler_params=pltpu.CompilerParams(
             vmem_limit_bytes=60 * MIB, collective_id=0, has_side_effects=True
@@ -872,6 +923,7 @@
     pairs = width // LANES
     half_pairs = pairs // 2
     steps = 4 * pairs
+    slots = weights.shape[0]
     load_qkv = pltpu.make_async_copy(qkv_hbm, dqkv_ref, in_sems.at[2])
     load_qkv.start()
 
@@ -904,7 +956,7 @@
                     act()
 
     def taps_copy(level):
-        return remote(taps_sum.at[level], taps_got.at[level], sems, 3 + level, wide ^ (1 << level), here)
+        return remote(taps_sum.at[level], taps_got.at[level], sems, 6 + level, wide ^ (1 << level), here)
 
     def taps_add(level):
         taps_copy(level).wait_recv()
@@ -971,35 +1023,62 @@
 
         lax.fori_loop(begin, end, body, 0)
 
+    slab = width // slots
+
     def weight_grads(half):
         span = width // 2
-        slab = span // 2
-        for part in range(4):
-            cols = slice(half * span, (half + 1) * span)
-            if part < 3:
-                left = dqkv_ref[:, part * width + half * span : part * width + (half + 1) * span]
-                found = mm(left, u_ref[...], TN).astype(BF16)
-            else:
-                found = mm(ctx_ref[:, cols], datt_ref[...], TN).astype(BF16)
+        for part in range(3):
+            left = dqkv_ref[:, part * width + half * span : part * width + (half + 1) * span]
+            found = mm(left, u_ref[...], TN).astype(BF16)
             for one in range(2):
                 weights[2 * half + one, part * slab : (part + 1) * slab, :] = found[
                     one * slab : (one + 1) * slab
                 ]
 
-    near_early = remote(weights.at[3], got_near.at[0], sems, 0, wide, here ^ 1)
-    near_late = remote(weights.at[1], got_near.at[1], sems, 1, wide, here ^ 1)
-    far = remote(chip_sum, got_far, sems, 2, wide, here ^ 2)
+    head, tail = slice(3 * slab), slice(3 * slab, 4 * slab)
+
+    def near_copy(early, rows, at):
+        return remote(
+            weights.at[3 if early else 1, rows], got_near.at[0 if early else 1, rows], sems, at, wide, here ^ 1
+        )
+
+    def far_copy(rows, at):
+        return remote(chip_sum.at[rows], got_far.at[rows], sems, at, wide, here ^ 2)
+
+    def add_chip(rows):
+        chip_sum[rows, :] = (weights[2, rows, :].astype(F32) + got_near[0, rows, :].astype(F32)).astype(BF16)
+
+    near_out, near_early = near_copy(True, tail, 0), near_copy(True, head, 1)
+    late_out, near_late = near_copy(False, tail, 2), near_copy(False, head, 3)
+    far_out, far = far_copy(tail, 4), far_copy(head, 5)
+
+    for part in range(width // PHASE):
+        cols = slice(part * PHASE, (part + 1) * PHASE)
+        found = mm(ctx_ref[:, cols], datt_ref[...], TN).astype(BF16)
+        for slot in range(slots):
+            low, high = max(part * PHASE, slot * slab), min((part + 1) * PHASE, (slot + 1) * slab)
+            if low < high:
+                weights[slot, 3 * slab + low - slot * slab : 3 * slab + high - slot * slab, :] = found[
+                    low - part * PHASE : high - part * PHASE
+                ]
+    near_out.start()
+    late_out.start()
+
+    def send_out():
+        near_out.wait_recv()
+        add_chip(tail)
+        far_out.start()
 
     later = lambda *which: partial(advance, *which)
     attend_loop(
         0, steps // 2,
-        [(2, later(2, 0)), (5, later(1)), (7, partial(taps_add, 0)), (8, later(2, 0)), (11, later(1))],
+        [(1, send_out), (2, later(2, 0)), (5, later(1)), (7, partial(taps_add, 0)), (8, later(2, 0)), (11, later(1))],
     )
     weight_grads(1)
     near_early.start()
     advance(2)
     near_early.wait_recv()
-    chip_sum[...] = (weights[2].astype(F32) + got_near[0].astype(F32)).astype(BF16)
+    add_chip(head)
     far.start()
     attend_loop(
         steps // 2, steps,
@@ -1011,8 +1090,10 @@
         taps_add(level)
     gtaps_ref[...] = taps_sum[levels]
     near_late.wait_recv()
+    late_out.wait_recv()
     while any(queues):
         advance(0, 1, 2)
+    far_out.wait_recv()
     far.wait_recv()
     own_ref[...] = (
         weights[0].astype(F32) + got_near[1].astype(F32) + got_far[...].astype(F32)
@@ -1021,9 +1102,8 @@
         one.wait_sends()
     for level in range(levels):
         taps_copy(level).wait_send()
-    near_early.wait_send()
-    near_late.wait_send()
-    far.wait_send()
+    for copy in (near_out, near_early, late_out, near_late, far_out, far):
+        copy.wait_send()
 
 
 def attn_backward(n_wide, datt, ctx, u, wout, parcels, qkv, probs):
@@ -1056,7 +1136,7 @@
             pltpu.VMEM((pieces, sum_landing(sum_rows, n_wide), CHUNK), BF16),
             pltpu.VMEM((levels + 1, 16, pieces * CHUNK), F32),
             pltpu.VMEM((levels, 16, pieces * CHUNK), F32),
-            pltpu.SemaphoreType.DMA((2, 3 + levels)),
+            pltpu.SemaphoreType.DMA((2, 6 + levels)),
             pltpu.SemaphoreType.DMA((3,)),
             pltpu.SemaphoreType.DMA((2, pieces * per_sum)),
         ],
@@ -1150,9 +1230,8 @@
     back = Return(dx, got_dx, sems, local_sems.at[0], 0, wide, here)
 
     def rows_step(at, sums):
-        source = (at // 4 + 2) % 4 ^ here
-        group = at % 4
-        span = ds(group * PHASE + source * ROWS, ROWS)
+        group, source = at // 4, at % 4
+        span = ds(at * ROWS, ROWS)
         unit, inv = normed(x_ref[span, :].astype(F32))
         grad = dh1[span, :]
         dx[group, source] = (
@@ -1160,56 +1239,55 @@
         ).astype(BF16)
         return tuple(total + fold(one) for total, one in zip(sums, (grad, grad * unit)))
 
+    partners = [(wide, here ^ 2)] + wide_partners(wide, here, n_wide)[::-1] + [(wide, here ^ 1)]
+    levels = len(partners)
+    tap_sums[0, :9, :] = dtaps_ref[:9, :]
+    tap_sums[0, 9:, :] = jnp.zeros((7, width), F32)
+
+    def taps_copy(level):
+        return remote(tap_sums.at[level], tap_got.at[level], small_sems, 2 * level + 1, *partners[level])
+
+    def taps_step(level):
+        taps_copy(level).wait_recv()
+        tap_sums[level + 1] = tap_sums[level] + tap_got[level]
+        if level + 1 < levels:
+            taps_copy(level + 1).start()
+
+    taps_copy(0).start()
     found = tuple(jnp.zeros((8, width), F32) for _ in range(2))
-    for at in range(4):
-        found = lax.fori_loop(4 * at, 4 * at + 4, rows_step, found)
-        if at < 2:
-            back.copies[at].start()
-        elif at == 3:
-            back.copies[2].start()
-    back.own.start()
+    for at in range(2):
+        found = lax.fori_loop(8 * at, 8 * at + 8, rows_step, found)
+        taps_step(at)
     dmod = [jnp.sum(one, axis=0, keepdims=True) for one in found]
     dmod += [dmod_ref[at : at + 1, :] for at in range(4)]
 
-    partners = wide_partners(wide, here, n_wide)[::-1] + [(wide, here ^ 2), (wide, here ^ 1)]
-    levels = len(partners)
     stack = jnp.concatenate([silu_ref[0:1, :].astype(F32)] + dmod + [jnp.zeros((SMALL - 7, width), F32)])
     small[0] = stack.astype(BF16)
-    tap_sums[0, :9, :] = dtaps_ref[:9, :]
-    tap_sums[0, 9:, :] = jnp.zeros((7, width), F32)
-
-    def small_copies(level):
+
+    def small_copy(level):
         have = 1 << level
-        return (
-            remote(small.at[:have], small.at[have : 2 * have], small_sems, 2 * level, *partners[level]),
-            remote(tap_sums.at[level], tap_got.at[level], small_sems, 2 * level + 1, *partners[level]),
-        )
-
-    def small_start(level):
-        for copy in small_copies(level):
-            copy.start()
-
-    def small_finish(level):
-        for copy in small_copies(level):
-            copy.wait_recv()
-        tap_sums[level + 1] = tap_sums[level] + tap_got[level]
-
-    small_start(0)
+        return remote(small.at[:have], small.at[have : 2 * have], small_sems, 2 * level, *partners[level])
+
+    small_copy(0).start()
+    for copy in back.copies:
+        copy.start()
+    back.own.start()
     advance(0, 1)
     for level in range(levels):
-        small_finish(level)
+        small_copy(level).wait_recv()
         if level + 1 < levels:
-            small_start(level + 1)
-        if level == 1:
-            advance(0, 1)
+            small_copy(level + 1).start()
+        if level >= 2:
+            taps_step(level)
+        advance(0, 1)
     dtaps_ref[...] = tap_sums[levels]
     while any(queues):
         advance(0, 1)
     block_back.wait()
     back.wait()
     for level in range(levels):
-        for copy in small_copies(level):
-            copy.wait_send()
+        small_copy(level).wait_send()
+        taps_copy(level).wait_send()
     for one in sums:
         one.wait_sends()
 
@@ -1302,7 +1380,7 @@
 
     def own_column(row, part):
         away = row ^ here
-        place = ((away // 2) % 2) * (devices // 4) + (away % 2) * (devices // 2)
+        place = ((away // 2) % 2) + (away % 2) * (devices // 2)
         return jnp.where(row < cond_ref.shape[0], place * SMALL + 1 + part, -1)
 
     load_ada.wait()
@@ -1367,7 +1445,7 @@
 
     n_wide = lax.axis_size("wide")
     qkv_t = w_qkv.transpose(2, 1, 0).reshape(w_qkv.shape[2], 3 * width)
-    ktaps_own = jnp.pad(k_ffn.reshape(9, local), ((0, 23), (0, 0)))
+    ktaps_own = jnp.pad(k_ffn.reshape(9, local), ((0, 7), (0, 0)))
     attn_taps = k_attn.reshape(9, width).astype(F32)
 
     cond_f = condition.astype(F32)
@@ -1379,7 +1457,7 @@
         live, own_silu, attn_taps, tokens, cotangent, w_ada, qkv_t, w_out, w_up, w_down, ktaps_own
     )
     cot = cot.reshape(rows_all, width)
-    ffn_taps = ktaps.reshape(lat_dev, -1, local)[:, :9].astype(F32)
+    ffn_taps = ktaps[:, :9].astype(F32)
     block_g, dx1, datt, dmod_mid, parcels = ffn(
         n_wide, live, h2, h2t, db, x1, cot, att, mod, wup, wdown, ffn_taps
     )

time: 376 us -> 350 us (0.931)
  Pallas kernels: 356 us -> 331 us
    pallas_call x1, Pallas kernels: 119 us -> 97.1 us  [front(): pl.pallas_call(front_kernel, out_shape=(shape((rows, width), BF16), shape...]
    pallas_call x1, Pallas kernels: 63.1 us -> 56 us  [attn_backward(): pl.pallas_call(partial(attn_backward_kernel, n_wide), out_shape=(shape((r...]
    pallas_call x1, Pallas kernels: 66.4 us -> 71.2 us  [input_backward(): pl.pallas_call(partial(input_backward_kernel, n_wide), out_shape=(back, b...]
where the time goes in v5:
time: 350 us; the launch traced here: 345 us
  Pallas kernels  331 us (95%)
  local copies, waits for them, and re-layouts  10.5 us (3%)
    pallas_call x1, Pallas kernels, front(): pl.pallas_call(front_kernel, out_shape=(shape((rows, width), BF16), shape...  97.1 us
    pallas_call x1, Pallas kernels, ffn(): pl.pallas_call(partial(ffn_kernel, n_wide), grid=(steps,), out_shape=(sha...  88.5 us
    pallas_call x1, Pallas kernels, input_backward(): pl.pallas_call(partial(input_backward_kernel, n_wide), out_shape=(back, b...  71.2 us
    pallas_call x1, Pallas kernels, attn_backward(): pl.pallas_call(partial(attn_backward_kernel, n_wide), out_shape=(shape((r...  56 us
    pallas_call x1, Pallas kernels, outputs(): pl.pallas_call(outputs_kernel, out_shape=(shape(w_ada.shape, F32), shape(...  17.8 us

profile of v5, /device:TPU:0, one launch (start us, length us, event | category | flops | bytes accessed | tf_op | source)
XLA Modules:
  0.0 345.1 jit_solution(10579972242120269063)
XLA Ops:
  1.3 0.7 convert_element_type.17
  2.0 0.6 broadcast_in_dim.8.silu_ref
  2.7 0.7 reshape.49
  3.4 0.6 pad.4.ktaps_src
  4.0 1.4 reshape.56.taps_ref
  5.4 2.1 copy.25
  7.5 97.1 %attn_forward.1 = (bf16[1024,768]{1,0:T(8,128)(2,1)}, bf16[4,4,64,768]{3,2,1,0:T(8,128)(2,1)}, f32[6,768]{1,0:T(8,128)}, bf16[1024,768]{1,0:T(8,128)(2,1)}, bf16...) custom-call(f32[1,1]{1,0:T(1,128)} %bitcast.1.live_ref, ...), custom_call_target="tpu_custom_call" | custom-call | tf_op jit(solution)/shard_map/attn_forward/pallas_call | solution.py:547
  104.7 1.6 slice_convert_fusion.taps_even.taps_odd
  106.2 88.5 %feed_forward.1 = (bf16[1024,768]{1,0:T(8,128)(2,1)}, f32[1024,768]{1,0:T(8,128)}, bf16[1024,768]{1,0:T(8,128)(2,1)}, f32[4,768]{1,0:T(4,128)}, bf16[3,1552,256]{2,1,0:T(8,128)(2,1)}) custom-call(f32[1,1]{1,0:T(1,128)} %bitcast.1.live_ref, bf16[1024,768]{1,0:T(8,128)(2,1)} %get-tuple-element.50.h2_ref, bf16[768,1024]{1,0:T(8,128)(2,1)} %get-tuple-element.51.h2t_ref, ...), custom_call_target="tpu_custom_call" | custom-call | tf_op jit(solution)/shard_map/feed_forward/pallas_call | solution.py:857
  194.7 56.0 %attn_backward.1 = (bf16[1024,2304]{1,0:T(8,128)(2,1)}, bf16[768,768]{1,0:T(8,128)(2,1)}, bf16[3,1536,256]{2,1,0:T(8,128)(2,1)}, f32[16,768]{1,0:T(8,128)}) custom-call(bf16[1024,768]{1,0:T(8,128)(2,1)} %get-tuple-element.61.datt_ref, bf16[1024,768]{1,0:T(8,128)(2,1)} %get-tuple-element.62.ctx_ref, bf16[1024,768]{1,0:T(8,128)(2,1)} %get-tuple-element.63.u_ref, ...), custom_call_target="tpu_custom_call" | custom-call | tf_op jit(solution)/shard_map/attn_backward/pallas_call | solution.py:1118
  250.7 0.0 copy-start
  250.7 71.2 %input_backward.1 = (bf16[4,4,64,768]{3,2,1,0:T(8,128)(2,1)}, bf16[4,4,64,768]{3,2,1,0:T(8,128)(2,1)}, bf16[2,384,768]{2,1,0:T(8,128)(2,1)}, bf16[32,16,768]{2,1,0:T(8,128)(2,1)}, f32[16,768]{1,0:T(8,128)}) custom-call(bf16[1024,768]{1,0:T(8,128)(2,1)} %get-tuple-element.49.x_ref, f32[1024,768]{1,0:T(8,128)} %get-tuple-element.60.dx1_ref, ...), custom_call_target="tpu_custom_call" | custom-call | tf_op jit(solution)/shard_map/input_backward/pallas_call | solution.py:1304
  321.9 1.4 reshape.52
  323.3 0.0 copy-done
  323.3 0.6 reshape.53
  324.0 17.8 %outputs.1 = (f32[768,4608]{1,0:T(8,128)}, f32[4,256,768]{2,1,0:T(8,128)}, bf16[4,256,768]{2,1,0:T(8,128)(2,1)}, f32[3,768,192]{2,1,0:T(8,128)}, f32[192,768]{1,...) custom-call(bf16[4,4,64,768]{3,2,1,0:T(8,128)(2,1)} %get-tuple-element.73.dx_in, ...), custom_call_target="tpu_custom_call" | custom-call | tf_op jit(solution)/shard_map/outputs/pallas_call | solution.py:1407
  341.7 2.9 copy.24
  (1 shorter events, 0.0 us)
Async XLA Ops:
  250.7 72.6 %copy-start = (f32[16,768]{1,0:T(8,128)S(1)}, f32[16,768]{1,0:T(8,128)}, u32[]{:S(2)}) copy-start(f32[16,768]{1,0:T(8,128)} %get-tuple-element.86) | copy-start | bytes 147460

commit v6 on v5

--- a/solution.py
+++ b/solution.py
@@ -217,7 +217,7 @@
 
 
 class WideSum:
-    def __init__(self, source, work, full, got, sems, first, wide, here, n_wide, done=0):
+    def __init__(self, source, work, full, got, sems, first, wide, here, n_wide, done=0, order=None):
         self.source, self.work, self.full, self.got = source, work, full, got
         self.rows = work.shape[0]
         self.levels = min(HALVINGS, n_wide.bit_length() - 1)
@@ -225,8 +225,9 @@
         self.done = done
         self.wide, self.here, self.sems, self.first = wide, here, sems, first
         self.offsets = [0]
+        self.masks = [1 << at for at in (order or range(HALVINGS)) if at < self.levels]
         for level in range(self.levels):
-            bit = (wide // 2**level) % 2
+            bit = (wide // self.masks[level]) % 2
             self.offsets.append(self.offsets[-1] + bit * (self.rows >> (level + 1)))
         self.waiting = []
 
@@ -243,7 +244,7 @@
         landing = self.rows - self.size(level)
         return remote(
             self.at(source, send, size), self.got.at[landing : landing + size],
-            self.sems, self.first + level, self.wide ^ (1 << level), self.here,
+            self.sems, self.first + level, self.wide ^ self.masks[level], self.here,
         )
 
     def start_half(self, level):
@@ -279,7 +280,7 @@
     def spread_copy(self, level):
         part = self.at(self.full, self.offsets[level + 1], self.size(level + 1))
         return remote(
-            part, part, self.sems, self.first + self.levels + level, self.wide ^ (1 << level), self.here
+            part, part, self.sems, self.first + self.levels + level, self.wide ^ self.masks[level], self.here
         )
 
     def actions(self):
@@ -334,11 +335,19 @@
 
 def front_kernel(
     live_ref, silu_ref, taps_ref, tokens_hbm, cot_hbm, ada_hbm, wqkv_src, wout_src, wup_src, wdown_src, ktaps_src,
-    x_ref, cot_ref, mod_ref, u_ref, qkv_ref, probs_ref, ctx_ref, att_ref, x1_ref, h2_ref, h2t_ref, db_ref,
-    wqkv_ref, wout_ref, wup_ref, wdown_ref, ktaps_ref,
-    base, shifted, shards, sent, sent_cot, got, ada, up_own, down_own, sems, local_sems, in_sems,
+    x_hbm, cot_hbm_out, u_hbm, qkv_hbm, probs_hbm, ctx_hbm, wqkv_hbm, wout_hbm,
+    mod_ref, att_ref, x1_ref, h2_ref, h2t_ref, db_ref, wup_ref, wdown_ref, ktaps_ref,
+    x_ref, cot_ref, u_ref, qkv_ref, probs_ref, ctx_ref, wqkv_ref, wout_ref,
+    base, shifted, shards, sent, sent_cot, got, ada, up_own, down_own, sems, local_sems, in_sems, out_sems,
 ):
     width = u_ref.shape[1]
+    flushed = []
+
+    def flush(src, dst):
+        copy = pltpu.make_async_copy(src, dst, out_sems.at[len(flushed)])
+        copy.start()
+        flushed.append(copy)
+
     rows_all = u_ref.shape[0]
     latents, shard_rows = shards.shape[:2]
     wide, here = lax.axis_index("wide"), lax.axis_index("narrow")
@@ -419,6 +428,7 @@
         for source in range(latents):
             start = group * PHASE + source * ROWS
             x_ref[start : start + ROWS, :] = got[group, source]
+    flush(x_ref, x_hbm)
 
     def norm_step(step, carry):
         group, part = step // (PHASE // ROWS), step % (PHASE // ROWS)
@@ -456,8 +466,10 @@
     g_up.swap()
     exchange_cot.start()
     lax.fori_loop(2 * blocks // 3, blocks, conv_step, 0)
+    flush(u_ref, u_hbm)
     g_qkv.share_corner()
     g_qkv.finish()
+    flush(wqkv_ref, wqkv_hbm)
 
     def project_step(step, carry):
         rows = ds(step * PHASE, PHASE)
@@ -490,16 +502,27 @@
         ctx_ref[rows, ds(pair * LANES, LANES)] = jnp.where(first, found[0], found[1]).astype(BF16)
         return carry
 
+    flush(qkv_ref, qkv_hbm)
     g_up.corner()
     g_out.share_corner()
-    lax.fori_loop(0, pairs, attend_step, 0)
+
+    def attend_group(group):
+        lax.fori_loop(group * pairs, (group + 1) * pairs, attend_step, 0)
+        done = slice(group * pairs, (group + 1) * pairs)
+        flush(probs_ref.at[done], probs_hbm.at[done])
+
+    attend_group(0)
     g_up.share_corner()
     exchange_cot.wait()
+    flush(cot_ref, cot_hbm_out)
     g_down.start_far()
-    lax.fori_loop(pairs, 3 * pairs, attend_step, 0)
+    attend_group(1)
+    attend_group(2)
     g_down.swap()
-    lax.fori_loop(3 * pairs, 4 * pairs, attend_step, 0)
+    attend_group(3)
+    flush(ctx_ref, ctx_hbm)
     g_out.finish()
+    flush(wout_ref, wout_hbm)
 
     def out_step(step, carry):
         rows = ds(step * PHASE, PHASE)
@@ -528,6 +551,8 @@
         ].T
     g_up.finish()
     g_down.finish()
+    for copy in flushed:
+        copy.wait()
     taps_own.wait()
     for one in taps_sends:
         one.wait()
@@ -544,30 +569,34 @@
     shape = jax.ShapeDtypeStruct
     full = lambda shard: shape((latents * shard.shape[0],) + shard.shape[1:], BF16)
     moved = (latents, 4, shard_rows // 4, width)
+    streamed = (
+        shape((rows, width), BF16),
+        shape((4, latents, shard_rows // 4, width), BF16),
+        shape((rows, width), BF16),
+        shape((rows, 3 * width), BF16),
+        shape((steps, PHASE, 2 * PHASE), BF16),
+        shape((rows, width), BF16),
+        full(wqkv),
+        full(wout),
+    )
     return pl.pallas_call(
         front_kernel,
-        out_shape=(
-            shape((rows, width), BF16),
-            shape((4, latents, shard_rows // 4, width), BF16),
+        out_shape=streamed
+        + (
             shape((6, width), F32),
-            shape((rows, width), BF16),
-            shape((rows, 3 * width), BF16),
-            shape((steps, PHASE, 2 * PHASE), BF16),
-            shape((rows, width), BF16),
             shape((rows, width), BF16),
             shape((rows, width), F32),
             shape((rows, width), BF16),
             shape((width, rows), BF16),
             shape((rows, width), BF16),
-            full(wqkv),
-            full(wout),
             full(wup),
             full(wdown),
             shape((latents,) + ktaps.shape, BF16),
         ),
         in_specs=[whole(pltpu.SMEM)] + [whole()] * 2 + [whole(pl.ANY)] * 3 + [whole()] * 2 + [whole(pl.ANY)] * 2 + [whole()],
-        out_specs=(whole(),) * 14 + (whole(pl.ANY),) * 2 + (whole(),),
-        scratch_shapes=[
+        out_specs=(whole(pl.ANY),) * 8 + (whole(),) * 6 + (whole(pl.ANY),) * 2 + (whole(),),
+        scratch_shapes=[pltpu.VMEM(one.shape, one.dtype) for one in streamed]
+        + [
             pltpu.VMEM((4, PAD, width), F32),
             pltpu.VMEM((4, PAD, width), F32),
             pltpu.VMEM((latents, shard_rows, width), BF16),
@@ -580,6 +609,7 @@
             pltpu.SemaphoreType.DMA((2, 9 + 4 * Gather.COPIES)),
             pltpu.SemaphoreType.DMA((7,)),
             pltpu.SemaphoreType.DMA((4,)),
+            pltpu.SemaphoreType.DMA((len(streamed) + 3,)),
         ],
         compiler_params=pltpu.CompilerParams(
             vmem_limit_bytes=60 * MIB, collective_id=0, has_side_effects=True
@@ -589,13 +619,17 @@
 
 
 def ffn_kernel(
-    n_wide, live_ref, h2_ref, h2t_ref, db_ref, x1_ref, cot_ref, att_ref, mod_ref,
+    n_wide, live_ref, h2_ref, h2t_ref, db_ref, x1_hbm, cot_hbm, att_hbm, mod_ref,
     wup_before, wup_even, wup_odd, wup_after, wdown_even, wdown_odd, taps_even, taps_odd,
     block_ref, dx1_ref, datt_ref, dmod_ref, sums_ref,
     hid_even, hid_odd, hid_moved, grad, grad_moved, slope, act, act_t, dhid, branch, dtaps,
-    work, chip_sum, got_near, got_far, got_sums, sems, sum_sems,
+    work, chip_sum, got_near, got_far, got_sums, x1_ref, cot_ref, att_ref, sems, sum_sems, in_sems,
 ):
     rows_all, width = h2_ref.shape
+    loads = [
+        pltpu.make_async_copy(src, dst, in_sems.at[at])
+        for at, (src, dst) in enumerate(((x1_hbm, x1_ref), (cot_hbm, cot_ref), (att_hbm, att_ref)))
+    ]
     dh2 = dx1_ref
     wide, here = lax.axis_index("wide"), lax.axis_index("narrow")
     step, steps = pl.program_id(0), pl.num_programs(0)
@@ -621,6 +655,8 @@
 
     @pl.when(step == 0)
     def _():
+        for load in loads:
+            load.start()
         barrier = pltpu.get_barrier_semaphore()
         for partner in partners:
             pl.semaphore_signal(
@@ -654,6 +690,29 @@
         if q < width // PHASE:
             slot[quarters[q], :] = mm(h2t_ref[quarters[q], :], dhid[...], NN).astype(BF16)
 
+    def forward_products(part, wdown, wup_last, slot):
+        grad[part, inside, :] = mm(db_ref[quarters[part], :], wdown[...], NT)
+        yield
+        for cols in quarters[: width // PHASE]:
+            dh2[quarters[part], cols] += mm(dhid[quarters[part], :], wup_last[cols, :], NT)
+            yield
+        if part < width // PHASE:
+            slot[quarters[part], :] = mm(h2t_ref[quarters[part], :], dhid[...], NN).astype(BF16)
+        yield
+
+    def backward_products(part, hid_next, wdown, wup_next, slot):
+        hid_next[part, inside, :] = mm(h2_ref[quarters[part], :], wup_next[...], NN)
+        yield
+        for cols in quarters[: width // PHASE]:
+            branch[quarters[part], cols] += mm(act[quarters[part], :], wdown[:, cols], NN)
+            yield
+        if part < width // CHUNK:
+            block = slice(part * CHUNK, (part + 1) * CHUNK)
+            slot[width + part * CHUNK : width + (part + 1) * CHUNK, :] = mm(
+                act_t[...], db_ref[:, block], NN
+            ).astype(BF16)
+        yield
+
     def forward(hid, wdown, taps_ref, wup_last, slot):
         taps = [[taps_ref[0, t : t + 1, lanes] for t in range(9)] for lanes in lane_blocks]
         for part in range(PHASE // ROWS):
@@ -662,10 +721,10 @@
                 for lanes in lane_blocks:
                     hid_moved[group, rows, lanes] = moved_cols(group, hid[group, rows, lanes])
         for part in range(PHASE // ROWS):
-            grad[part, inside, :] = mm(db_ref[quarters[part], :], wdown[...], NT)
-            weights_back(part, wup_last, slot)
+            products = forward_products(part, wdown, wup_last, slot)
             for group in range(4):
                 for at, lanes in enumerate(lane_blocks):
+                    next(products, None)
                     total = jnp.zeros((ROWS, LANES), F32)
                     for tap in range(9):
                         total += taps[at][tap] * static_tap(
@@ -694,16 +753,11 @@
                     grad_moved[group, rows, lanes] = moved_cols(group, value)
         sums = [[jnp.zeros((8, LANES), F32) for _ in range(9)] for _ in lane_blocks]
         for part in range(PHASE // ROWS):
-            hid_next[part, inside, :] = mm(h2_ref[quarters[part], :], wup_next[...], NN)
-            branch[quarters[part], :] += mm(act[quarters[part], :], wdown[...], NN)
-            if part < width // CHUNK:
-                block = slice(part * CHUNK, (part + 1) * CHUNK)
-                slot[width + part * CHUNK : width + (part + 1) * CHUNK, :] = mm(
-                    act_t[...], db_ref[:, block], NN
-                ).astype(BF16)
+            products = backward_products(part, hid_next, wdown, wup_next, slot)
             for group in range(4):
                 start = group * PHASE + part * ROWS
                 for at, lanes in enumerate(lane_blocks):
+                    next(products, None)
                     own = hid[group, HALF + part * ROWS : HALF + (part + 1) * ROWS, lanes]
                     total = jnp.zeros((ROWS, LANES), F32)
                     for tap in range(9):
@@ -765,6 +819,8 @@
         for q in range(4):
             weights_back(q, wup_odd, work.at[2])
         settle(step)
+        for load in loads:
+            load.wait()
         gate_one, scale_two, gate_two = mod_ref[2:3, :], mod_ref[4:5, :], mod_ref[5:6, :]
         live = live_ref[0, 0]
 
@@ -869,9 +925,9 @@
             keep(rows, width),
             keep(width, rows),
             keep(rows, width),
-            keep(rows, width),
-            keep(rows, width),
-            keep(rows, width),
+            whole(pl.ANY),
+            whole(pl.ANY),
+            whole(pl.ANY),
             keep(6, width),
             up_block(-1, 1),
             up_block(0, 0),
@@ -902,8 +958,12 @@
             pltpu.VMEM((steps,) + parcel, BF16),
             pltpu.VMEM((per,) + parcel, BF16),
             pltpu.VMEM((per, sum_landing(2 * width, n_wide), CHUNK), BF16),
+            pltpu.VMEM((rows, width), F32),
+            pltpu.VMEM((rows, width), BF16),
+            pltpu.VMEM((rows, width), BF16),
             pltpu.SemaphoreType.DMA((2, steps + per)),
             pltpu.SemaphoreType.DMA((2, per * HALVINGS)),
+            pltpu.SemaphoreType.DMA((3,)),
         ],
         compiler_params=pltpu.CompilerParams(
             vmem_limit_bytes=62 * MIB, collective_id=1, has_side_effects=True
@@ -1157,12 +1217,21 @@
 
 
 def input_backward_kernel(
-    n_wide, x_ref, dx1_ref, dqkv_ref, mod_ref, taps_ref, wqkv_ref, own_ref, silu_ref, dmod_ref, block_in,
-    got_dx, got_block, full, small, dtaps_ref,
-    base, shifted, first_in, dh1, dx, work, got_sums, tap_sums, tap_got, sems, local_sems, sum_sems, small_sems,
+    n_wide, x_ref, mod_ref, taps_ref, own_ref, silu_ref, dmod_ref, dx1_hbm, dqkv_hbm, wqkv_hbm, block_in,
+    got_dx, got_block, full, small, late, dtaps_ref,
+    base, shifted, first_in, dh1, dx1_ref, dqkv_ref, wqkv_ref, dx, work, got_sums, tap_sums, tap_got,
+    sems, local_sems, sum_sems, small_sems, late_sems,
 ):
     rows_all, width = x_ref.shape
     wide, here = lax.axis_index("wide"), lax.axis_index("narrow")
+    loads = [
+        pltpu.make_async_copy(src, dst, local_sems.at[2 + at])
+        for at, (src, dst) in enumerate(
+            ((dqkv_hbm, dqkv_ref), (wqkv_hbm, wqkv_ref), (dx1_hbm, dx1_ref))
+        )
+    ]
+    for load in loads:
+        load.start()
     shift_one, scale_one = mod_ref[0:1, :], mod_ref[1:2, :]
     greet([(wide, peer) for peer in narrow_peers(here)] + wide_partners(wide, here, n_wide))
     pieces = full.shape[0]
@@ -1170,7 +1239,7 @@
     per_sum = sum_semaphores(n_wide)
     sums = [
         WideSum(own_ref.at[at * rows : (at + 1) * rows], work.at[at], full.at[at], got_sums.at[at], sum_sems,
-                at * per_sum, wide, here, n_wide)
+                at * per_sum, wide, here, n_wide, order=((0, 1, 2), (1, 2, 0))[at])
         for at in range(pieces)
     ]
     queues = [one.actions() for one in sums]
@@ -1181,6 +1250,25 @@
                 for act in queues[at].pop(0):
                     act()
 
+    partners = [(wide, here ^ 2)] + wide_partners(wide, here, n_wide)[::-1] + [(wide, here ^ 1)]
+    levels = len(partners)
+
+    def small_copy(level):
+        have = 1 << level
+        return remote(small.at[:have], small.at[have : 2 * have], small_sems, 2 * level, *partners[level])
+
+    def late_copy(level):
+        have = 1 << level
+        return remote(late.at[:have], late.at[have : 2 * have], late_sems, level, *partners[level])
+
+    def small_step(level):
+        small_copy(level).wait_recv()
+        if level + 1 < levels:
+            small_copy(level + 1).start()
+
+    early = [silu_ref[0:1, :].astype(F32)] + [dmod_ref[at : at + 1, :] for at in range(4)]
+    small[0] = jnp.concatenate(early + [jnp.zeros((SMALL - 5, width), F32)]).astype(BF16)
+    small_copy(0).start()
     advance(0, 1)
     block_back = Return(block_in, got_block, sems, local_sems.at[1], 3, wide, here)
     block_back.start()
@@ -1206,9 +1294,12 @@
         base[group, HALF : HALF + PHASE, :] = total
         return carry
 
-    lax.fori_loop(0, 3, du_step, 0)
-    advance(0)
-    lax.fori_loop(3, 4, du_step, 0)
+    loads[0].wait()
+    loads[1].wait()
+    small_step(0)
+    lax.fori_loop(0, 2, du_step, 0)
+    advance(0, 1)
+    lax.fori_loop(2, 4, du_step, 0)
 
     def conv_step(block, carry):
         lanes = ds(block * LANES, LANES)
@@ -1219,10 +1310,13 @@
 
     for block in range(width // LANES):
         if block % 2:
-            advance(0)
-        else:
-            advance(1)
+            advance(0, 1)
+        if 1 <= block < levels:
+            small_step(block)
         lax.fori_loop(block, block + 1, conv_step, 0)
+    for level in range(max(1, width // LANES), levels):
+        small_step(level)
+    loads[2].wait()
 
     def fold(value):
         return value.reshape(ROWS // 8, 8, width).sum(axis=0)
@@ -1239,8 +1333,6 @@
         ).astype(BF16)
         return tuple(total + fold(one) for total, one in zip(sums, (grad, grad * unit)))
 
-    partners = [(wide, here ^ 2)] + wide_partners(wide, here, n_wide)[::-1] + [(wide, here ^ 1)]
-    levels = len(partners)
     tap_sums[0, :9, :] = dtaps_ref[:9, :]
     tap_sums[0, 9:, :] = jnp.zeros((7, width), F32)
 
@@ -1258,28 +1350,25 @@
     for at in range(2):
         found = lax.fori_loop(8 * at, 8 * at + 8, rows_step, found)
         taps_step(at)
-    dmod = [jnp.sum(one, axis=0, keepdims=True) for one in found]
-    dmod += [dmod_ref[at : at + 1, :] for at in range(4)]
-
-    stack = jnp.concatenate([silu_ref[0:1, :].astype(F32)] + dmod + [jnp.zeros((SMALL - 7, width), F32)])
-    small[0] = stack.astype(BF16)
-
-    def small_copy(level):
-        have = 1 << level
-        return remote(small.at[:have], small.at[have : 2 * have], small_sems, 2 * level, *partners[level])
-
-    small_copy(0).start()
+    chunks = [
+        jnp.sum(one, axis=0, keepdims=True)[:, at * LANES : (at + 1) * LANES]
+        for one in found
+        for at in range(width // LANES)
+    ]
+    late[0] = jnp.concatenate(chunks + [jnp.zeros((SMALL - len(chunks), LANES), F32)]).astype(BF16)
+    late_copy(0).start()
     for copy in back.copies:
         copy.start()
     back.own.start()
     advance(0, 1)
     for level in range(levels):
-        small_copy(level).wait_recv()
+        late_copy(level).wait_recv()
         if level + 1 < levels:
-            small_copy(level + 1).start()
+            late_copy(level + 1).start()
         if level >= 2:
             taps_step(level)
-        advance(0, 1)
+        if level % 2:
+            advance(0, 1)
     dtaps_ref[...] = tap_sums[levels]
     while any(queues):
         advance(0, 1)
@@ -1287,6 +1376,7 @@
     back.wait()
     for level in range(levels):
         small_copy(level).wait_send()
+        late_copy(level).wait_send()
         taps_copy(level).wait_send()
     for one in sums:
         one.wait_sends()
@@ -1308,32 +1398,37 @@
             back,
             shape((pieces, sum_rows, width), BF16),
             shape((1 << levels, SMALL, width), BF16),
+            shape((1 << levels, SMALL, LANES), BF16),
             shape((SMALL, width), F32),
         ),
-        in_specs=[whole()] * 10,
-        out_specs=(whole(),) * 5,
+        in_specs=[whole()] * 6 + [whole(pl.ANY)] * 4,
+        out_specs=(whole(),) * 6,
         scratch_shapes=[pltpu.VMEM((4, PAD, width), F32)] * 3
         + [
             pltpu.VMEM((rows, width), F32),
+            pltpu.VMEM((rows, width), F32),
+            pltpu.VMEM((rows, 3 * width), BF16),
+            pltpu.VMEM(wqkv.shape, BF16),
             pltpu.VMEM((4, slots, rows // (4 * slots), width), BF16),
             pltpu.VMEM((pieces, sum_rows, width), BF16),
             pltpu.VMEM((pieces, sum_landing(sum_rows, n_wide), width), BF16),
             pltpu.VMEM((levels + 1, SMALL, width), F32),
             pltpu.VMEM((levels, SMALL, width), F32),
             pltpu.SemaphoreType.DMA((2, 6)),
-            pltpu.SemaphoreType.DMA((2,)),
+            pltpu.SemaphoreType.DMA((5,)),
             pltpu.SemaphoreType.DMA((2, pieces * per_sum)),
             pltpu.SemaphoreType.DMA((2, 2 * levels)),
+            pltpu.SemaphoreType.DMA((2, levels)),
         ],
         compiler_params=pltpu.CompilerParams(
             vmem_limit_bytes=56 * MIB, collective_id=3, has_side_effects=True
         ),
         name="input_backward",
-    )(x, dx1, dqkv, mod, taps, wqkv, own, silu_row, dmod, block)
+    )(x, mod, taps, own, silu_row, dmod, dx1, dqkv, wqkv, block)
 
 
 def outputs_kernel(
-    dx_in, block_in, attn_sum, ffn_sum, small, cond_ref, ada_hbm,
+    dx_in, block_in, attn_sum, ffn_sum, small, late, cond_ref, ada_hbm,
     gada_hbm, dx_hbm, block_hbm, gqkv_hbm, gout_hbm, gup_hbm, gdown_hbm, gcond_ref,
     ada, gada, dx, block, gqkv, gout, gup, gdown, sems, in_sem,
 ):
@@ -1353,9 +1448,25 @@
     pick = lambda row: mm(
         one_hot(devices, devices * SMALL, lambda at: at * SMALL + row), shares, NN
     ).astype(BF16)
+    late_shares = late[...].reshape(devices * SMALL, LANES)
+    blocks = width // LANES
+
+    def pick_late(part):
+        return jnp.concatenate(
+            [
+                mm(
+                    one_hot(devices, devices * SMALL, lambda at, at_row=part * blocks + at_block: at * SMALL + at_row),
+                    late_shares, NN,
+                )
+                for at_block in range(blocks)
+            ],
+            axis=1,
+        ).astype(BF16)
+
     silu_all = pick(0)
+    dmods = [pick_late(part) if part < 2 else pick(part - 1) for part in range(6)]
     for part in range(6):
-        gada[part] = mm(silu_all, pick(1 + part), TN)
+        gada[part] = mm(silu_all, dmods[part], TN)
         put(gada.at[part], gada_hbm.at[:, part * width : (part + 1) * width])
     slab = attn_sum.shape[1] // 2
     for part in range(3):
@@ -1378,17 +1489,16 @@
         put(gdown.at[cols], gdown_hbm.at[cols])
     put(gup, gup_hbm)
 
-    def own_column(row, part):
+    def own_place(row):
         away = row ^ here
         place = ((away // 2) % 2) + (away % 2) * (devices // 2)
-        return jnp.where(row < cond_ref.shape[0], place * SMALL + 1 + part, -1)
+        return jnp.where(row < cond_ref.shape[0], place, -1)
 
     load_ada.wait()
+    choose = one_hot(16, devices, own_place)
     grad_silu = jnp.zeros((16, width), F32)
     for part in range(6):
-        own = mm(
-            one_hot(16, devices * SMALL, lambda row, part=part: own_column(row, part)), shares, NN
-        ).astype(BF16)
+        own = mm(choose, dmods[part], NN).astype(BF16)
         grad_silu += mm(own, ada[:, part * width : (part + 1) * width], NT)
     cond = cond_ref[...].astype(F32)
     gate = 1.0 / (1.0 + jnp.exp(-cond))
@@ -1397,7 +1507,7 @@
         copy.wait()
 
 
-def outputs(dx, block, attn_sum, ffn_sum, small, cond, w_ada):
+def outputs(dx, block, attn_sum, ffn_sum, small, late, cond, w_ada):
     slots, _, quarter, width = dx.shape
     slab = attn_sum.shape[1] // 2
     pieces = ffn_sum.shape[0]
@@ -1416,7 +1526,7 @@
             shape((local, width), F32),
             shape(cond.shape, F32),
         ),
-        in_specs=[whole()] * 6 + [whole(pl.ANY)],
+        in_specs=[whole()] * 7 + [whole(pl.ANY)],
         out_specs=(whole(pl.ANY),) * 7 + (whole(),),
         scratch_shapes=[
             pltpu.VMEM(w_ada.shape, BF16),
@@ -1432,7 +1542,7 @@
         ],
         compiler_params=pltpu.CompilerParams(vmem_limit_bytes=56 * MIB),
         name="outputs",
-    )(dx, block, attn_sum, ffn_sum, small, cond, w_ada)
+    )(dx, block, attn_sum, ffn_sum, small, late, cond, w_ada)
 
 
 def per_device(
@@ -1453,7 +1563,7 @@
     own_silu = jnp.broadcast_to(lax.dynamic_slice_in_dim(silu_low, here, 1, 0), (16, width))
     live = (here < counts[0]).astype(F32).reshape(1, 1)
 
-    (x, cot, mod, u, qkv, probs, ctx, att, x1, h2, h2t, db, wqkv, wout, wup, wdown, ktaps) = front(
+    (x, cot, u, qkv, probs, ctx, wqkv, wout, mod, att, x1, h2, h2t, db, wup, wdown, ktaps) = front(
         live, own_silu, attn_taps, tokens, cotangent, w_ada, qkv_t, w_out, w_up, w_down, ktaps_own
     )
     cot = cot.reshape(rows_all, width)
@@ -1463,11 +1573,11 @@
     )
     block_g = block_g.reshape(4, lat_dev, shard_rows // 4, width)
     dqkv, own, ffn_sum, gtaps = attn_backward(n_wide, datt, ctx, u, wout, parcels, qkv, probs)
-    got_dx, got_block, attn_sum, small, dattn_taps = input_backward(
+    got_dx, got_block, attn_sum, small, late, dattn_taps = input_backward(
         n_wide, x, dx1, dqkv, mod, attn_taps, wqkv, own, own_silu, dmod_mid, block_g
     )
     grad_w_ada, grad_tokens, block, gqkv, grad_w_out, grad_w_up, grad_w_down, grad_condition = outputs(
-        got_dx, got_block, attn_sum, ffn_sum, small, condition, w_ada
+        got_dx, got_block, attn_sum, ffn_sum, small, late, condition, w_ada
     )
     grad_k_ffn = gtaps[:9].reshape(3, 3, local)
     grad_k_attn = dattn_taps[:9].reshape(3, 3, width)

time: 350 us -> 336 us (0.960)
  the two profiles are of different devices: /device:TPU:0 before, /device:TPU:3 now
where the time goes in v6:
time: 336 us; the launch traced here: 330 us
  Pallas kernels  315 us (94%)
  local copies, waits for them, and re-layouts  10.5 us (3%)
    pallas_call x1, Pallas kernels, front(): pl.pallas_call(front_kernel, out_shape=streamed + (shape((6, width), F32)...  88.8 us
    pallas_call x1, Pallas kernels, ffn(): pl.pallas_call(partial(ffn_kernel, n_wide), grid=(steps,), out_shape=(sha...  85.5 us
    pallas_call x1, Pallas kernels, input_backward(): pl.pallas_call(partial(input_backward_kernel, n_wide), out_shape=(back, b...  65.3 us
    pallas_call x1, Pallas kernels, attn_backward(): pl.pallas_call(partial(attn_backward_kernel, n_wide), out_shape=(shape((r...  57.3 us
    pallas_call x1, Pallas kernels, outputs(): pl.pallas_call(outputs_kernel, out_shape=(shape(w_ada.shape, F32), shape(...  18.3 us

profile of v6, /device:TPU:3, one launch (start us, length us, event | category | flops | bytes accessed | tf_op | source)
XLA Modules:
  0.0 329.8 jit_solution(15147756207214661303)
XLA Ops:
  1.3 0.7 convert_element_type.17
  2.0 0.6 broadcast_in_dim.8.silu_ref
  2.7 0.7 reshape.49
  3.4 0.6 pad.4.ktaps_src
  4.0 1.4 reshape.56.taps_ref
  5.4 2.1 copy.25
  7.5 88.8 %attn_forward.1 = (bf16[1024,768]{1,0:T(8,128)(2,1)}, bf16[4,4,64,768]{3,2,1,0:T(8,128)(2,1)}, bf16[1024,768]{1,0:T(8,128)(2,1)}, bf16[1024,2304]{1,0:T(8,128)(2...) custom-call(f32[1,1]{1,0:T(1,128)} %bitcast.1.live_ref, ...), custom_call_target="tpu_custom_call" | custom-call | tf_op jit(solution)/shard_map/attn_forward/pallas_call | solution.py:582
  96.3 1.6 slice_convert_fusion.taps_even.taps_odd
  97.9 85.5 %feed_forward.1 = (bf16[1024,768]{1,0:T(8,128)(2,1)}, f32[1024,768]{1,0:T(8,128)}, bf16[1024,768]{1,0:T(8,128)(2,1)}, f32[4,768]{1,0:T(4,128)}, bf16[3,1552,256]{2,1,0:T(8,128)(2,1)}) custom-call(f32[1,1]{1,0:T(1,128)} %bitcast.1.live_ref, bf16[1024,768]{1,0:T(8,128)(2,1)} %get-tuple-element.52.h2_ref, bf16[768,1024]{1,0:T(8,128)(2,1)} %get-tuple-element.53.h2t_ref, ...), custom_call_target="tpu_custom_call" | custom-call | tf_op jit(solution)/shard_map/feed_forward/pallas_call | solution.py:913
  183.4 57.3 %attn_backward.1 = (bf16[1024,2304]{1,0:T(8,128)(2,1)}, bf16[768,768]{1,0:T(8,128)(2,1)}, bf16[3,1536,256]{2,1,0:T(8,128)(2,1)}, f32[16,768]{1,0:T(8,128)}) custom-call(bf16[1024,768]{1,0:T(8,128)(2,1)} %get-tuple-element.61.datt_ref, bf16[1024,768]{1,0:T(8,128)(2,1)} %get-tuple-element.62.ctx_ref, bf16[1024,768]{1,0:T(8,128)(2,1)} %get-tuple-element.63.u_ref, ...), custom_call_target="tpu_custom_call" | custom-call | tf_op jit(solution)/shard_map/attn_backward/pallas_call | solution.py:1178
  240.7 0.0 copy-start
  240.7 65.3 %input_backward.1 = (bf16[4,4,64,768]{3,2,1,0:T(8,128)(2,1)}, bf16[4,4,64,768]{3,2,1,0:T(8,128)(2,1)}, bf16[2,384,768]{2,1,0:T(8,128)(2,1)}, bf16[32,16,768]{2,1...) custom-call(bf16[1024,768]{1,0:T(8,128)(2,1)} %get-tuple-element.50.x_ref, ...), custom_call_target="tpu_custom_call" | custom-call | tf_op jit(solution)/shard_map/input_backward/pallas_call | solution.py:1394
  306.0 1.4 reshape.52
  307.4 0.0 copy-done
  307.4 0.6 reshape.53
  308.1 18.3 %outputs.1 = (f32[768,4608]{1,0:T(8,128)}, f32[4,256,768]{2,1,0:T(8,128)}, bf16[4,256,768]{2,1,0:T(8,128)(2,1)}, f32[3,768,192]{2,1,0:T(8,128)}, f32[192,768]{1,...) custom-call(bf16[4,4,64,768]{3,2,1,0:T(8,128)(2,1)} %get-tuple-element.74.dx_in, ...), custom_call_target="tpu_custom_call" | custom-call | tf_op jit(solution)/shard_map/outputs/pallas_call | solution.py:1517
  326.4 2.9 copy.24
  (1 shorter events, 0.0 us)
Async XLA Ops:
  240.7 66.8 %copy-start = (f32[16,768]{1,0:T(8,128)S(1)}, f32[16,768]{1,0:T(8,128)}, u32[]{:S(2)}) copy-start(f32[16,768]{1,0:T(8,128)} %get-tuple-element.88) | copy-start | bytes 147460

commit v7 on v6

--- a/solution.py
+++ b/solution.py
@@ -214,6 +214,8 @@
 
 
 HALVINGS = 3
+EARLY = 32
+SMALL = 16
 
 
 class WideSum:
@@ -307,6 +309,13 @@
 
 def halvings_ahead(pieces, levels):
     return [min(levels, pieces - at) for at in range(pieces)]
+
+
+def lane_rows(values_in, rows):
+    cut = [
+        one[:, at * LANES : (at + 1) * LANES] for one in values_in for at in range(one.shape[1] // LANES)
+    ]
+    return jnp.concatenate(cut + [jnp.zeros((rows - len(cut), LANES), F32)]).astype(BF16)
 
 
 def greet(partners):
@@ -445,7 +454,7 @@
     def conv_step(block, carry):
         lanes = ds(block * LANES, LANES)
         shift_cols(base, shifted, lanes)
-        taps = [taps_ref[t : t + 1, lanes] for t in range(9)]
+        taps = [taps_ref[t // 3, t % 3 : t % 3 + 1, lanes].astype(F32) for t in range(9)]
 
         def rows_step(step, carry):
             for group in range(4):
@@ -464,7 +473,7 @@
     g_qkv.corner()
     g_out.corner()
     g_up.swap()
-    exchange_cot.start()
+    g_down.start_far()
     lax.fori_loop(2 * blocks // 3, blocks, conv_step, 0)
     flush(u_ref, u_hbm)
     g_qkv.share_corner()
@@ -505,6 +514,8 @@
     flush(qkv_ref, qkv_hbm)
     g_up.corner()
     g_out.share_corner()
+    g_down.swap()
+    exchange_cot.start()
 
     def attend_group(group):
         lax.fori_loop(group * pairs, (group + 1) * pairs, attend_step, 0)
@@ -513,12 +524,10 @@
 
     attend_group(0)
     g_up.share_corner()
-    exchange_cot.wait()
-    flush(cot_ref, cot_hbm_out)
-    g_down.start_far()
     attend_group(1)
+    g_down.corner()
     attend_group(2)
-    g_down.swap()
+    g_down.share_corner()
     attend_group(3)
     flush(ctx_ref, ctx_hbm)
     g_out.finish()
@@ -542,9 +551,9 @@
         db_ref[rows, :] = (cot_ref[group, source].astype(F32) * live * gate_two).astype(BF16)
         return carry
 
-    g_down.corner()
+    exchange_cot.wait()
+    flush(cot_ref, cot_hbm_out)
     lax.fori_loop(0, rows_all // ROWS, second_step, 0)
-    g_down.share_corner()
     for part in range(4):
         h2t_ref[:, part * PHASE : (part + 1) * PHASE] = h2_ref[
             part * PHASE : (part + 1) * PHASE, :
@@ -714,7 +723,7 @@
         yield
 
     def forward(hid, wdown, taps_ref, wup_last, slot):
-        taps = [[taps_ref[0, t : t + 1, lanes] for t in range(9)] for lanes in lane_blocks]
+        taps = [[taps_ref[0, t : t + 1, lanes].astype(F32) for t in range(9)] for lanes in lane_blocks]
         for part in range(PHASE // ROWS):
             rows = slice(HALF + part * ROWS, HALF + (part + 1) * ROWS)
             for group in range(4):
@@ -741,7 +750,7 @@
                     )
 
     def backward(hid, hid_next, wdown, wup_next, taps_ref, slot):
-        taps = [[taps_ref[0, t : t + 1, lanes] for t in range(9)] for lanes in lane_blocks]
+        taps = [[taps_ref[0, t : t + 1, lanes].astype(F32) for t in range(9)] for lanes in lane_blocks]
         act_t[...] = act[...].T
         for part in range(PHASE // ROWS):
             rows = slice(HALF + part * ROWS, HALF + (part + 1) * ROWS)
@@ -855,27 +864,6 @@
                 sums[at].half_copy(level).wait_send()
 
 
-def conv_back(grad, grad_moved, source, lanes, taps, dtaps_ref, out_ref):
-    def rows_step(step, sums):
-        sums = list(sums)
-        for group in range(4):
-            total = jnp.zeros((ROWS, LANES), F32)
-            own = source[group, ds(HALF + step * ROWS, ROWS, HALF), lanes]
-            for tap in range(9):
-                moved = tap_value(
-                    grad, grad_moved, group, 2 - tap // 3, 2 - tap % 3, step * ROWS, lanes
-                )
-                total += taps[tap] * moved
-                sums[tap] += (own * moved).reshape(ROWS // 8, 8, LANES).sum(axis=0)
-            out_ref[ds(group * PHASE + step * ROWS, ROWS), lanes] = total.astype(out_ref.dtype)
-        return tuple(sums)
-
-    start = tuple(jnp.zeros((8, LANES), F32) for _ in range(9))
-    sums = lax.fori_loop(0, PHASE // ROWS, rows_step, start)
-    for tap in range(9):
-        dtaps_ref[tap : tap + 1, lanes] = jnp.sum(sums[tap], axis=0, keepdims=True)
-
-
 def ffn(n_wide, live, h2, h2t, db, x1, cot, att, mod, wup, wdown, taps):
     rows, width = h2.shape
     shards, _, local = taps.shape
@@ -908,7 +896,7 @@
             slot, part = slot_and_part(step, odd)
             return slot, 0, part
 
-        return pl.BlockSpec((1, 9, CHUNK), index)
+        return pl.BlockSpec((1, taps.shape[1], CHUNK), index)
 
     return pl.pallas_call(
         partial(ffn_kernel, n_wide),
@@ -973,10 +961,10 @@
 
 
 def attn_backward_kernel(
-    n_wide, datt_ref, ctx_ref, u_ref, wout_ref, parcels, qkv_hbm, probs_hbm,
-    dqkv_ref, own_ref, full, gtaps_ref,
+    n_wide, datt_ref, ctx_ref, u_ref, wout_ref, parcels, silu_ref, dmod_ref, qkv_hbm, probs_hbm,
+    dqkv_ref, own_ref, full, gtaps_ref, small,
     dctx, probs_buf, weights, got_near, chip_sum, got_far, work, got_sums, taps_sum, taps_got,
-    sems, in_sems, sum_sems,
+    sems, in_sems, sum_sems, small_sems,
 ):
     rows_all, width = u_ref.shape
     wide, here = lax.axis_index("wide"), lax.axis_index("narrow")
@@ -1026,6 +1014,20 @@
 
     for at in range(pieces):
         taps_sum[0, :, at * CHUNK : (at + 1) * CHUNK] = parcels[at, rows:, :].astype(F32)
+    partners = wide_partners(wide, here, n_wide) + [(wide, here ^ 1), (wide, here ^ 2)]
+
+    def small_copy(level):
+        have = 1 << level
+        return remote(small.at[:have], small.at[have : 2 * have], small_sems, level, *partners[level])
+
+    def small_step(level):
+        small_copy(level).wait_recv()
+        if level + 1 < len(partners):
+            small_copy(level + 1).start()
+
+    early = [silu_ref[0:1, :].astype(F32)] + [dmod_ref[at : at + 1, :] for at in range(4)]
+    small[0] = lane_rows(early, EARLY)
+    small_copy(0).start()
     taps_copy(0).start()
     advance(2, 0, 1)
 
@@ -1130,9 +1132,11 @@
         far_out.start()
 
     later = lambda *which: partial(advance, *which)
+    small_plan = [(2 * level + 3, partial(small_step, level)) for level in range(len(partners) - 1)]
     attend_loop(
         0, steps // 2,
-        [(1, send_out), (2, later(2, 0)), (5, later(1)), (7, partial(taps_add, 0)), (8, later(2, 0)), (11, later(1))],
+        [one for one in small_plan if one[0] < steps // 2]
+        + [(1, send_out), (2, later(2, 0)), (5, later(1)), (7, partial(taps_add, 0)), (8, later(2, 0)), (11, later(1))],
     )
     weight_grads(1)
     near_early.start()
@@ -1142,10 +1146,12 @@
     far.start()
     attend_loop(
         steps // 2, steps,
-        [(13, later(1, 0)), (14, partial(taps_add, 1)), (16, later(2))],
+        [one for one in small_plan if one[0] >= steps // 2]
+        + [(13, later(1, 0)), (14, partial(taps_add, 1)), (16, later(2))],
     )
     weight_grads(0)
     near_late.start()
+    small_step(len(partners) - 1)
     for level in range(2, levels):
         taps_add(level)
     gtaps_ref[...] = taps_sum[levels]
@@ -1164,9 +1170,11 @@
         taps_copy(level).wait_send()
     for copy in (near_out, near_early, late_out, near_late, far_out, far):
         copy.wait_send()
-
-
-def attn_backward(n_wide, datt, ctx, u, wout, parcels, qkv, probs):
+    for level in range(len(partners)):
+        small_copy(level).wait_send()
+
+
+def attn_backward(n_wide, datt, ctx, u, wout, parcels, silu_row, dmod, qkv, probs):
     rows, width = u.shape
     slots = lax.axis_size("narrow")
     slab = wout.shape[0] // slots
@@ -1182,9 +1190,10 @@
             shape((4 * slab, width), BF16),
             shape((pieces, sum_rows, CHUNK), BF16),
             shape((16, pieces * CHUNK), F32),
+            shape((n_wide * slots, EARLY, LANES), BF16),
         ),
-        in_specs=[whole()] * 5 + [whole(pl.ANY)] * 2,
-        out_specs=(whole(),) * 4,
+        in_specs=[whole()] * 7 + [whole(pl.ANY)] * 2,
+        out_specs=(whole(),) * 5,
         scratch_shapes=[
             pltpu.VMEM((rows, width), BF16),
             pltpu.VMEM((2, PHASE, 2 * PHASE), BF16),
@@ -1199,12 +1208,13 @@
             pltpu.SemaphoreType.DMA((2, 6 + levels)),
             pltpu.SemaphoreType.DMA((3,)),
             pltpu.SemaphoreType.DMA((2, pieces * per_sum)),
+            pltpu.SemaphoreType.DMA((2, levels + 2)),
         ],
         compiler_params=pltpu.CompilerParams(
             vmem_limit_bytes=56 * MIB, collective_id=2, has_side_effects=True
         ),
         name="attn_backward",
-    )(datt, ctx, u, wout, parcels, qkv, probs)
+    )(datt, ctx, u, wout, parcels, silu_row, dmod, qkv, probs)
 
 
 def one_hot(rows, columns, wanted):
@@ -1213,14 +1223,11 @@
     return jnp.where(column == wanted(row), 1.0, 0.0).astype(BF16)
 
 
-SMALL = 16
-
-
 def input_backward_kernel(
-    n_wide, x_ref, mod_ref, taps_ref, own_ref, silu_ref, dmod_ref, dx1_hbm, dqkv_hbm, wqkv_hbm, block_in,
-    got_dx, got_block, full, small, late, dtaps_ref,
-    base, shifted, first_in, dh1, dx1_ref, dqkv_ref, wqkv_ref, dx, work, got_sums, tap_sums, tap_got,
-    sems, local_sems, sum_sems, small_sems, late_sems,
+    n_wide, x_ref, mod_ref, taps_ref, own_ref, dx1_hbm, dqkv_hbm, wqkv_hbm, block_in,
+    got_dx, got_block, full, late, dtaps_ref,
+    base, shifted, first_in, dh1, dx1_ref, dqkv_ref, wqkv_ref, dx, work, got_sums, tap_parts, tap_sums, tap_got,
+    sems, local_sems, sum_sems, taps_sems, late_sems,
 ):
     rows_all, width = x_ref.shape
     wide, here = lax.axis_index("wide"), lax.axis_index("narrow")
@@ -1233,7 +1240,7 @@
     for load in loads:
         load.start()
     shift_one, scale_one = mod_ref[0:1, :], mod_ref[1:2, :]
-    greet([(wide, peer) for peer in narrow_peers(here)] + wide_partners(wide, here, n_wide))
+    greet([(wide, peer) for peer in narrow_peers(here)] + [(wide ^ away, here) for away in range(1, n_wide)])
     pieces = full.shape[0]
     rows = full.shape[1]
     per_sum = sum_semaphores(n_wide)
@@ -1250,25 +1257,19 @@
                 for act in queues[at].pop(0):
                     act()
 
-    partners = [(wide, here ^ 2)] + wide_partners(wide, here, n_wide)[::-1] + [(wide, here ^ 1)]
-    levels = len(partners)
-
-    def small_copy(level):
-        have = 1 << level
-        return remote(small.at[:have], small.at[have : 2 * have], small_sems, 2 * level, *partners[level])
-
-    def late_copy(level):
-        have = 1 << level
-        return remote(late.at[:have], late.at[have : 2 * have], late_sems, level, *partners[level])
-
-    def small_step(level):
-        small_copy(level).wait_recv()
-        if level + 1 < levels:
-            small_copy(level + 1).start()
-
-    early = [silu_ref[0:1, :].astype(F32)] + [dmod_ref[at : at + 1, :] for at in range(4)]
-    small[0] = jnp.concatenate(early + [jnp.zeros((SMALL - 5, width), F32)]).astype(BF16)
-    small_copy(0).start()
+    levels = n_wide.bit_length() - 1
+    late_wide = [
+        remote(late.at[0], late.at[away], late_sems, away - 1, wide ^ away, here) for away in range(1, n_wide)
+    ]
+    late_narrow = [
+        remote(late.at[:n_wide], late.at[away * n_wide : (away + 1) * n_wide], late_sems, n_wide - 2 + away,
+               wide, here ^ away)
+        for away in (2, 3, 1)
+    ]
+    taps_narrow = [
+        remote(tap_sums.at[levels], tap_got.at[levels + away - 1], taps_sems, levels + away - 1, wide, here ^ away)
+        for away in (2, 3, 1)
+    ]
     advance(0, 1)
     block_back = Return(block_in, got_block, sems, local_sems.at[1], 3, wide, here)
     block_back.start()
@@ -1296,100 +1297,118 @@
 
     loads[0].wait()
     loads[1].wait()
-    small_step(0)
     lax.fori_loop(0, 2, du_step, 0)
     advance(0, 1)
     lax.fori_loop(2, 4, du_step, 0)
 
-    def conv_step(block, carry):
-        lanes = ds(block * LANES, LANES)
-        shift_cols(base, shifted, lanes)
-        conv_back(base, shifted, first_in, lanes, [taps_ref[t : t + 1, lanes] for t in range(9)],
-                  dtaps_ref, dh1)
+    blocks = width // LANES
+
+    def shift_step(block, carry):
+        shift_cols(base, shifted, ds(block * LANES, LANES))
         return carry
 
-    for block in range(width // LANES):
-        if block % 2:
-            advance(0, 1)
-        if 1 <= block < levels:
-            small_step(block)
-        lax.fori_loop(block, block + 1, conv_step, 0)
-    for level in range(max(1, width // LANES), levels):
-        small_step(level)
-    loads[2].wait()
-
-    def fold(value):
-        return value.reshape(ROWS // 8, 8, width).sum(axis=0)
-
-    back = Return(dx, got_dx, sems, local_sems.at[0], 0, wide, here)
-
-    def rows_step(at, sums):
-        group, source = at // 4, at % 4
-        span = ds(at * ROWS, ROWS)
-        unit, inv = normed(x_ref[span, :].astype(F32))
-        grad = dh1[span, :]
-        dx[group, source] = (
-            dx1_ref[span, :] + norm_back(unit, inv, grad * (1.0 + scale_one))
-        ).astype(BF16)
-        return tuple(total + fold(one) for total, one in zip(sums, (grad, grad * unit)))
-
-    tap_sums[0, :9, :] = dtaps_ref[:9, :]
-    tap_sums[0, 9:, :] = jnp.zeros((7, width), F32)
+    lax.fori_loop(0, blocks, shift_step, 0)
+    tap_parts[...] = jnp.zeros_like(tap_parts)
+    advance(0, 1)
 
     def taps_copy(level):
-        return remote(tap_sums.at[level], tap_got.at[level], small_sems, 2 * level + 1, *partners[level])
+        return remote(tap_sums.at[level], tap_got.at[level], taps_sems, level, wide ^ (1 << level), here)
 
     def taps_step(level):
         taps_copy(level).wait_recv()
         tap_sums[level + 1] = tap_sums[level] + tap_got[level]
         if level + 1 < levels:
             taps_copy(level + 1).start()
-
-    taps_copy(0).start()
+        else:
+            for copy in taps_narrow:
+                copy.start()
+
+    def fold(value):
+        return value.reshape(ROWS // 8, 8, width).sum(axis=0)
+
+    back = Return(dx, got_dx, sems, local_sems.at[0], 0, wide, here)
     found = tuple(jnp.zeros((8, width), F32) for _ in range(2))
-    for at in range(2):
-        found = lax.fori_loop(8 * at, 8 * at + 8, rows_step, found)
-        taps_step(at)
-    chunks = [
-        jnp.sum(one, axis=0, keepdims=True)[:, at * LANES : (at + 1) * LANES]
-        for one in found
-        for at in range(width // LANES)
-    ]
-    late[0] = jnp.concatenate(chunks + [jnp.zeros((SMALL - len(chunks), LANES), F32)]).astype(BF16)
-    late_copy(0).start()
-    for copy in back.copies:
+    for at, away in enumerate((2, 3, 1, 0)):
+        source = away ^ here
+
+        def conv_step(block, carry, source=source):
+            lanes = ds(block * LANES, LANES)
+            taps = [taps_ref[t // 3, t % 3 : t % 3 + 1, lanes].astype(F32) for t in range(9)]
+            sums = [jnp.zeros((8, LANES), F32) for _ in range(9)]
+            for group in range(4):
+                total = jnp.zeros((ROWS, LANES), F32)
+                own = first_in[group, ds(HALF + source * ROWS, ROWS, HALF), lanes]
+                for tap in range(9):
+                    moved = tap_value(
+                        base, shifted, group, 2 - tap // 3, 2 - tap % 3, source * ROWS, lanes
+                    )
+                    total += taps[tap] * moved
+                    sums[tap] += (own * moved).reshape(ROWS // 8, 8, LANES).sum(axis=0)
+                dh1[ds(group * PHASE + source * ROWS, ROWS), lanes] = total
+            for tap in range(9):
+                tap_parts[tap, :, lanes] += sums[tap]
+            return carry
+
+        def rows_step(group, sums, source=source):
+            span = ds(group * PHASE + source * ROWS, ROWS)
+            unit, inv = normed(x_ref[span, :].astype(F32))
+            grad = dh1[span, :]
+            dx[group, source] = (
+                dx1_ref[span, :] + norm_back(unit, inv, grad * (1.0 + scale_one))
+            ).astype(BF16)
+            return tuple(total + fold(one) for total, one in zip(sums, (grad, grad * unit)))
+
+        lax.fori_loop(0, blocks, conv_step, 0)
+        if at == 0:
+            loads[2].wait()
+        if at == 3:
+            for tap in range(9):
+                tap_sums[0, tap : tap + 1, :] = jnp.sum(tap_parts[tap], axis=0, keepdims=True)
+            tap_sums[0, 9:, :] = jnp.zeros((7, width), F32)
+            taps_copy(0).start()
+        advance(*((0, 1), (0, 1), (0,), (1,))[at])
+        found = lax.fori_loop(0, 4, rows_step, found)
+        if at < 3:
+            back.copies[at].start()
+    back.own.start()
+    late[0] = lane_rows([jnp.sum(one, axis=0, keepdims=True) for one in found], SMALL)
+    for copy in late_wide:
         copy.start()
-    back.own.start()
-    advance(0, 1)
-    for level in range(levels):
-        late_copy(level).wait_recv()
-        if level + 1 < levels:
-            late_copy(level + 1).start()
-        if level >= 2:
-            taps_step(level)
-        if level % 2:
-            advance(0, 1)
-    dtaps_ref[...] = tap_sums[levels]
+    taps_step(0)
+    for copy in late_wide:
+        copy.wait_recv()
+    for copy in late_narrow:
+        copy.start()
+    for level in range(1, levels):
+        taps_step(level)
+        advance(level % 2)
+    for copy in late_narrow:
+        copy.wait_recv()
+    total = tap_sums[levels]
+    for at, copy in enumerate(taps_narrow):
+        copy.wait_recv()
+        total += tap_got[levels + (1, 2, 0)[at]]
+    dtaps_ref[...] = total
     while any(queues):
         advance(0, 1)
     block_back.wait()
     back.wait()
+    for copy in late_wide + late_narrow + taps_narrow:
+        copy.wait_send()
     for level in range(levels):
-        small_copy(level).wait_send()
-        late_copy(level).wait_send()
         taps_copy(level).wait_send()
     for one in sums:
         one.wait_sends()
 
 
-def input_backward(n_wide, x, dx1, dqkv, mod, taps, wqkv, own, silu_row, dmod, block):
+def input_backward(n_wide, x, dx1, dqkv, mod, taps, wqkv, own, block):
     rows, width = x.shape
     slots = lax.axis_size("narrow")
     pieces = 2
     sum_rows = own.shape[0] // pieces
     shape = jax.ShapeDtypeStruct
     per_sum = sum_semaphores(n_wide)
-    levels = (n_wide * slots).bit_length() - 1
+    levels = n_wide.bit_length() - 1
     back = shape((slots, 4, rows // (4 * slots), width), BF16)
     return pl.pallas_call(
         partial(input_backward_kernel, n_wide),
@@ -1397,12 +1416,11 @@
             back,
             back,
             shape((pieces, sum_rows, width), BF16),
-            shape((1 << levels, SMALL, width), BF16),
-            shape((1 << levels, SMALL, LANES), BF16),
+            shape((n_wide * slots, SMALL, LANES), BF16),
             shape((SMALL, width), F32),
         ),
-        in_specs=[whole()] * 6 + [whole(pl.ANY)] * 4,
-        out_specs=(whole(),) * 6,
+        in_specs=[whole()] * 4 + [whole(pl.ANY)] * 4,
+        out_specs=(whole(),) * 5,
         scratch_shapes=[pltpu.VMEM((4, PAD, width), F32)] * 3
         + [
             pltpu.VMEM((rows, width), F32),
@@ -1412,31 +1430,35 @@
             pltpu.VMEM((4, slots, rows // (4 * slots), width), BF16),
             pltpu.VMEM((pieces, sum_rows, width), BF16),
             pltpu.VMEM((pieces, sum_landing(sum_rows, n_wide), width), BF16),
+            pltpu.VMEM((9, 8, width), F32),
             pltpu.VMEM((levels + 1, SMALL, width), F32),
-            pltpu.VMEM((levels, SMALL, width), F32),
+            pltpu.VMEM((levels + 3, SMALL, width), F32),
             pltpu.SemaphoreType.DMA((2, 6)),
             pltpu.SemaphoreType.DMA((5,)),
             pltpu.SemaphoreType.DMA((2, pieces * per_sum)),
-            pltpu.SemaphoreType.DMA((2, 2 * levels)),
-            pltpu.SemaphoreType.DMA((2, levels)),
+            pltpu.SemaphoreType.DMA((2, levels + 3)),
+            pltpu.SemaphoreType.DMA((2, n_wide + 2)),
         ],
         compiler_params=pltpu.CompilerParams(
             vmem_limit_bytes=56 * MIB, collective_id=3, has_side_effects=True
         ),
         name="input_backward",
-    )(x, mod, taps, own, silu_row, dmod, dx1, dqkv, wqkv, block)
+    )(x, mod, taps, own, dx1, dqkv, wqkv, block)
 
 
 def outputs_kernel(
-    dx_in, block_in, attn_sum, ffn_sum, small, late, cond_ref, ada_hbm,
-    gada_hbm, dx_hbm, block_hbm, gqkv_hbm, gout_hbm, gup_hbm, gdown_hbm, gcond_ref,
-    ada, gada, dx, block, gqkv, gout, gup, gdown, sems, in_sem,
+    dx_in, block_in, attn_sum, ffn_sum, small, late, cond_ref, kattn_in, kffn_in, ada_hbm,
+    gada_hbm, dx_hbm, block_hbm, gqkv_hbm, gout_hbm, gup_hbm, gdown_hbm, gcond_ref, kattn_ref, kffn_ref,
+    ada, gada, dx, block, gqkv, gout, gup, gdown, early_rows, late_rows, sems, in_sem,
 ):
-    width = small.shape[-1]
+    width = gout.shape[-1]
     here = lax.axis_index("narrow")
     load_ada = pltpu.make_async_copy(ada_hbm, ada, in_sem.at[0])
     load_ada.start()
     started = []
+    for row in range(3):
+        kattn_ref[row] = kattn_in[3 * row : 3 * row + 3, :]
+        kffn_ref[row] = kffn_in[3 * row : 3 * row + 3, :]
 
     def put(src, dst):
         copy = pltpu.make_async_copy(src, dst, sems.at[len(started)])
@@ -1444,27 +1466,18 @@
         started.append(copy)
 
     devices = small.shape[0]
-    shares = small[...].reshape(devices * SMALL, width)
-    pick = lambda row: mm(
-        one_hot(devices, devices * SMALL, lambda at: at * SMALL + row), shares, NN
-    ).astype(BF16)
-    late_shares = late[...].reshape(devices * SMALL, LANES)
     blocks = width // LANES
-
-    def pick_late(part):
-        return jnp.concatenate(
-            [
-                mm(
-                    one_hot(devices, devices * SMALL, lambda at, at_row=part * blocks + at_block: at * SMALL + at_row),
-                    late_shares, NN,
-                )
-                for at_block in range(blocks)
-            ],
-            axis=1,
-        ).astype(BF16)
-
-    silu_all = pick(0)
-    dmods = [pick_late(part) if part < 2 else pick(part - 1) for part in range(6)]
+    early_rows[...] = small[...].astype(F32).reshape(devices * EARLY, LANES)
+    late_rows[...] = late[...].astype(F32).reshape(devices * SMALL, LANES)
+
+    def pick(ref, share, number):
+        cut = [ref[pl.ds(number * blocks + at, devices, share), :] for at in range(blocks)]
+        return jnp.concatenate(cut, axis=1).astype(BF16)
+
+    silu_all = pick(early_rows, EARLY, 0)
+    dmods = [
+        pick(late_rows, SMALL, part) if part < 2 else pick(early_rows, EARLY, part - 1) for part in range(6)
+    ]
     for part in range(6):
         gada[part] = mm(silu_all, dmods[part], TN)
         put(gada.at[part], gada_hbm.at[:, part * width : (part + 1) * width])
@@ -1491,8 +1504,7 @@
 
     def own_place(row):
         away = row ^ here
-        place = ((away // 2) % 2) + (away % 2) * (devices // 2)
-        return jnp.where(row < cond_ref.shape[0], place, -1)
+        return jnp.where(row < cond_ref.shape[0], away * (devices // 4), -1)
 
     load_ada.wait()
     choose = one_hot(16, devices, own_place)
@@ -1507,7 +1519,7 @@
         copy.wait()
 
 
-def outputs(dx, block, attn_sum, ffn_sum, small, late, cond, w_ada):
+def outputs(dx, block, attn_sum, ffn_sum, small, late, cond, kattn, kffn, w_ada):
     slots, _, quarter, width = dx.shape
     slab = attn_sum.shape[1] // 2
     pieces = ffn_sum.shape[0]
@@ -1525,9 +1537,11 @@
             shape((width, local), F32),
             shape((local, width), F32),
             shape(cond.shape, F32),
+            shape((3, 3, width), F32),
+            shape((3, 3, local), F32),
         ),
-        in_specs=[whole()] * 7 + [whole(pl.ANY)],
-        out_specs=(whole(pl.ANY),) * 7 + (whole(),),
+        in_specs=[whole()] * 9 + [whole(pl.ANY)],
+        out_specs=(whole(pl.ANY),) * 7 + (whole(),) * 3,
         scratch_shapes=[
             pltpu.VMEM(w_ada.shape, BF16),
             pltpu.VMEM((6, width, width), F32),
@@ -1537,12 +1551,14 @@
             pltpu.VMEM((slab, width), F32),
             pltpu.VMEM((width, local), F32),
             pltpu.VMEM((local, width), F32),
+            pltpu.VMEM((small.shape[0] * EARLY, LANES), F32),
+            pltpu.VMEM((small.shape[0] * SMALL, LANES), F32),
             pltpu.SemaphoreType.DMA((6 + 3 + 1 + 2 * slots + pieces + 1,)),
             pltpu.SemaphoreType.DMA((1,)),
         ],
         compiler_params=pltpu.CompilerParams(vmem_limit_bytes=56 * MIB),
         name="outputs",
-    )(dx, block, attn_sum, ffn_sum, small, late, cond, w_ada)
+    )(dx, block, attn_sum, ffn_sum, small, late, cond, kattn, kffn, w_ada)
 
 
 def per_device(
@@ -1556,7 +1572,6 @@
     n_wide = lax.axis_size("wide")
     qkv_t = w_qkv.transpose(2, 1, 0).reshape(w_qkv.shape[2], 3 * width)
     ktaps_own = jnp.pad(k_ffn.reshape(9, local), ((0, 7), (0, 0)))
-    attn_taps = k_attn.reshape(9, width).astype(F32)
 
     cond_f = condition.astype(F32)
     silu_low = jax.nn.silu(cond_f).astype(BF16)
@@ -1564,23 +1579,25 @@
     live = (here < counts[0]).astype(F32).reshape(1, 1)
 
     (x, cot, u, qkv, probs, ctx, wqkv, wout, mod, att, x1, h2, h2t, db, wup, wdown, ktaps) = front(
-        live, own_silu, attn_taps, tokens, cotangent, w_ada, qkv_t, w_out, w_up, w_down, ktaps_own
+        live, own_silu, k_attn, tokens, cotangent, w_ada, qkv_t, w_out, w_up, w_down, ktaps_own
     )
     cot = cot.reshape(rows_all, width)
-    ffn_taps = ktaps[:, :9].astype(F32)
     block_g, dx1, datt, dmod_mid, parcels = ffn(
-        n_wide, live, h2, h2t, db, x1, cot, att, mod, wup, wdown, ffn_taps
+        n_wide, live, h2, h2t, db, x1, cot, att, mod, wup, wdown, ktaps
     )
     block_g = block_g.reshape(4, lat_dev, shard_rows // 4, width)
-    dqkv, own, ffn_sum, gtaps = attn_backward(n_wide, datt, ctx, u, wout, parcels, qkv, probs)
-    got_dx, got_block, attn_sum, small, late, dattn_taps = input_backward(
-        n_wide, x, dx1, dqkv, mod, attn_taps, wqkv, own, own_silu, dmod_mid, block_g
+    dqkv, own, ffn_sum, gtaps, small = attn_backward(
+        n_wide, datt, ctx, u, wout, parcels, own_silu, dmod_mid, qkv, probs
     )
-    grad_w_ada, grad_tokens, block, gqkv, grad_w_out, grad_w_up, grad_w_down, grad_condition = outputs(
-        got_dx, got_block, attn_sum, ffn_sum, small, late, condition, w_ada
+    got_dx, got_block, attn_sum, late, dattn_taps = input_backward(
+        n_wide, x, dx1, dqkv, mod, k_attn, wqkv, own, block_g
     )
-    grad_k_ffn = gtaps[:9].reshape(3, 3, local)
-    grad_k_attn = dattn_taps[:9].reshape(3, 3, width)
+    (
+        grad_w_ada, grad_tokens, block, gqkv, grad_w_out, grad_w_up, grad_w_down, grad_condition,
+        grad_k_attn, grad_k_ffn,
+    ) = outputs(
+        got_dx, got_block, attn_sum, ffn_sum, small, late, condition, dattn_taps, gtaps, w_ada
+    )
     grad_w_qkv = gqkv.transpose(1, 0, 2)
     return (
         block,

time: 336 us -> 321 us (0.955)
  the two profiles are of different devices: /device:TPU:3 before, /device:TPU:0 now
where the time goes in v7:
time: 321 us; the launch traced here: 315 us
  Pallas kernels  305 us (95%)
  local copies, waits for them, and re-layouts  7.03 us (2%)
    pallas_call x1, Pallas kernels, ffn(): pl.pallas_call(partial(ffn_kernel, n_wide), grid=(steps,), out_shape=(sha...  85.7 us
    pallas_call x1, Pallas kernels, front(): pl.pallas_call(front_kernel, out_shape=streamed + (shape((6, width), F32)...  83.4 us
    pallas_call x1, Pallas kernels, attn_backward(): pl.pallas_call(partial(attn_backward_kernel, n_wide), out_shape=(shape((r...  61.5 us
    pallas_call x1, Pallas kernels, input_backward(): pl.pallas_call(partial(input_backward_kernel, n_wide), out_shape=(back, b...  57.2 us
    pallas_call x1, Pallas kernels, outputs(): pl.pallas_call(outputs_kernel, out_shape=(shape(w_ada.shape, F32), shape(...  17.4 us

profile of v7, /device:TPU:0, one launch (start us, length us, event | category | flops | bytes accessed | tf_op | source)
XLA Modules:
  0.0 314.7 jit_solution(11224211472311721000)
XLA Ops:
  1.3 0.7 convert_element_type.9
  2.0 0.6 broadcast_in_dim.8.silu_ref
  2.7 0.7 reshape.40
  3.4 0.6 pad.4.ktaps_src
  4.0 2.1 copy.25
  6.2 83.4 %attn_forward.1 = (bf16[1024,768]{1,0:T(8,128)(2,1)}, bf16[4,4,64,768]{3,2,1,0:T(8,128)(2,1)}, bf16[1024,768]{1,0:T(8,128)(2,1)}, bf16[1024,2304]{1,0:T(8,128)(2...) custom-call(f32[1,1]{1,0:T(1,128)} %bitcast.1.live_ref, ...), custom_call_target="tpu_custom_call" | custom-call | tf_op jit(solution)/shard_map/attn_forward/pallas_call | solution.py:591
  89.5 85.7 %feed_forward.1 = (bf16[1024,768]{1,0:T(8,128)(2,1)}, f32[1024,768]{1,0:T(8,128)}, bf16[1024,768]{1,0:T(8,128)(2,1)}, f32[4,768]{1,0:T(4,128)}, bf16[3,1552,256]{2,1,0:T(8,128)(2,1)}) custom-call(f32[1,1]{1,0:T(1,128)} %bitcast.1.live_ref, bf16[1024,768]{1,0:T(8,128)(2,1)} %get-tuple-element.54.h2_ref, bf16[768,1024]{1,0:T(8,128)(2,1)} %get-tuple-element.55.h2t_ref, ...), custom_call_target="tpu_custom_call" | custom-call | tf_op jit(solution)/shard_map/feed_forward/pallas_call | solution.py:901
  175.2 61.5 %attn_backward.1 = (bf16[1024,2304]{1,0:T(8,128)(2,1)}, bf16[768,768]{1,0:T(8,128)(2,1)}, bf16[3,1536,256]{2,1,0:T(8,128)(2,1)}, f32[16,768]{1,0:T(8,128)}, bf16[32,32,128]{2,1,0:T(8,128)(2,1)}) custom-call(bf16[1024,768]{1,0:T(8,128)(2,1)} %get-tuple-element.63.datt_ref, bf16[1024,768]{1,0:T(8,128)(2,1)} %get-tuple-element.64.ctx_ref, ...), custom_call_target="tpu_custom_call" | custom-call | tf_op jit(solution)/shard_map/attn_backward/pallas_call | solution.py:1186
  236.8 57.2 %input_backward.1 = (bf16[4,4,64,768]{3,2,1,0:T(8,128)(2,1)}, bf16[4,4,64,768]{3,2,1,0:T(8,128)(2,1)}, bf16[2,384,768]{2,1,0:T(8,128)(2,1)}, bf16[32,16,128]{2,1,0:T(8,128)(2,1)}, f32[16,768]{1,0:T(8,128)}) custom-call(bf16[1024,768]{1,0:T(8,128)(2,1)} %get-tuple-element.52.x_ref, f32[6,768]{1,0:T(8,128)} %get-tuple-element.53.mod_ref, ...), custom_call_target="tpu_custom_call" | custom-call | tf_op jit(solution)/shard_map/input_backward/pallas_call | solution.py:1413
  293.9 17.4 %outputs.1 = (f32[768,4608]{1,0:T(8,128)}, f32[4,256,768]{2,1,0:T(8,128)}, bf16[4,256,768]{2,1,0:T(8,128)(2,1)}, f32[3,768,192]{2,1,0:T(8,128)}, f32[192,768]{1,...) custom-call(bf16[4,4,64,768]{3,2,1,0:T(8,128)(2,1)} %get-tuple-eleme, ...), custom_call_target="tpu_custom_call" | custom-call | tf_op jit(solution)/shard_map/outputs/pallas_call | solution.py:1529
  311.4 2.9 copy.24
  (1 shorter events, 0.0 us)

commit v8 on v7

--- a/solution.py
+++ b/solution.py
@@ -387,7 +387,6 @@
 
         lax.fori_loop(0, latents, one, 0)
 
-    permute(sent)
     pl.semaphore_wait(barrier, len(partners))
     exchange = Exchange(sent, got, sems, local_sems.at[0], 0, wide, here)
     exchange_cot = Exchange(sent_cot, cot_ref, sems, local_sems.at[1], 3, wide, here)
@@ -408,6 +407,8 @@
         remote(ktaps_src, ktaps_ref.at[peer ^ here], sems, 6 + at, wide, peer)
         for at, peer in enumerate(narrow_peers(here))
     ]
+    g_qkv.start_far()
+    permute(sent)
     exchange.start()
     load_cot = pltpu.make_async_copy(cot_hbm, shards, in_sems.at[0])
     load_cot.start()
@@ -426,13 +427,15 @@
         )[0:1, :]
     load_cot.wait()
     permute(sent_cot)
+    g_qkv.swap()
     shift_one, scale_one, gate_one = mod_ref[0:1, :], mod_ref[1:2, :], mod_ref[2:3, :]
     shift_two, scale_two, gate_two = mod_ref[3:4, :], mod_ref[4:5, :], mod_ref[5:6, :]
     clear_edges(base)
     clear_edges(shifted)
     exchange.wait()
-    g_qkv.start_far()
     g_out.start_far()
+    g_up.start_far()
+    g_qkv.corner()
     for group in range(4):
         for source in range(latents):
             start = group * PHASE + source * ROWS
@@ -447,9 +450,8 @@
         return carry
 
     lax.fori_loop(0, rows_all // ROWS, norm_step, 0)
-    g_qkv.swap()
+    g_qkv.share_corner()
     g_out.swap()
-    g_up.start_far()
 
     def conv_step(block, carry):
         lanes = ds(block * LANES, LANES)
@@ -470,13 +472,11 @@
 
     blocks = width // LANES
     lax.fori_loop(0, 2 * blocks // 3, conv_step, 0)
-    g_qkv.corner()
     g_out.corner()
     g_up.swap()
     g_down.start_far()
     lax.fori_loop(2 * blocks // 3, blocks, conv_step, 0)
     flush(u_ref, u_hbm)
-    g_qkv.share_corner()
     g_qkv.finish()
     flush(wqkv_ref, wqkv_hbm)
 
@@ -1132,7 +1132,8 @@
         far_out.start()
 
     later = lambda *which: partial(advance, *which)
-    small_plan = [(2 * level + 3, partial(small_step, level)) for level in range(len(partners) - 1)]
+    hops = len(partners) - 1
+    small_plan = [(4 + 18 * level // hops, partial(small_step, level)) for level in range(hops)]
     attend_loop(
         0, steps // 2,
         [one for one in small_plan if one[0] < steps // 2]

time: 321 us -> 314 us (0.978)
  Pallas kernels: 305 us -> 299 us
    pallas_call x1, Pallas kernels: 83.4 us -> 80 us  [front(): pl.pallas_call(front_kernel, out_shape=streamed + (shape((6, width), F32)...]
where the time goes in v8:
time: 314 us; the launch traced here: 309 us
  Pallas kernels  299 us (95%)
  local copies, waits for them, and re-layouts  7.03 us (2%)
    pallas_call x1, Pallas kernels, ffn(): pl.pallas_call(partial(ffn_kernel, n_wide), grid=(steps,), out_shape=(sha...  83.5 us
    pallas_call x1, Pallas kernels, front(): pl.pallas_call(front_kernel, out_shape=streamed + (shape((6, width), F32)...  80 us
    pallas_call x1, Pallas kernels, input_backward(): pl.pallas_call(partial(input_backward_kernel, n_wide), out_shape=(back, b...  59.4 us
    pallas_call x1, Pallas kernels, attn_backward(): pl.pallas_call(partial(attn_backward_kernel, n_wide), out_shape=(shape((r...  58.6 us
    pallas_call x1, Pallas kernels, outputs(): pl.pallas_call(outputs_kernel, out_shape=(shape(w_ada.shape, F32), shape(...  17.4 us

profile of v8, /device:TPU:0, one launch (start us, length us, event | category | flops | bytes accessed | tf_op | source)
XLA Modules:
  0.0 308.5 jit_solution(15473012277877841339)
XLA Ops:
  1.3 0.7 convert_element_type.9
  2.0 0.6 broadcast_in_dim.8.silu_ref
  2.7 0.7 reshape.40
  3.4 0.6 pad.4.ktaps_src
  4.0 2.1 copy.25
  6.2 80.0 %attn_forward.1 = (bf16[1024,768]{1,0:T(8,128)(2,1)}, bf16[4,4,64,768]{3,2,1,0:T(8,128)(2,1)}, bf16[1024,768]{1,0:T(8,128)(2,1)}, bf16[1024,2304]{1,0:T(8,128)(2...) custom-call(f32[1,1]{1,0:T(1,128)} %bitcast.1.live_ref, ...), custom_call_target="tpu_custom_call" | custom-call | tf_op jit(solution)/shard_map/attn_forward/pallas_call | solution.py:591
  86.2 83.5 %feed_forward.1 = (bf16[1024,768]{1,0:T(8,128)(2,1)}, f32[1024,768]{1,0:T(8,128)}, bf16[1024,768]{1,0:T(8,128)(2,1)}, f32[4,768]{1,0:T(4,128)}, bf16[3,1552,256]{2,1,0:T(8,128)(2,1)}) custom-call(f32[1,1]{1,0:T(1,128)} %bitcast.1.live_ref, bf16[1024,768]{1,0:T(8,128)(2,1)} %get-tuple-element.54.h2_ref, bf16[768,1024]{1,0:T(8,128)(2,1)} %get-tuple-element.55.h2t_ref, ...), custom_call_target="tpu_custom_call" | custom-call | tf_op jit(solution)/shard_map/feed_forward/pallas_call | solution.py:901
  169.7 58.6 %attn_backward.1 = (bf16[1024,2304]{1,0:T(8,128)(2,1)}, bf16[768,768]{1,0:T(8,128)(2,1)}, bf16[3,1536,256]{2,1,0:T(8,128)(2,1)}, f32[16,768]{1,0:T(8,128)}, bf16[32,32,128]{2,1,0:T(8,128)(2,1)}) custom-call(bf16[1024,768]{1,0:T(8,128)(2,1)} %get-tuple-element.63.datt_ref, bf16[1024,768]{1,0:T(8,128)(2,1)} %get-tuple-element.64.ctx_ref, ...), custom_call_target="tpu_custom_call" | custom-call | tf_op jit(solution)/shard_map/attn_backward/pallas_call | solution.py:1187
  228.3 59.4 %input_backward.1 = (bf16[4,4,64,768]{3,2,1,0:T(8,128)(2,1)}, bf16[4,4,64,768]{3,2,1,0:T(8,128)(2,1)}, bf16[2,384,768]{2,1,0:T(8,128)(2,1)}, bf16[32,16,128]{2,1,0:T(8,128)(2,1)}, f32[16,768]{1,0:T(8,128)}) custom-call(bf16[1024,768]{1,0:T(8,128)(2,1)} %get-tuple-element.52.x_ref, f32[6,768]{1,0:T(8,128)} %get-tuple-element.53.mod_ref, ...), custom_call_target="tpu_custom_call" | custom-call | tf_op jit(solution)/shard_map/input_backward/pallas_call | solution.py:1414
  287.7 17.4 %outputs.1 = (f32[768,4608]{1,0:T(8,128)}, f32[4,256,768]{2,1,0:T(8,128)}, bf16[4,256,768]{2,1,0:T(8,128)(2,1)}, f32[3,768,192]{2,1,0:T(8,128)}, f32[192,768]{1,...) custom-call(bf16[4,4,64,768]{3,2,1,0:T(8,128)(2,1)} %get-tuple-eleme, ...), custom_call_target="tpu_custom_call" | custom-call | tf_op jit(solution)/shard_map/outputs/pallas_call | solution.py:1530
  305.2 2.9 copy.24
  (1 shorter events, 0.0 us)
